TPU v7x, 32 devices: a whole 2x2x4 slice. The times are simulated.
32 devices in a mesh: dp: 16 (over z, y, core), mp: 2 (over x).
Axes of the slice: x: 2, y: 2, z: 4, core: 2. Of those that a mesh axis runs over, the one named last changes fastest.
Arguments:
- image_tokens: bfloat16 [48, 256, 1536], P('dp', 'mp'), may hold values from -6 to 6
- text_tokens: bfloat16 [48, 128, 1536], P('dp', 'mp'), may hold values from -6 to 6
- condition: bfloat16 [48, 1536], P('dp', 'mp'), may hold values from -6 to 6
- live_table: int32 [16, 3], P('dp'), may hold values from 0 to 1, as said below
- ada_weight: float32 [2, 1536, 9216], P(None, ('mp', 'dp')), may hold values from -0.15625 to 0.15625
- ada_bias: float32 [2, 9216], P(None, 'dp'), may hold values from -3 to 3
- qkv_weight: float32 [2, 3, 1536, 1536], P(None, None, 'dp', 'mp'), may hold values from -0.15625 to 0.15625
- qv_bias: float32 [2, 2, 1536], P(None, None, ('mp', 'dp')), may hold values from -3 to 3
- proj_weight: float32 [2, 1536, 1536], P(None, 'mp', 'dp'), may hold values from -1.25 to 1.25
- proj_bias: float32 [2, 1536], P(None, 'dp'), may hold values from -3 to 3
- fc1_weight: float32 [2, 1536, 6144], P(None, 'dp', 'mp'), may hold values from -0.15625 to 0.15625
- fc1_bias: float32 [2, 6144], P(None, ('mp', 'dp')), may hold values from -3 to 3
- fc2_weight: float32 [2, 6144, 1536], P(None, 'mp', 'dp'), may hold values from -0.078125 to 0.078125
- fc2_bias: float32 [2, 1536], P(None, 'dp'), may hold values from -3 to 3
- image_cotangent: bfloat16 [48, 256, 1536], P('dp', 'mp'), may hold values from -6 to 6
- text_cotangent: bfloat16 [48, 128, 1536], P('dp', 'mp'), may hold values from -6 to 6
Outputs:
- image_out: bfloat16 [48, 256, 1536], P('dp', 'mp')
- text_out: bfloat16 [48, 128, 1536], P('dp', 'mp')
- ada_weight_grad: float32 [2, 1536, 9216], P(None, ('mp', 'dp'))
- ada_bias_grad: float32 [2, 9216], P(None, 'dp')
- qkv_weight_grad: float32 [2, 3, 1536, 1536], P(None, None, 'dp', 'mp')
- qv_bias_grad: float32 [2, 2, 1536], P(None, None, ('mp', 'dp'))
- proj_weight_grad: float32 [2, 1536, 1536], P(None, 'mp', 'dp')
- proj_bias_grad: float32 [2, 1536], P(None, 'dp')
- fc1_weight_grad: float32 [2, 1536, 6144], P(None, 'dp', 'mp')
- fc1_bias_grad: float32 [2, 6144], P(None, ('mp', 'dp'))
- fc2_weight_grad: float32 [2, 6144, 1536], P(None, 'mp', 'dp')
- fc2_bias_grad: float32 [2, 1536], P(None, 'dp')
- image_grad: float32 [48, 256, 1536], P('dp', 'mp')
- text_grad: float32 [48, 128, 1536], P('dp', 'mp')
- condition_grad: float32 [48, 1536], P('dp', 'mp')
Inputs may be any that keep to these rules, and one draw needn't show every extreme that they name: `live_table`: every row has a live entry, and some row has all 3 entries live.
All inputs are finite; a program needn't handle non-finite values.
Results may differ from a plain program's by a relative error of at most 0.02.
The roundings to bfloat16 on the way count: a program that leaves them out, or rounds other values in their place, can miss the bound.
Values may be sent and summed in bfloat16 or wider, within the bound.
No kernel may reach another device: no remote copies, remote signals or barrier semaphores. Data moves between devices by JAX's collectives and lax.ppermute only.
A program may use at most 960 MiB of HBM per device.

v0:
```python
import jax
import jax.numpy as jnp
from jax import lax
from jax.sharding import PartitionSpec as P

HEAD_DIM = 64


EPSILON = 1e-06


def layer_norm(values):
    center = values - jnp.mean(values, axis=-1, keepdims=True)
    inverse = lax.rsqrt(jnp.mean(center * center, axis=-1, keepdims=True) + EPSILON)
    return (center * inverse, inverse)


def norm_back(normed, inverse, upstream):
    mean_up = jnp.mean(upstream, axis=-1, keepdims=True)
    mean_cross = jnp.mean(upstream * normed, axis=-1, keepdims=True)
    return inverse * (upstream - mean_up - normed * mean_cross)


def gelu_tanh(values):
    return jax.nn.gelu(values, approximate=True)


def when_live(live_flag, function, operands):

    def skipped(inputs):
        return jax.tree.map(jnp.zeros_like, function(inputs))

    return lax.cond(live_flag, function, skipped, operands)


def split_heads(matrix):
    return matrix.reshape(matrix.shape[0], matrix.shape[1] // HEAD_DIM, HEAD_DIM)


def joint_scores(query_all, key_all):
    scores = jnp.einsum(
        "qhd,khd->hqk",
        split_heads(query_all),
        split_heads(key_all),
        preferred_element_type=jnp.float32,
    )
    return scores * HEAD_DIM ** (-0.5)


def attention_forward(operands):
    image_rows, text_rows, qkv_weights, qv_biases, proj_weights = operands
    columns = []
    for select in range(3):
        pieces = []
        for stream, token_rows in ((1, text_rows), (0, image_rows)):
            product = jnp.dot(
                token_rows, qkv_weights[stream, select], preferred_element_type=jnp.float32
            )
            if select == 0:
                product = product + qv_biases[stream, 0]
            if select == 2:
                product = product + qv_biases[stream, 1]
            pieces.append(product.astype(jnp.bfloat16))
        columns.append(jnp.concatenate(pieces, axis=0))
    query_all, key_all, value_all = columns
    scores = joint_scores(query_all, key_all)
    highest = jnp.max(scores, axis=-1, keepdims=True)
    log_total = highest + jnp.log(jnp.sum(jnp.exp(scores - highest), axis=-1, keepdims=True))
    probs_low = jnp.exp(scores - log_total).astype(jnp.bfloat16)
    attended_heads = jnp.einsum(
        "hqk,khd->qhd", probs_low, split_heads(value_all), preferred_element_type=jnp.float32
    )
    attended_heads = attended_heads.reshape(query_all.shape).astype(jnp.bfloat16)
    text_len = text_rows.shape[0]
    image_part = jnp.dot(
        attended_heads[text_len:], proj_weights[0], preferred_element_type=jnp.float32
    )
    text_part = jnp.dot(
        attended_heads[:text_len], proj_weights[1], preferred_element_type=jnp.float32
    )
    return (query_all, key_all, value_all, log_total, attended_heads, image_part, text_part)


def mlp_forward(operands):
    image_rows, text_rows, up_weights, up_biases, down_weights = operands
    results = []
    for stream, token_rows in ((0, image_rows), (1, text_rows)):
        pre_active = (
            jnp.dot(token_rows, up_weights[stream], preferred_element_type=jnp.float32)
            + up_biases[stream]
        )
        activated = gelu_tanh(pre_active).astype(jnp.bfloat16)
        results.append(
            (
                pre_active,
                activated,
                jnp.dot(activated, down_weights[stream], preferred_element_type=jnp.float32),
            )
        )
    return tuple(results)


def mlp_backward(operands):
    (
        image_rows,
        text_rows,
        pre_actives,
        activations,
        image_upstream,
        text_upstream,
        up_weights,
        down_weights,
    ) = operands
    up_weight_grads, up_bias_grads, down_weight_grads, back_rows = ([], [], [], [])
    for stream, token_rows, upstream in (
        (0, image_rows, image_upstream),
        (1, text_rows, text_upstream),
    ):
        down_weight_grads.append(
            jnp.einsum(
                "lf,ld->fd", activations[stream], upstream, preferred_element_type=jnp.float32
            )
        )
        grad_active = jnp.einsum(
            "ld,fd->lf", upstream, down_weights[stream], preferred_element_type=jnp.float32
        )
        unused, pullback = jax.vjp(gelu_tanh, pre_actives[stream])
        grad_pre = pullback(grad_active)[0].astype(jnp.bfloat16)
        up_bias_grads.append(jnp.sum(grad_pre.astype(jnp.float32), axis=0))
        up_weight_grads.append(
            jnp.einsum("ld,lf->df", token_rows, grad_pre, preferred_element_type=jnp.float32)
        )
        back_rows.append(
            jnp.einsum(
                "lf,df->ld", grad_pre, up_weights[stream], preferred_element_type=jnp.float32
            )
        )
    return (
        jnp.stack(up_weight_grads),
        jnp.stack(up_bias_grads),
        jnp.stack(down_weight_grads),
        back_rows[0],
        back_rows[1],
    )


def attention_backward(operands):
    (
        image_rows,
        text_rows,
        query_all,
        key_all,
        value_all,
        log_total,
        attended_heads,
        image_upstream,
        text_upstream,
        qkv_weights,
        proj_weights,
    ) = operands
    text_len = text_rows.shape[0]
    total_len = query_all.shape[0]
    proj_grads = jnp.stack(
        [
            jnp.einsum(
                "le,ld->ed",
                attended_heads[text_len:],
                image_upstream,
                preferred_element_type=jnp.float32,
            ),
            jnp.einsum(
                "le,ld->ed",
                attended_heads[:text_len],
                text_upstream,
                preferred_element_type=jnp.float32,
            ),
        ]
    )
    grad_mixed = jnp.concatenate(
        [
            jnp.einsum(
                "ld,ed->le", text_upstream, proj_weights[1], preferred_element_type=jnp.float32
            ),
            jnp.einsum(
                "ld,ed->le", image_upstream, proj_weights[0], preferred_element_type=jnp.float32
            ),
        ],
        axis=0,
    ).astype(jnp.bfloat16)
    scores = joint_scores(query_all, key_all)
    probability = jnp.exp(scores - log_total)
    grad_probs = jnp.einsum(
        "qhd,khd->hqk",
        split_heads(grad_mixed),
        split_heads(value_all),
        preferred_element_type=jnp.float32,
    )
    row_dot = jnp.sum(probability * grad_probs, axis=-1, keepdims=True)
    grad_scores = (probability * (grad_probs - row_dot)).astype(jnp.bfloat16)
    score_scale = HEAD_DIM ** (-0.5)
    flat_shape = query_all.shape
    grad_query = (
        (
            jnp.einsum(
                "hqk,khd->qhd",
                grad_scores,
                split_heads(key_all),
                preferred_element_type=jnp.float32,
            )
            * score_scale
        )
        .reshape(flat_shape)
        .astype(jnp.bfloat16)
    )
    grad_key = (
        (
            jnp.einsum(
                "hqk,qhd->khd",
                grad_scores,
                split_heads(query_all),
                preferred_element_type=jnp.float32,
            )
            * score_scale
        )
        .reshape(flat_shape)
        .astype(jnp.bfloat16)
    )
    grad_value = (
        jnp.einsum(
            "hqk,qhd->khd",
            probability.astype(jnp.bfloat16),
            split_heads(grad_mixed),
            preferred_element_type=jnp.float32,
        )
        .reshape(flat_shape)
        .astype(jnp.bfloat16)
    )
    stacked = jnp.stack([grad_query, grad_key, grad_value])
    qkv_grads, bias_grads, back_rows = ([], [], [])
    for stream, token_rows, row_start, row_stop in (
        (0, image_rows, text_len, total_len),
        (1, text_rows, 0, text_len),
    ):
        row_block = stacked[:, row_start:row_stop]
        qkv_grads.append(
            jnp.einsum("ld,tle->tde", token_rows, row_block, preferred_element_type=jnp.float32)
        )
        bias_grads.append(jnp.sum(row_block[0::2].astype(jnp.float32), axis=1))
        back_rows.append(
            jnp.einsum(
                "tle,tde->ld", row_block, qkv_weights[stream], preferred_element_type=jnp.float32
            )
        )
    return (jnp.stack(qkv_grads), jnp.stack(bias_grads), proj_grads, back_rows[0], back_rows[1])


def forward_step(weights, token_streams, cond_now, live_flag):
    ada_weights, ada_biases, qkv_weights, qv_biases, proj_weights = weights[0:5]
    proj_biases, up_weights, up_biases, down_weights, down_biases = weights[5:10]
    silu_cond = jax.nn.silu(cond_now.astype(jnp.float32)).astype(jnp.bfloat16)
    partial_mod = jnp.einsum(
        "r,srk->sk", silu_cond, ada_weights, preferred_element_type=jnp.float32
    )
    modulation = lax.psum(partial_mod, "mp") + ada_biases.astype(jnp.float32)
    modulation = modulation.reshape(2, 6, token_streams[0].shape[-1])
    hidden_rows, first_norm, first_inverse, joint_in = ([], [], [], [])
    for stream in range(2):
        rows_value = token_streams[stream].astype(jnp.float32)
        normed, inverse = layer_norm(rows_value)
        hidden_rows.append(rows_value)
        first_norm.append(normed)
        first_inverse.append(inverse)
        joint_in.append(
            (normed * (1.0 + modulation[stream, 1]) + modulation[stream, 0]).astype(jnp.bfloat16)
        )
    image_all, text_all = (
        lax.all_gather(joint_in[0], "mp", axis=0, tiled=True),
        lax.all_gather(joint_in[1], "mp", axis=0, tiled=True),
    )
    attention = when_live(
        live_flag, attention_forward, (image_all, text_all, qkv_weights, qv_biases, proj_weights)
    )
    image_sum, text_sum = (
        lax.psum_scatter(
            attention[5].astype(jnp.bfloat16), "mp", scatter_dimension=0, tiled=True
        ).astype(jnp.float32),
        lax.psum_scatter(
            attention[6].astype(jnp.bfloat16), "mp", scatter_dimension=0, tiled=True
        ).astype(jnp.float32),
    )
    attention_sums = (image_sum, text_sum)
    first_branch, residual, second_norm, second_inverse, mlp_in = ([], [], [], [], [])
    for stream in range(2):
        branch = attention_sums[stream] + proj_biases[stream].astype(jnp.float32)
        resid_rows = hidden_rows[stream] + modulation[stream, 2] * branch
        normed, inverse = layer_norm(resid_rows)
        first_branch.append(branch)
        residual.append(resid_rows)
        second_norm.append(normed)
        second_inverse.append(inverse)
        mlp_in.append(
            (normed * (1.0 + modulation[stream, 4]) + modulation[stream, 3]).astype(jnp.bfloat16)
        )
    image_mlp, text_mlp = (
        lax.all_gather(mlp_in[0], "mp", axis=0, tiled=True),
        lax.all_gather(mlp_in[1], "mp", axis=0, tiled=True),
    )
    feed_forward = when_live(
        live_flag, mlp_forward, (image_mlp, text_mlp, up_weights, up_biases, down_weights)
    )
    image_down, text_down = (
        lax.psum_scatter(
            feed_forward[0][2].astype(jnp.bfloat16), "mp", scatter_dimension=0, tiled=True
        ).astype(jnp.float32),
        lax.psum_scatter(
            feed_forward[1][2].astype(jnp.bfloat16), "mp", scatter_dimension=0, tiled=True
        ).astype(jnp.float32),
    )
    down_sums = (image_down, text_down)
    outputs, second_branch = ([], [])
    for stream in range(2):
        branch = down_sums[stream] + down_biases[stream].astype(jnp.float32)
        second_branch.append(branch)
        outputs.append(residual[stream] + modulation[stream, 5] * branch)
    saved = (
        modulation,
        silu_cond,
        first_norm,
        first_inverse,
        first_branch,
        second_norm,
        second_inverse,
        second_branch,
        image_all,
        text_all,
        attention[0:5],
        image_mlp,
        text_mlp,
        feed_forward,
    )
    return (saved, outputs)


def backward_step(weights, saved, cotangents, cond_now, live_flag):
    ada_weights, ada_biases, qkv_weights, qv_biases, proj_weights = weights[0:5]
    proj_biases, up_weights, up_biases, down_weights, down_biases = weights[5:10]
    (
        modulation,
        silu_cond,
        first_norm,
        first_inverse,
        first_branch,
        second_norm,
        second_inverse,
        second_branch,
        image_all,
        text_all,
        attention,
        image_mlp,
        text_mlp,
        feed_forward,
    ) = saved
    gate_two, down_bias_grad, branch_low = ([], [], [])
    for stream in range(2):
        upstream = cotangents[stream]
        gate_two.append(jnp.sum(upstream * second_branch[stream], axis=0))
        branch_grad = upstream * modulation[stream, 5]
        down_bias_grad.append(jnp.sum(branch_grad, axis=0))
        branch_low.append(branch_grad.astype(jnp.bfloat16))
    image_up, text_up = (
        lax.all_gather(branch_low[0], "mp", axis=0, tiled=True),
        lax.all_gather(branch_low[1], "mp", axis=0, tiled=True),
    )
    mlp_grads = when_live(
        live_flag,
        mlp_backward,
        (
            image_mlp,
            text_mlp,
            (feed_forward[0][0], feed_forward[1][0]),
            (feed_forward[0][1], feed_forward[1][1]),
            image_up,
            text_up,
            up_weights,
            down_weights,
        ),
    )
    image_back, text_back = (
        lax.psum_scatter(
            mlp_grads[3].astype(jnp.bfloat16), "mp", scatter_dimension=0, tiled=True
        ).astype(jnp.float32),
        lax.psum_scatter(
            mlp_grads[4].astype(jnp.bfloat16), "mp", scatter_dimension=0, tiled=True
        ).astype(jnp.float32),
    )
    mlp_back = (image_back, text_back)
    shift_two, scale_two, gate_one, proj_bias_grad, resid_grads, attention_low = (
        [],
        [],
        [],
        [],
        [],
        [],
    )
    for stream in range(2):
        shift_two.append(jnp.sum(mlp_back[stream], axis=0))
        scale_two.append(jnp.sum(mlp_back[stream] * second_norm[stream], axis=0))
        resid_grad = cotangents[stream] + norm_back(
            second_norm[stream],
            second_inverse[stream],
            mlp_back[stream] * (1.0 + modulation[stream, 4]),
        )
        resid_grads.append(resid_grad)
        gate_one.append(jnp.sum(resid_grad * first_branch[stream], axis=0))
        attention_grad = resid_grad * modulation[stream, 2]
        proj_bias_grad.append(jnp.sum(attention_grad, axis=0))
        attention_low.append(attention_grad.astype(jnp.bfloat16))
    image_dy, text_dy = (
        lax.all_gather(attention_low[0], "mp", axis=0, tiled=True),
        lax.all_gather(attention_low[1], "mp", axis=0, tiled=True),
    )
    attention_grads = when_live(
        live_flag,
        attention_backward,
        (
            image_all,
            text_all,
            attention[0],
            attention[1],
            attention[2],
            attention[3],
            attention[4],
            image_dy,
            text_dy,
            qkv_weights,
            proj_weights,
        ),
    )
    image_in, text_in = (
        lax.psum_scatter(
            attention_grads[3].astype(jnp.bfloat16), "mp", scatter_dimension=0, tiled=True
        ).astype(jnp.float32),
        lax.psum_scatter(
            attention_grads[4].astype(jnp.bfloat16), "mp", scatter_dimension=0, tiled=True
        ).astype(jnp.float32),
    )
    attention_back = (image_in, text_in)
    input_grads, mod_rows, bias_rows = ([], [], [])
    for stream in range(2):
        shift_one = jnp.sum(attention_back[stream], axis=0)
        scale_one = jnp.sum(attention_back[stream] * first_norm[stream], axis=0)
        input_grads.append(
            resid_grads[stream]
            + norm_back(
                first_norm[stream],
                first_inverse[stream],
                attention_back[stream] * (1.0 + modulation[stream, 1]),
            )
        )
        mod_rows.append(
            jnp.concatenate(
                [
                    shift_one,
                    scale_one,
                    gate_one[stream],
                    shift_two[stream],
                    scale_two[stream],
                    gate_two[stream],
                ]
            )
        )
        bias_rows.append(jnp.stack([proj_bias_grad[stream], down_bias_grad[stream]]))
    mod_grads, bias_grads = (
        lax.psum(jnp.stack(mod_rows).astype(jnp.bfloat16), "mp").astype(jnp.float32),
        lax.psum(jnp.stack(bias_rows).astype(jnp.bfloat16), "mp").astype(jnp.float32),
    )
    silu_grad = jnp.einsum(
        "sk,srk->r", mod_grads, ada_weights.astype(jnp.float32), precision=lax.Precision.HIGHEST
    )
    unused, pullback = jax.vjp(jax.nn.silu, cond_now.astype(jnp.float32))
    cond_grad = pullback(silu_grad)[0]
    pieces = (
        mod_grads,
        attention_grads[0],
        attention_grads[1],
        attention_grads[2],
        bias_grads[:, 0],
        mlp_grads[0],
        mlp_grads[1],
        mlp_grads[2],
        bias_grads[:, 1],
    )
    return (pieces, input_grads, cond_grad, silu_cond, mod_grads)


def body(
    image_tokens,
    text_tokens,
    condition,
    live_table,
    ada_weight,
    ada_bias,
    qkv_weight,
    qv_bias,
    proj_weight,
    proj_bias,
    fc1_weight,
    fc1_bias,
    fc2_weight,
    fc2_bias,
    image_cotangent,
    text_cotangent,
):
    shards = tuple(
        (
            master.astype(jnp.bfloat16)
            for master in (
                ada_weight,
                ada_bias,
                qkv_weight,
                qv_bias,
                proj_weight,
                proj_bias,
                fc1_weight,
                fc1_bias,
                fc2_weight,
                fc2_bias,
            )
        )
    )
    totals = None
    image_outs, text_outs, image_grads, text_grads, cond_grads = ([], [], [], [], [])
    silu_list, factor_list = ([], [])
    for micro_index in range(image_tokens.shape[0]):
        live_flag = live_table[0, micro_index] > 0
        flag_value = live_table[0, micro_index].astype(jnp.float32)
        forward_weights = (
            lax.all_gather(shards[0], "dp", axis=1, tiled=True),
            lax.all_gather(shards[1], "dp", axis=1, tiled=True),
            lax.all_gather(shards[2], "dp", axis=2, tiled=True),
            lax.all_gather(shards[3], "dp", axis=2, tiled=True),
            lax.all_gather(shards[4], "dp", axis=2, tiled=True),
            lax.all_gather(shards[5], "dp", axis=1, tiled=True),
            lax.all_gather(shards[6], "dp", axis=1, tiled=True),
            lax.all_gather(shards[7], "dp", axis=1, tiled=True),
            lax.all_gather(shards[8], "dp", axis=2, tiled=True),
            lax.all_gather(shards[9], "dp", axis=1, tiled=True),
        )
        token_streams = (image_tokens[micro_index], text_tokens[micro_index])
        saved, outputs = forward_step(
            forward_weights, token_streams, condition[micro_index], live_flag
        )
        image_outs.append((outputs[0] * flag_value).astype(jnp.bfloat16))
        text_outs.append((outputs[1] * flag_value).astype(jnp.bfloat16))
        backward_weights = (
            lax.all_gather(shards[0], "dp", axis=1, tiled=True),
            lax.all_gather(shards[1], "dp", axis=1, tiled=True),
            lax.all_gather(shards[2], "dp", axis=2, tiled=True),
            lax.all_gather(shards[3], "dp", axis=2, tiled=True),
            lax.all_gather(shards[4], "dp", axis=2, tiled=True),
            lax.all_gather(shards[5], "dp", axis=1, tiled=True),
            lax.all_gather(shards[6], "dp", axis=1, tiled=True),
            lax.all_gather(shards[7], "dp", axis=1, tiled=True),
            lax.all_gather(shards[8], "dp", axis=2, tiled=True),
            lax.all_gather(shards[9], "dp", axis=1, tiled=True),
        )
        cotangents = (
            image_cotangent[micro_index].astype(jnp.float32) * flag_value,
            text_cotangent[micro_index].astype(jnp.float32) * flag_value,
        )
        pieces, input_grads, cond_grad, silu_cond, mod_grads = backward_step(
            backward_weights, saved, cotangents, condition[micro_index], live_flag
        )
        image_grads.append(input_grads[0])
        text_grads.append(input_grads[1])
        cond_grads.append(cond_grad)
        silu_list.append(silu_cond)
        factor_list.append(mod_grads)
        if totals is None:
            totals = pieces
        else:
            totals = tuple((summed + addend for summed, addend in zip(totals, pieces)))
    dense = None
    for silu_row, factor_rows in zip(silu_list, factor_list):
        outer = jnp.einsum("r,sk->srk", silu_row.astype(jnp.float32), factor_rows)
        dense = outer if dense is None else dense + outer
    reduced = (
        lax.psum_scatter(dense.astype(jnp.bfloat16), "dp", scatter_dimension=1, tiled=True).astype(
            jnp.float32
        ),
        lax.psum_scatter(
            totals[0].astype(jnp.bfloat16), "dp", scatter_dimension=1, tiled=True
        ).astype(jnp.float32),
        lax.psum_scatter(
            totals[1].astype(jnp.bfloat16), "dp", scatter_dimension=2, tiled=True
        ).astype(jnp.float32),
        lax.psum_scatter(
            totals[2].astype(jnp.bfloat16), "dp", scatter_dimension=2, tiled=True
        ).astype(jnp.float32),
        lax.psum_scatter(
            totals[3].astype(jnp.bfloat16), "dp", scatter_dimension=2, tiled=True
        ).astype(jnp.float32),
        lax.psum_scatter(
            totals[4].astype(jnp.bfloat16), "dp", scatter_dimension=1, tiled=True
        ).astype(jnp.float32),
        lax.psum_scatter(
            totals[5].astype(jnp.bfloat16), "dp", scatter_dimension=1, tiled=True
        ).astype(jnp.float32),
        lax.psum_scatter(
            totals[6].astype(jnp.bfloat16), "dp", scatter_dimension=1, tiled=True
        ).astype(jnp.float32),
        lax.psum_scatter(
            totals[7].astype(jnp.bfloat16), "dp", scatter_dimension=2, tiled=True
        ).astype(jnp.float32),
        lax.psum_scatter(
            totals[8].astype(jnp.bfloat16), "dp", scatter_dimension=1, tiled=True
        ).astype(jnp.float32),
    )
    return (
        jnp.stack(image_outs),
        jnp.stack(text_outs),
        reduced[0],
        reduced[1],
        reduced[2],
        reduced[3],
        reduced[4],
        reduced[5],
        reduced[6],
        reduced[7],
        reduced[8],
        reduced[9],
        jnp.stack(image_grads),
        jnp.stack(text_grads),
        jnp.stack(cond_grads),
    )


def solution(mesh):
    placed = (
        P("dp", "mp", None),
        P("dp", "mp", None),
        P("dp", "mp"),
        P("dp", None),
        P(None, ("mp", "dp"), None),
        P(None, "dp"),
        P(None, None, "dp", "mp"),
        P(None, None, ("mp", "dp")),
        P(None, "mp", "dp"),
        P(None, "dp"),
        P(None, "dp", "mp"),
        P(None, ("mp", "dp")),
        P(None, "mp", "dp"),
        P(None, "dp"),
        P("dp", "mp", None),
        P("dp", "mp", None),
    )
    return jax.shard_map(
        body,
        mesh=mesh,
        in_specs=placed,
        out_specs=(
            P("dp", "mp", None),
            P("dp", "mp", None),
            P(None, ("mp", "dp"), None),
            P(None, "dp"),
            P(None, None, "dp", "mp"),
            P(None, None, ("mp", "dp")),
            P(None, "mp", "dp"),
            P(None, "dp"),
            P(None, "dp", "mp"),
            P(None, ("mp", "dp")),
            P(None, "mp", "dp"),
            P(None, "dp"),
            P("dp", "mp", None),
            P("dp", "mp", None),
            P("dp", "mp"),
        ),
        check_vma=False,
    )
```

profile of v0, /device:TPU:0, one launch (start us, length us, event | category | flops | bytes accessed | tf_op | source)
XLA Modules:
  0.0 3704.9 jit_solution(841952366983563891)
XLA Ops:
  13.2 143.7 %all-gather.10.cloned.1.call-done = bf16[2,768,9216]{2,1,0:T(8,128)(2,1)} async-done(((bf16[2,48,9216]{2,1,0:T(8,128)(2,1)}), bf16[2,768,9216]{2,1,0:T(8,128)(2,1)}) %all-gather.10.cloned.1.call-update) | async-done | bytes 28311568 | tf_op jit(solution)/shard_map/all_gather | solution.py:538
  156.9 12.8 fusion.667
  170.4 12.8 fusion.666
  183.9 12.9 fusion.665
  201.4 20.6 all-gather
  223.5 19.4 all_gather.141
  277.8 111.9 %all-gather.12.cloned.1.call-done = bf16[2,3,1536,768]{3,2,1,0:T(8,128)(2,1)} async-done(((bf16[2,3,96,768]{3,2,1,0:T(8,128)(2,1)}), bf16[2,3,1536,768]{3,2,1,0:T(8,128)(2,1)}) %all-gather.12.cloned.1.call-update) | async-done | bytes 14155792 | tf_op jit(solution)/shard_map/all_gather | solution.py:540
  398.5 65.7 %all-gather.1 = bf16[16,96,2]{1,2,0:T(2,128)(2,1)S(1)} all-gather(bf16[1,96,2]{1,2,0:T(2,128)(2,1)S(1)} %convert_bitcast_fusion.9), channel_id=1, replica_groups=mesh['dp'=16,'mp'=2] {'dp'}, dimensions={0}, use_global_device_ids=true | all-gather | bytes 6528 | tf_op jit(solution)/shard_map/all_gather | solution.py:543
  495.0 52.6 %conditional.14 = (bf16[384,768]{1,0:T(8,128)(2,1)S(1)}, bf16[384,768]{1,0:T(8,128)(2,1)S(1)}, bf16[384,768]{1,0:T(8,128)(2,1)}, f32[12,384,1]{1,0,2:T(8,128)}, ...) conditional(s32[]{:T(128)} %bitcast.206, () %tuple.112, ...), branch_computations={%region_23.24_spmd, %region_24.27_spmd} | conditional | flops 4096326144 | bytes 114622832 | solution.py:33
  569.3 50.4 %conditional.16 = (bf16[384,768]{1,0:T(8,128)(2,1)}, bf16[384,768]{1,0:T(8,128)(2,1)}, bf16[384,768]{1,0:T(8,128)(2,1)}, f32[12,384,1]{1,0,2:T(8,128)}, bf16[384...) conditional(s32[]{:T(128)} %bitcast.212, () %tuple.116, ...), branch_computations={%region_41.42_spmd, %region_42.45_spmd} | conditional | flops 4096326144 | bytes 105234656 | solution.py:33
  630.4 17.6 all-gather.2
  658.0 19.9 all_gather.159
  698.0 80.0 %all-gather.16.cloned.1.call-done = bf16[2,1536,3072]{2,1,0:T(8,128)(2,1)} async-done(((bf16[2,96,3072]{2,1,0:T(8,128)(2,1)}), bf16[2,1536,3072]{2,1,0:T(8,128)(2,1)}) %all-gather.16.cloned.1.call-update) | async-done | bytes 18874384 | tf_op jit(solution)/shard_map/all_gather | solution.py:544
  778.0 101.0 %all-gather.18.cloned.1.call-done = bf16[2,3072,1536]{1,0,2:T(2,128)(2,1)} async-done(((bf16[2,3072,96]{1,0,2:T(2,128)(2,1)}), bf16[2,3072,1536]{1,0,2:T(2,128)(2,1)}) %all-gather.18.cloned.1.call-update) | async-done | bytes 18874384 | tf_op jit(solution)/shard_map/all_gather | solution.py:546
  884.7 35.8 conditional.18
  897.2 12.5 broadcast.771.clone
  924.0 258.8 %reduce-scatter.69.cloned.1.call-done = bf16[64,1536]{1,0:T(8,128)(2,1)} async-done(((bf16[128,1536]{1,0:T(8,128)(2,1)}), bf16[64,1536]{1,0:T(8,128)(2,1)}) %reduce-scatter.69.cloned.1.call-update) | async-done | bytes 196624 | tf_op jit(solution)/shard_map/reduce_scatter | solution.py:392
  1207.5 16.0 all_gather.157
  1224.4 71.6 %conditional.17 = (f32[256,3072]{1,0:T(8,128)}, bf16[256,3072]{1,0:T(8,128)(2,1)S(1)}, bf16[256,1536]{1,0:T(8,128)(2,1)S(1)}, f32[128,3072]{1,0:T(8,128)}, bf16[...) conditional(s32[]{:T(128)} %bitcast.212, () %tuple.118, (bf16[2,1536,3072]{2,1,0:T(8,128)(2,1)}, ...), branch_computations={%region_51.52_spmd, %region_52.53_spmd} | conditional | flops 7259559936 | bytes 158134544 | solution.py:33
  1233.1 46.4 %copy.404 = bf16[2,3072,1536]{2,1,0:T(8,128)(2,1)} copy(bf16[2,3072,1536]{1,0,2:T(2,128)(2,1)} %get-tuple-element.871) | data formatting | bytes 37748736 | tf_op jit(solution)/shard_map
  1304.1 13.3 all_gather.153
  1318.4 72.7 %conditional.15 = (f32[256,3072]{1,0:T(8,128)}, bf16[256,3072]{1,0:T(8,128)(2,1)S(1)}, bf16[256,1536]{1,0:T(8,128)(2,1)}, f32[128,3072]{1,0:T(8,128)}, bf16[128,...) conditional(s32[]{:T(128)} %bitcast.206, () %tuple.114, (bf16[2,1536,3072]{2,1,0:T(8,128)(2,1)}, ...), branch_computations={%region_33.34_spmd, %region_34.35_spmd} | conditional | flops 7259559936 | bytes 158134544 | solution.py:33
  1327.3 46.4 %copy.401 = bf16[2,3072,1536]{2,1,0:T(8,128)(2,1)} copy(bf16[2,3072,1536]{1,0,2:T(2,128)(2,1)} %get-tuple-element.861) | data formatting | bytes 37748736 | tf_op jit(solution)/shard_map
  1395.8 21.2 all-gather.3
  1428.1 21.2 reduce-scatter.61.cloned.1.call-done
  1449.4 20.2 reduce-scatter.55.cloned.1.call-done
  1484.9 218.2 %conditional.22 = (f32[2,3072]{1,0:T(2,128)S(1)}, bf16[256,1536]{1,0:T(8,128)(2,1)}, bf16[128,1536]{1,0:T(8,128)(2,1)}, f32[2,1536,3072]{2,1,0:T(8,128)}, f32[2,3072,1536]{1,2,0:T(8,128)}) conditional(s32[]{:T(128)} %bitcast.212, () %tuple.129, (bf16[2,3072,1536]{1,0,2:T(2,128)(2,1)}, bf16[256,1536]{1,0:T(8,128)(2,1)}, f32[256,3072]{1,0:T(8,128)}, ...), branch_computations={%region_117.118_spmd, %region_118.121_spmd} | conditional | flops 14540341248 | bytes 492380416 | solution.py:33
  1485.1 46.3 %copy.417 = bf16[2,3072,1536]{2,1,0:T(8,128)(2,1)} copy(bf16[2,3072,1536]{1,0,2:T(2,128)(2,1)} %get-tuple-element.915) | data formatting | bytes 37748736 | tf_op jit(solution)/shard_map
  1559.2 21.2 pad_maximum_fusion.22
  1580.4 37.2 %copy.486 = f32[2,1536,3072]{2,1,0:T(8,128)} copy(f32[2,1536,3072]{1,2,0:T(8,128)} %pad_maximum_fusion.22) | data formatting | bytes 75497472 | tf_op jit(solution)/shard_map/cond | solution.py:33
  1645.2 21.0 pad_maximum_fusion.23
  1666.2 36.7 copy.488
  1709.8 14.3 all_gather.163
  1724.1 217.1 %conditional.20 = (f32[2,3072]{1,0:T(2,128)}, bf16[256,1536]{1,0:T(8,128)(2,1)}, bf16[128,1536]{1,0:T(8,128)(2,1)}, f32[2,1536,3072]{2,1,0:T(8,128)}, f32[2,3072,1536]{1,2,0:T(8,128)}) conditional(s32[]{:T(128)} %bitcast.206, () %tuple.125, (bf16[2,3072,1536]{1,0,2:T(2,128)(2,1)}, bf16[256,1536]{1,0:T(8,128)(2,1)}, f32[256,3072]{1,0:T(8,128)}, ...), branch_computations={%region_87.88_spmd, %region_88.91_spmd} | conditional | flops 14540341248 | bytes 487760128 | solution.py:33
  1724.1 46.2 %copy.411 = bf16[2,3072,1536]{2,1,0:T(8,128)(2,1)} copy(bf16[2,3072,1536]{1,0,2:T(2,128)(2,1)} %get-tuple-element.894) | data formatting | bytes 37748736 | tf_op jit(solution)/shard_map
  1797.1 21.1 pad_maximum_fusion.11
  1818.2 37.1 %copy.478 = f32[2,1536,3072]{2,1,0:T(8,128)} copy(f32[2,1536,3072]{1,2,0:T(8,128)} %pad_maximum_fusion.11) | data formatting | bytes 75497472 | tf_op jit(solution)/shard_map/cond | solution.py:33
  1883.0 21.0 pad_maximum_fusion.12
  1904.0 36.8 copy.480
  1964.2 19.7 all_gather.162
  1983.9 24.2 conditional.19
  2046.4 122.8 %conditional.21 = (f32[2,2,768]{2,1,0:T(2,128)S(1)}, bf16[256,1536]{1,0:T(8,128)(2,1)S(1)}, bf16[128,1536]{1,0:T(8,128)(2,1)}, f32[2,3,1536,768]{3,2,1,0:T(8,128)}, f32[2,768,1536]{1,2,0:T(8,128)}) conditional(s32[]{:T(128)} %bitcast.206, () %tuple.124, (bf16[384,768]{1,0:T(8,128)(2,1)}, bf16[384,768]{1,0:T(8,128)(2,1)}, f32[12,384,1]{1,0,2:T(8,128)}, ...), branch_computations={%region_97.98_spmd, %region_98.0_spmd} | conditional | flops 8419732992 | bytes 368179616 | solution.py:33
  2053.3 12.9 copy.414
  2110.4 27.9 copy.482
  2182.1 120.0 %conditional.23 = (f32[2,2,768]{2,1,0:T(2,128)S(1)}, bf16[256,1536]{1,0:T(8,128)(2,1)}, bf16[128,1536]{1,0:T(8,128)(2,1)}, f32[2,3,1536,768]{3,2,1,0:T(8,128)}, f32[2,768,1536]{1,2,0:T(8,128)}) conditional(s32[]{:T(128)} %bitcast.212, () %tuple.128, (bf16[384,768]{1,0:T(8,128)(2,1)}, bf16[384,768]{1,0:T(8,128)(2,1)}, f32[12,384,1]{1,0,2:T(8,128)}, ...), branch_computations={%region_127.128_spmd, %region_128.0_spmd} | conditional | flops 8419732992 | bytes 360388960 | solution.py:33
  2189.3 12.7 copy.420
  2243.4 28.3 copy.490
  2319.9 98.3 %reduce-scatter.91.cloned.1.call-done = bf16[64,1536]{1,0:T(8,128)(2,1)} async-done(((bf16[128,1536]{1,0:T(8,128)(2,1)}), bf16[64,1536]{1,0:T(8,128)(2,1)}) %reduce-scatter.91.cloned.1.call-update) | async-done | bytes 196624 | tf_op jit(solution)/shard_map/reduce_scatter | solution.py:443
  2438.6 20.2 reduce-scatter.89.cloned.1.call-done
  2475.4 19.1 all-reduce.7.cloned.1.call-done
  2514.3 32.1 add_convert_fusion.3
  2546.5 42.8 %add_convert_fusion.1 = bf16[2,3072,1536]{1,2,0:T(8,128)(2,1)} fusion(f32[2,3072,1536]{1,2,0:T(8,128)} %get-tuple-element.945, f32[2,3072,1536]{1,2,0:T(8,128)} %get-tuple-element.937, f32[2,3072,1536]{1,2,0:T(8,128)} %get-tuple-element.941), kind=kLoop, calls=%fused_computation.502 | loop fusion | flops 28311552 | bytes 132120576 | tf_op jit(solution)/shard_map/convert_element_type | solution.py:613
  2589.4 42.7 %add_convert_fusion.2 = bf16[2,1536,3072]{2,1,0:T(8,128)(2,1)} fusion(f32[2,1536,3072]{2,1,0:T(8,128)} %get-tuple-element.944, f32[2,1536,3072]{2,1,0:T(8,128)} %get-tuple-element.936, f32[2,1536,3072]{2,1,0:T(8,128)} %get-tuple-element.940), kind=kLoop, calls=%fused_computation.503 | loop fusion | flops 28311552 | bytes 132120576 | tf_op jit(solution)/shard_map/convert_element_type | solution.py:607
  2633.1 14.2 fusion.435
  2667.4 12.9 convolution_reduce_fusion.1
  2680.3 13.1 convolution_reduce_fusion.2
  2693.5 12.9 convolution_reduce_fusion
  2708.4 21.0 reduce-scatter.111.cloned.1.call-done
  2730.8 65.3 %reduce-scatter.103.cloned.1.call-done = bf16[576,2]{1,0:T(8,128)(2,1)} async-done(((bf16[9216,2]{1,0:T(8,128)(2,1)}), bf16[576,2]{1,0:T(8,128)(2,1)}) %reduce-scatter.103.cloned.1.call-update) | async-done | bytes 2320
  2797.7 76.7 %reduce-scatter.97.cloned.1.call-done = bf16[2,768,96]{1,2,0:T(8,128)(2,1)} async-done(((bf16[2,768,1536]{1,2,0:T(8,128)(2,1)}), bf16[2,768,96]{1,2,0:T(8,128)(2,1)}) %reduce-scatter.97.cloned.1.call-update) | async-done | bytes 294928 | tf_op jit(solution)/shard_map/reduce_scatter | solution.py:600
  2876.3 147.6 %reduce-scatter.95.cloned.1.call-done = bf16[2,3,96,768]{3,2,1,0:T(8,128)(2,1)} async-done(((bf16[2,3,1536,768]{3,2,1,0:T(8,128)(2,1)}), bf16[2,3,96,768]{3,2,1,0:T(8,128)(2,1)}) %reduce-scatter.95.cloned.1.call-update) | async-done | bytes 884752 | tf_op jit(solution)/shard_map/reduce_scatter | solution.py:594
  3026.4 196.0 %reduce-scatter.101.cloned.1.call-done = bf16[2,3072,96]{1,2,0:T(8,128)(2,1)} async-done(((bf16[2,3072,1536]{1,2,0:T(8,128)(2,1)}), bf16[2,3072,96]{1,2,0:T(8,128)(2,1)}) %reduce-scatter.101.cloned.1.call-update) | async-done | bytes 1179664 | tf_op jit(solution)/shard_map/reduce_scatter | solution.py:612
  3225.3 195.6 %reduce-scatter.99.cloned.1.call-done = bf16[2,96,3072]{2,1,0:T(8,128)(2,1)} async-done(((bf16[2,1536,3072]{2,1,0:T(8,128)(2,1)}), bf16[2,96,3072]{2,1,0:T(8,128)(2,1)}) %reduce-scatter.99.cloned.1.call-update) | async-done | bytes 1179664 | tf_op jit(solution)/shard_map/reduce_scatter | solution.py:606
  3423.9 270.2 %reduce-scatter.93.cloned.1.call-done = bf16[2,48,9216]{2,1,0:T(8,128)(2,1)} async-done(((bf16[2,768,9216]{2,1,0:T(8,128)(2,1)}), bf16[2,48,9216]{2,1,0:T(8,128)(2,1)}) %reduce-scatter.93.cloned.1.call-update) | async-done | bytes 1769488 | tf_op jit(solution)/shard_map/reduce_scatter | solution.py:588
  (1073 shorter events, 878.7 us)
Async XLA Ops:
  7.2 149.7 %all-gather.10.cloned.1.call-start = ((), (), s32[]{:S(2)}) async-start(), calls=%async_computation.34 | async-start | bytes 30081024 | tf_op jit(solution)/shard_map/all_gather | solution.py:538
  10.7 234.1 %all-reduce.5.cloned.1.call-start = ((), (), s32[]{:S(2)}) async-start(), calls=%async_computation.73 | async-start | bytes 442368 | tf_op jit(solution)/shard_map/psum | solution.py:264
  197.6 80.2 %all-gather.14.cloned.1.call-start = ((), (), s32[]{:S(2)}) async-start(), calls=%async_computation.36 | async-start | bytes 5013504 | tf_op jit(solution)/shard_map/all_gather | solution.py:542
  200.2 189.5 %all-gather.12.cloned.1.call-start = ((), (), s32[]{:S(2)}) async-start(), calls=%async_computation.35 | async-start | bytes 15040512 | tf_op jit(solution)/shard_map/all_gather | solution.py:540
  201.3 267.3 %reduce-scatter.47.cloned.1.call-start = ((), (), s32[]{:S(2)}) async-start(), calls=%async_computation.40 | async-start | bytes 589824 | tf_op jit(solution)/shard_map/reduce_scatter | solution.py:287
  394.0 85.9 %reduce-scatter.45.cloned.1.call-start = ((), (), s32[]{:S(2)}) async-start(), calls=%async_computation.37 | async-start | bytes 1179648 | tf_op jit(solution)/shard_map/reduce_scatter | solution.py:284
  397.8 280.2 %reduce-scatter.53.cloned.1.call-start = ((), (), s32[]{:S(2)}) async-start(), calls=%async_computation.43 | async-start | bytes 589824 | tf_op jit(solution)/shard_map/reduce_scatter | solution.py:287
  547.6 130.4 %reduce-scatter.59.cloned.1.call-start = ((), (), s32[]{:S(2)}) async-start(), calls=%async_computation.46 | async-start | bytes 589824 | tf_op jit(solution)/shard_map/reduce_scatter | solution.py:287
  620.4 66.2 %reduce-scatter.51.cloned.1.call-start = ((), (), s32[]{:S(2)}) async-start(), calls=%async_computation.42 | async-start | bytes 1179648 | tf_op jit(solution)/shard_map/reduce_scatter | solution.py:284
  621.2 65.5 %reduce-scatter.57.cloned.1.call-start = ((), (), s32[]{:S(2)}) async-start(), calls=%async_computation.45 | async-start | bytes 1179648 | tf_op jit(solution)/shard_map/reduce_scatter | solution.py:284
  621.8 156.2 %all-gather.16.cloned.1.call-start = ((), (), s32[]{:S(2)}) async-start(), calls=%async_computation.38 | async-start | bytes 20054016 | tf_op jit(solution)/shard_map/all_gather | solution.py:544
  624.9 254.1 %all-gather.18.cloned.1.call-start = ((), (), s32[]{:S(2)}) async-start(), calls=%async_computation.39 | async-start | bytes 20054016 | tf_op jit(solution)/shard_map/all_gather | solution.py:546
  629.5 553.3 %reduce-scatter.69.cloned.1.call-start = ((), (), s32[]{:S(2)}) async-start(), calls=%async_computation.51 | async-start | bytes 589824 | tf_op jit(solution)/shard_map/reduce_scatter | solution.py:392
  883.6 299.2 %copy-start.7 = (bf16[3,64,1536]{2,1,0:T(8,128)(2,1)S(1)}, bf16[3,64,1536]{2,1,0:T(8,128)(2,1)}, u32[]{:S(2)}) copy-start(bf16[3,64,1536]{2,1,0:T(8,128)(2,1)} %param.41) | copy-start | bytes 1769476
  883.6 299.2 %copy-start.52 = (bf16[64,1536]{1,0:T(8,128)(2,1)S(1)}, bf16[64,1536]{1,0:T(8,128)(2,1)}, u32[]{:S(2)}) copy-start(bf16[64,1536]{1,0:T(8,128)(2,1)} %reduce-scatter.53.cloned.1.call-done) | copy-start | bytes 589828
  883.6 299.2 %copy-start.152 = (f32[1536]{0:T(1024)S(1)}, f32[1536]{0:T(1024)}, u32[]{:S(2)}) copy-start(f32[1536]{0:T(1024)} %copy-done.151) | copy-start | bytes 18436
  883.6 299.2 %copy-start.171 = (f32[1536]{0:T(1024)S(1)}, f32[1536]{0:T(1024)}, u32[]{:S(2)}) copy-start(f32[1536]{0:T(1024)} %get-tuple-element.1087) | copy-start | bytes 18436
  920.5 283.1 %copy-start.1 = (bf16[3,128,1536]{2,1,0:T(8,128)(2,1)S(1)}, bf16[3,128,1536]{2,1,0:T(8,128)(2,1)}, u32[]{:S(2)}) copy-start(bf16[3,128,1536]{2,1,0:T(8,128)(2,1)} %param.40) | copy-start | bytes 3538948
  920.5 283.0 %copy-start.13 = (bf16[128,1536]{1,0:T(8,128)(2,1)S(1)}, bf16[128,1536]{1,0:T(8,128)(2,1)}, u32[]{:S(2)}) copy-start(bf16[128,1536]{1,0:T(8,128)(2,1)} %reduce-scatter.57.cloned.1.call-done) | copy-start | bytes 1179652
  920.5 283.0 %copy-start.16 = (bf16[128,1536]{1,0:T(8,128)(2,1)S(1)}, bf16[128,1536]{1,0:T(8,128)(2,1)}, u32[]{:S(2)}) copy-start(bf16[128,1536]{1,0:T(8,128)(2,1)} %reduce-scatter.45.cloned.1.call-done) | copy-start | bytes 1179652
  920.5 283.0 %copy-start.18 = (bf16[128,1536]{1,0:T(8,128)(2,1)S(1)}, bf16[128,1536]{1,0:T(8,128)(2,1)}, u32[]{:S(2)}) copy-start(bf16[128,1536]{1,0:T(8,128)(2,1)} %reduce-scatter.51.cloned.1.call-done) | copy-start | bytes 1179652
  920.6 283.0 %copy-start.149 = (f32[1536]{0:T(1024)S(1)}, f32[1536]{0:T(1024)}, u32[]{:S(2)}) copy-start(f32[1536]{0:T(1024)} %copy-done.148) | copy-start | bytes 18436
  920.6 283.0 %copy-start.163 = (f32[1536]{0:T(1024)S(1)}, f32[1536]{0:T(1024)}, u32[]{:S(2)}) copy-start(f32[1536]{0:T(1024)} %get-tuple-element.1095) | copy-start | bytes 18436
  920.6 283.0 %copy-start.166 = (f32[1536]{0:T(1024)S(1)}, f32[1536]{0:T(1024)}, u32[]{:S(2)}) copy-start(f32[1536]{0:T(1024)} %get-tuple-element.1083) | copy-start | bytes 18436
  920.6 283.0 %copy-start.169 = (f32[1536]{0:T(1024)S(1)}, f32[1536]{0:T(1024)}, u32[]{:S(2)}) copy-start(f32[1536]{0:T(1024)} %get-tuple-element.1071) | copy-start | bytes 18436
  920.6 283.0 %copy-start.192 = (f32[1536]{0:T(1024)S(1)}, f32[1536]{0:T(1024)}, u32[]{:S(2)}) copy-start(f32[1536]{0:T(1024)} %get-tuple-element.1065) | copy-start | bytes 18436
  920.6 283.0 %copy-start.252 = (f32[128]{0:T(128)S(1)}, f32[128]{0:T(128)}, u32[]{:S(2)}) copy-start(f32[128]{0:T(128)} %copy-done.251) | copy-start | bytes 1540
  920.6 283.0 %copy-start.269 = (f32[128]{0:T(128)S(1)}, f32[128]{0:T(128)}, u32[]{:S(2)}) copy-start(f32[128]{0:T(128)} %copy-done.268) | copy-start | bytes 1540
  920.7 282.9 %reduce-scatter.71.cloned.1.call-start = ((), (), s32[]{:S(2)}) async-start(), calls=%async_computation.52 | async-start | bytes 1179648 | tf_op jit(solution)/shard_map/reduce_scatter | solution.py:389
  921.2 495.9 %reduce-scatter.63.cloned.1.call-start = ((), (), s32[]{:S(2)}) async-start(), calls=%async_computation.48 | async-start | bytes 589824 | tf_op jit(solution)/shard_map/reduce_scatter | solution.py:315
  922.0 284.2 %copy-start.240 = (f32[64]{0:T(128)}, f32[64]{0:T(128)S(1)}, u32[]{:S(2)}) copy-start(f32[64]{0:T(128)S(1)} %broadcast_multiply_fusion.30) | copy-start | bytes 772
  922.6 283.6 %copy-start.242 = (f32[64]{0:T(128)}, f32[64]{0:T(128)S(1)}, u32[]{:S(2)}) copy-start(f32[64]{0:T(128)S(1)} %broadcast_multiply_fusion.32) | copy-start | bytes 772
  923.2 283.0 %copy-start.248 = (f32[128]{0:T(128)}, f32[128]{0:T(128)S(1)}, u32[]{:S(2)}) copy-start(f32[128]{0:T(128)S(1)} %broadcast_multiply_fusion.12) | copy-start | bytes 1540
  923.9 282.3 %copy-start.250 = (f32[128]{0:T(128)}, f32[128]{0:T(128)S(1)}, u32[]{:S(2)}) copy-start(f32[128]{0:T(128)S(1)} %broadcast_multiply_fusion.14) | copy-start | bytes 1540
  923.9 282.3 %copy-start.188 = (f32[1536]{0:T(1024)S(1)}, f32[1536]{0:T(1024)}, u32[]{:S(2)}) copy-start(f32[1536]{0:T(1024)} %get-tuple-element.1089) | copy-start | bytes 18436
  923.9 282.4 %copy-start.190 = (f32[1536]{0:T(1024)S(1)}, f32[1536]{0:T(1024)}, u32[]{:S(2)}) copy-start(f32[1536]{0:T(1024)} %get-tuple-element.1077) | copy-start | bytes 18436
  923.9 282.4 %copy-start.219 = (f32[1536]{0:T(1024)S(1)}, f32[1536]{0:T(1024)}, u32[]{:S(2)}) copy-start(f32[1536]{0:T(1024)} %get-tuple-element.1076) | copy-start | bytes 18436
  923.9 282.4 %copy-start.220 = (f32[1536]{0:T(1024)S(1)}, f32[1536]{0:T(1024)}, u32[]{:S(2)}) copy-start(f32[1536]{0:T(1024)} %get-tuple-element.1088) | copy-start | bytes 18436
  923.9 493.2 %reduce-scatter.67.cloned.1.call-start = ((), (), s32[]{:S(2)}) async-start(), calls=%async_computation.50 | async-start | bytes 589824 | tf_op jit(solution)/shard_map/reduce_scatter | solution.py:315
  1296.7 120.5 %reduce-scatter.65.cloned.1.call-start = ((), (), s32[]{:S(2)}) async-start(), calls=%async_computation.49 | async-start | bytes 589824 | tf_op jit(solution)/shard_map/reduce_scatter | solution.py:315
  1391.8 36.3 reduce-scatter.49.cloned.1.call-start
  1392.4 57.0 %reduce-scatter.61.cloned.1.call-start = ((), (), s32[]{:S(2)}) async-start(), calls=%async_computation.47 | async-start | bytes 1179648 | tf_op jit(solution)/shard_map/reduce_scatter | solution.py:312
  1393.2 76.5 %reduce-scatter.55.cloned.1.call-start = ((), (), s32[]{:S(2)}) async-start(), calls=%async_computation.44 | async-start | bytes 1179648 | tf_op jit(solution)/shard_map/reduce_scatter | solution.py:312
  1393.7 615.1 %reduce-scatter.85.cloned.1.call-start = ((), (), s32[]{:S(2)}) async-start(), calls=%async_computation.59 | async-start | bytes 589824 | tf_op jit(solution)/shard_map/reduce_scatter | solution.py:392
  1703.2 305.7 %reduce-scatter.77.cloned.1.call-start = ((), (), s32[]{:S(2)}) async-start(), calls=%async_computation.55 | async-start | bytes 589824 | tf_op jit(solution)/shard_map/reduce_scatter | solution.py:392
  1941.2 90.3 %reduce-scatter.87.cloned.1.call-start = ((), (), s32[]{:S(2)}) async-start(), calls=%async_computation.60 | async-start | bytes 1179648 | tf_op jit(solution)/shard_map/reduce_scatter | solution.py:389
  1941.9 89.6 %reduce-scatter.79.cloned.1.call-start = ((), (), s32[]{:S(2)}) async-start(), calls=%async_computation.56 | async-start | bytes 1179648 | tf_op jit(solution)/shard_map/reduce_scatter | solution.py:389
  1946.1 363.6 %reduce-scatter.75.cloned.1.call-start = ((), (), s32[]{:S(2)}) async-start(), calls=%async_computation.54 | async-start | bytes 589824 | tf_op jit(solution)/shard_map/reduce_scatter | solution.py:443
  2008.2 306.7 %reduce-scatter.73.cloned.1.call-start = ((), (), s32[]{:S(2)}) async-start(), calls=%async_computation.53 | async-start | bytes 1179648 | tf_op jit(solution)/shard_map/reduce_scatter | solution.py:440
  2008.8 311.1 %reduce-scatter.83.cloned.1.call-start = ((), (), s32[]{:S(2)}) async-start(), calls=%async_computation.58 | async-start | bytes 589824 | tf_op jit(solution)/shard_map/reduce_scatter | solution.py:443
  2170.1 248.1 %reduce-scatter.91.cloned.1.call-start = ((), (), s32[]{:S(2)}) async-start(), calls=%async_computation.62 | async-start | bytes 589824 | tf_op jit(solution)/shard_map/reduce_scatter | solution.py:443
  2302.2 136.4 %reduce-scatter.81.cloned.1.call-start = ((), (), s32[]{:S(2)}) async-start(), calls=%async_computation.57 | async-start | bytes 1179648 | tf_op jit(solution)/shard_map/reduce_scatter | solution.py:440
  2302.9 155.8 %reduce-scatter.89.cloned.1.call-start = ((), (), s32[]{:S(2)}) async-start(), calls=%async_computation.61 | async-start | bytes 1179648 | tf_op jit(solution)/shard_map/reduce_scatter | solution.py:440
  2312.8 181.7 %all-reduce.7.cloned.1.call-start = ((), (), s32[]{:S(2)}) async-start(), calls=%async_computation.74 | async-start | bytes 294912 | tf_op jit(solution)/shard_map/psum | solution.py:474
  2471.9 175.5 %reduce-scatter.109.cloned.1.call-start = ((), (), s32[]{:S(2)}) async-start(), calls=%async_computation.71 | async-start | bytes 835584
  2474.0 180.4 %reduce-scatter.105.cloned.1.call-start = ((), (), s32[]{:S(2)}) async-start(), calls=%async_computation.69 | async-start | bytes 208896
  2475.4 231.6 %reduce-scatter.107.cloned.1.call-start = ((), (), s32[]{:S(2)}) async-start(), calls=%async_computation.70 | async-start | bytes 417792
  2497.7 231.7 %reduce-scatter.111.cloned.1.call-start = ((), (), s32[]{:S(2)}) async-start(), calls=%async_computation.72 | async-start | bytes 417792
  2498.8 297.4 %reduce-scatter.103.cloned.1.call-start = ((), (), s32[]{:S(2)}) async-start(), calls=%async_computation.68 | async-start | bytes 2506752
  2501.9 372.6 %reduce-scatter.97.cloned.1.call-start = ((), (), s32[]{:S(2)}) async-start(), calls=%async_computation.65 | async-start | bytes 5013504 | tf_op jit(solution)/shard_map/reduce_scatter | solution.py:600
  2514.3 509.6 %reduce-scatter.95.cloned.1.call-start = ((), (), s32[]{:S(2)}) async-start(), calls=%async_computation.64 | async-start | bytes 15040512 | tf_op jit(solution)/shard_map/reduce_scatter | solution.py:594
  2546.5 675.9 %reduce-scatter.101.cloned.1.call-start = ((), (), s32[]{:S(2)}) async-start(), calls=%async_computation.67 | async-start | bytes 20054016 | tf_op jit(solution)/shard_map/reduce_scatter | solution.py:612
  2589.4 831.6 %reduce-scatter.99.cloned.1.call-start = ((), (), s32[]{:S(2)}) async-start(), calls=%async_computation.66 | async-start | bytes 20054016 | tf_op jit(solution)/shard_map/reduce_scatter | solution.py:606
  2632.2 1061.8 %reduce-scatter.93.cloned.1.call-start = ((), (), s32[]{:S(2)}) async-start(), calls=%async_computation.63 | async-start | bytes 30081024 | tf_op jit(solution)/shard_map/reduce_scatter | solution.py:588
  (248 other events, 10163.8 us)
Sparse Core Ops, SparseCore 0:
  10.8 146.0 all-gather.9
  197.7 22.9 all-reduce.4
  223.6 54.1 all-gather.13
  280.5 109.1 all-gather.11
  394.1 58.5 reduce-scatter.46
  455.4 17.4 reduce-scatter.44
  547.7 12.2 reduce-scatter.52
  620.6 9.4 reduce-scatter.58
  632.9 17.4 reduce-scatter.50
  653.1 25.6 reduce-scatter.56
  681.0 96.9 all-gather.15
  780.0 98.9 all-gather.17
  920.8 261.9 reduce-scatter.68
  1185.6 17.9 reduce-scatter.70
  1205.7 17.4 reduce-scatter.62
  1296.8 15.4 reduce-scatter.66
  1391.9 13.2 reduce-scatter.64
  1407.4 17.4 reduce-scatter.48
  1427.7 21.6 reduce-scatter.60
  1452.1 17.4 reduce-scatter.54
  1703.3 16.2 reduce-scatter.84
  1941.3 16.7 reduce-scatter.76
  1960.3 24.4 reduce-scatter.86
  1987.6 17.4 reduce-scatter.78
  2008.3 108.2 reduce-scatter.74
  2119.3 21.6 reduce-scatter.72
  2169.5 111.4 reduce-scatter.82
  2302.3 115.8 reduce-scatter.90
  2421.0 17.4 reduce-scatter.80
  2441.3 17.4 reduce-scatter.88
  2472.0 22.4 all-reduce.6
  2498.6 56.5 reduce-scatter.108
  2559.0 52.6 reduce-scatter.104
  2616.2 54.5 reduce-scatter.106
  2674.8 54.6 reduce-scatter.110
  2734.1 61.9 reduce-scatter.102
  2799.8 74.5 reduce-scatter.96
  2879.2 144.6 reduce-scatter.94
  3028.4 193.9 reduce-scatter.100
  3227.1 193.8 reduce-scatter.98
  3425.7 268.3 reduce-scatter.92
where the time goes:
time: 3730 us; the launch traced here: 3700 us
  waiting for transfers between devices  1870 us (50%)
  local copies, waits for them, and re-layouts  618 us (17%)
  other arithmetic  413 us (11%)
  blocking collectives  393 us (11%)
  matrix products  368 us (10%)
    another operation x41, local copies, waits for them, and re-layouts  303 us
    reduce_scatter x1, waiting for transfers between devices, body(): lax.psum_scatter(dense.astype(jnp.bfloat16), 'dp', scatter_dimension=1, t...  270 us
    reduce_scatter x3, waiting for transfers between devices, backward_step(): lax.psum_scatter(mlp_grads[4].astype(jnp.bfloat16), 'mp', scatter_dimensi...  259 us
    cond x8, local copies, waits for them, and re-layouts, when_live(): return lax.cond(live_flag, function, skipped, operands)  223 us
    reduce_scatter x1, waiting for transfers between devices, body(): lax.psum_scatter(totals[7].astype(jnp.bfloat16), 'dp', scatter_dimension=...  196 us
    reduce_scatter x1, waiting for transfers between devices, body(): lax.psum_scatter(totals[5].astype(jnp.bfloat16), 'dp', scatter_dimension=...  196 us
    reduce_scatter x1, waiting for transfers between devices, body(): lax.psum_scatter(totals[1].astype(jnp.bfloat16), 'dp', scatter_dimension=...  148 us
    all_gather x1, waiting for transfers between devices, body(): lax.all_gather(shards[0], 'dp', axis=1, tiled=True)  144 us
  transfers between devices with their start and end apart: 41, of which 20 were waited for; matrix products, arithmetic and copies ran while one was open for 27% of the time, Pallas kernels for 0%

commit v1 on v0

v1 whole, which is shorter than its diff:
```python
import functools

import jax
import jax.numpy as jnp
from jax import lax
from jax.experimental import pallas as pl
from jax.experimental.pallas import tpu as pltpu
from jax.sharding import PartitionSpec as P

HEAD_DIM = 64
EPSILON = 1e-06
F32 = jnp.float32
BF16 = jnp.bfloat16


def layer_norm(values):
    center = values - jnp.mean(values, axis=-1, keepdims=True)
    inverse = lax.rsqrt(jnp.mean(center * center, axis=-1, keepdims=True) + EPSILON)
    return (center * inverse, inverse)


def norm_back(normed, inverse, upstream):
    mean_up = jnp.mean(upstream, axis=-1, keepdims=True)
    mean_cross = jnp.mean(upstream * normed, axis=-1, keepdims=True)
    return inverse * (upstream - mean_up - normed * mean_cross)


def gelu_tanh(values):
    return jax.nn.gelu(values, approximate=True)


def dot(left, right, dims):
    return lax.dot_general(left, right, (dims, ((), ())), preferred_element_type=F32)


NN = ((1,), (0,))
NT = ((1,), (1,))
TN = ((0,), (0,))


def join_rows(text_ref, image_ref):
    width = text_ref.shape[-1]
    return jnp.concatenate(
        [text_ref[...].reshape(-1, width), image_ref[...].reshape(-1, width)], axis=0
    )


def attention_kernel(qi, ki, vi, qt, kt, vt, oi, ot):
    query, key, value = join_rows(qt, qi), join_rows(kt, ki), join_rows(vt, vi)
    width = query.shape[1]
    head_of = lax.broadcasted_iota(jnp.int32, query.shape, 1) // HEAD_DIM
    out = jnp.zeros(query.shape, F32)
    for head in range(width // HEAD_DIM):
        inside = head_of == head
        scores = dot(jnp.where(inside, query, jnp.zeros_like(query)), key, NT) * HEAD_DIM**-0.5
        raised = jnp.exp(scores - jnp.max(scores, axis=1, keepdims=True))
        probs = raised * (1.0 / jnp.sum(raised, axis=1, keepdims=True))
        out = jnp.where(inside, dot(probs.astype(BF16), value, NN), out)
    text_rows = ot.shape[0] * ot.shape[1]
    ot[...] = out[:text_rows].astype(BF16).reshape(ot.shape)
    oi[...] = out[text_rows:].astype(BF16).reshape(oi.shape)


def attention_back_kernel(qi, ki, vi, gi, qt, kt, vt, gt, di, dt):
    query, key, value, grad = (
        join_rows(qt, qi),
        join_rows(kt, ki),
        join_rows(vt, vi),
        join_rows(gt, gi),
    )
    width = query.shape[1]
    head_of = lax.broadcasted_iota(jnp.int32, query.shape, 1) // HEAD_DIM
    blank = jnp.zeros_like(query)
    dq, dk, dv = (jnp.zeros(query.shape, F32) for _ in range(3))
    scale = HEAD_DIM**-0.5
    for head in range(width // HEAD_DIM):
        inside = head_of == head
        scores = dot(jnp.where(inside, key, blank), query, NT) * scale
        raised = jnp.exp(scores - jnp.max(scores, axis=0, keepdims=True))
        probs = raised * (1.0 / jnp.sum(raised, axis=0, keepdims=True))
        grad_probs = dot(jnp.where(inside, value, blank), grad, NT)
        delta = jnp.sum(probs * grad_probs, axis=0, keepdims=True)
        grad_scores = (probs * (grad_probs - delta)).astype(BF16)
        dv = jnp.where(inside, dot(probs.astype(BF16), grad, NN), dv)
        dk = jnp.where(inside, dot(grad_scores, query, NN) * scale, dk)
        dq = jnp.where(inside, dot(grad_scores, key, TN) * scale, dq)
    text_rows = dt.shape[1] * dt.shape[2]
    for place, value_now in enumerate((dq, dk, dv)):
        low = value_now.astype(BF16)
        dt[place] = low[:text_rows].reshape(dt.shape[1:])
        di[place] = low[text_rows:].reshape(di.shape[1:])


def head_block(width):
    return 128 if width % 128 == 0 else width


def picked(array, place, lanes, first=0):
    groups, rows = array.shape[1], array.shape[3]
    return pl.BlockSpec(
        (None, groups, None, rows, lanes), lambda seq, block: (place, 0, seq + first, 0, block)
    )


def plain(array, lanes, first=0):
    groups, rows = array.shape[0], array.shape[2]
    return pl.BlockSpec(
        (groups, None, rows, lanes), lambda seq, block: (0, seq + first, 0, block)
    )


def attention_forward(image, text):
    seqs, width = image.shape[2], image.shape[4]
    lanes = head_block(width)
    shapes = [jax.ShapeDtypeStruct(a.shape[1:], BF16) for a in (image, text)]
    return pl.pallas_call(
        attention_kernel,
        grid=(seqs, width // lanes),
        in_specs=[picked(a, place, lanes) for a in (image, text) for place in range(3)],
        out_specs=[plain(s, lanes) for s in shapes],
        out_shape=shapes,
        compiler_params=pltpu.CompilerParams(
            dimension_semantics=("parallel", "parallel"), vmem_limit_bytes=48 * 2**20
        ),
        name="attention_forward",
    )(image, image, image, text, text, text)


def attention_backward(image, text, image_grad, text_grad, first):
    width = image.shape[4]
    lanes = head_block(width)

    def whole(shape):
        return pl.BlockSpec(
            (3, shape[1], None, shape[3], lanes), lambda seq, block: (0, 0, seq, 0, block)
        )

    specs = []
    for array, grad in ((image, image_grad), (text, text_grad)):
        specs += [picked(array, place, lanes, first) for place in range(3)]
        specs.append(plain(grad, lanes, first))
    shapes = [a.shape[:2] + (1,) + a.shape[3:] for a in (image, text)]
    return pl.pallas_call(
        attention_back_kernel,
        grid=(1, width // lanes),
        in_specs=specs,
        out_specs=[whole(shape) for shape in shapes],
        out_shape=[jax.ShapeDtypeStruct(shape, BF16) for shape in shapes],
        compiler_params=pltpu.CompilerParams(
            dimension_semantics=("parallel", "parallel"), vmem_limit_bytes=48 * 2**20
        ),
        name="attention_backward",
    )(image, image, image, image_grad, text, text, text, text_grad)


def ring_of(chips):
    wide = 1
    while (2 * wide) ** 2 <= chips:
        wide *= 2
    long = chips // wide
    order = [row * wide for row in range(long)]
    for turn, row in enumerate(reversed(range(long))):
        across = list(range(1, wide))
        order += [row * wide + col for col in (across if turn % 2 == 0 else across[::-1])]
    return order


class Ring:
    def __init__(self, stream, dp, kind=BF16):
        self.kind, self.dp = kind, dp
        self.chips = dp // 2
        order = ring_of(self.chips)
        me = lax.axis_index("dp")
        chip, self.core = me // 2, me % 2
        way = 1 if stream == 0 else -1
        self.hop = [
            (2 * order[i] + c, 2 * order[(i + way) % self.chips] + c)
            for i in range(self.chips)
            for c in range(2)
        ]
        self.targets = []
        for step in range(self.chips):
            at = jnp.int32(0)
            for spot, here in enumerate(order):
                at = at + jnp.where(chip == here, order[(spot - way * (1 + step)) % self.chips], 0)
            self.targets.append(at)
        self.views, self.flying = [], []
        self.step = 0
        self.result = None

    def give(self, grad):
        view = grad.astype(self.kind).reshape((self.chips, 2, -1, grad.shape[-1]))
        gift = lax.dynamic_index_in_dim(view, 1 - self.core, 1, False)
        self.views.append(view)
        self.flying.append(lax.ppermute(gift, "dp", [(i, i ^ 1) for i in range(self.dp)]))

    def block(self):
        at = self.targets[self.step]
        parts = []
        for view, got in zip(self.views, self.got):
            start = (at, self.core, 0, 0)
            kept = lax.dynamic_slice(view, start, (1, 1) + view.shape[2:])[0, 0]
            came = lax.dynamic_index_in_dim(got, at, 0, False)
            parts.append(kept.astype(F32) + came.astype(F32))
        return jnp.concatenate(parts, axis=1)

    def advance(self):
        if self.step == 0:
            self.got = self.flying
            total = self.block()
        else:
            total = self.flying[0].astype(F32) + self.block()
        if self.step == self.chips - 1:
            self.result = total
            self.flying = []
        else:
            self.flying = [lax.ppermute(total.astype(self.kind), "dp", self.hop)]
        self.step += 1

    def finish(self):
        while self.result is None:
            self.advance()
        return self.result


def beat(value, *groups):
    for number, group in enumerate(groups):
        if group[0].result is not None:
            continue
        value, flights = lax.optimization_barrier((value, [ring.flying for ring in group]))
        for ring, flight in zip(group, flights):
            ring.flying = flight
            ring.advance()
        if group[0].result is None:
            return value
        if number + 1 == len(groups) or not groups[number + 1][0].flying:
            return value
    return value


def tie(*values):
    return lax.optimization_barrier(values)


def body(
    mp,
    dp,
    image_tokens,
    text_tokens,
    condition,
    live_table,
    ada_weight,
    ada_bias,
    qkv_weight,
    qv_bias,
    proj_weight,
    proj_bias,
    fc1_weight,
    fc1_bias,
    fc2_weight,
    fc2_bias,
    image_cotangent,
    text_cotangent,
):
    seqs, width = image_tokens.shape[0], image_tokens.shape[2]
    my_dp = lax.axis_index("dp")
    swap = [(0, 1), (1, 0)]

    def share(rows):
        if mp == 2:
            return jnp.stack([rows, lax.ppermute(rows, "mp", swap)])
        return lax.all_gather(rows, "mp", axis=0, tiled=False)

    def collect(parts):
        if mp == 2:
            return parts[0] + lax.ppermute(parts[1].astype(BF16), "mp", swap).astype(F32)
        low = parts.astype(BF16)
        return lax.psum_scatter(low, "mp", scatter_dimension=0, tiled=False).astype(F32)

    def sum_mp(values):
        if mp == 2:
            return values + lax.ppermute(values, "mp", swap)
        return lax.psum(values, "mp")

    def flat(array):
        return array.reshape(-1, array.shape[-1])

    def gather_small(rows):
        reach = 1
        while reach < dp:
            other = lax.ppermute(rows, "dp", [(i, i ^ reach) for i in range(dp)])
            low_half = (my_dp & reach) == 0
            rows = jnp.concatenate(
                [jnp.where(low_half, rows, other), jnp.where(low_half, other, rows)], axis=0
            )
            reach *= 2
        return rows

    def gather_vector(vector):
        vector = jnp.pad(vector, (0, -vector.size % 2048)).reshape(1, -1, 128)
        return lax.all_gather(vector, "dp", axis=0, tiled=True).reshape(dp, -1)

    small = [condition, ada_bias, qv_bias, proj_bias, fc1_bias, fc2_bias]
    sizes = [a.size for a in small]
    packed = jnp.concatenate([a.astype(BF16).reshape(-1) for a in small])
    packed = jnp.pad(packed, (0, -packed.size % 2048)).reshape(1, -1, 128)
    packed = gather_small(packed).reshape(dp, -1)
    pieces, at = [], 0
    for array, size in zip(small, sizes):
        pieces.append(packed[:, at : at + size].reshape((dp,) + array.shape))
        at += size
    cond_all = pieces[0].reshape(dp * seqs, -1)
    ada_biases, proj_biases, up_biases, down_biases = (
        jnp.moveaxis(pieces[i], 0, 1).reshape(2, -1).astype(F32) for i in (1, 3, 4, 5)
    )
    qv_biases = jnp.moveaxis(pieces[2], 0, 2).reshape(2, 2, -1).astype(F32)

    attention_low = [qkv_weight.astype(BF16), jnp.swapaxes(proj_weight.astype(BF16), 1, 2)[:, None]]
    attention_full = lax.all_gather(
        jnp.concatenate(attention_low, axis=1), "dp", axis=2, tiled=True
    )
    up_full = lax.all_gather(fc1_weight.astype(BF16), "dp", axis=1, tiled=True)
    down_full = lax.all_gather(
        jnp.swapaxes(fc2_weight.astype(BF16), 1, 2), "dp", axis=1, tiled=True
    )

    ada_low = ada_weight.astype(BF16)
    ada_rows = ada_low.shape[1]
    silu_all = jax.nn.silu(cond_all.astype(F32)).astype(BF16)
    silu_mine = lax.dynamic_slice_in_dim(silu_all, my_dp * ada_rows, ada_rows, axis=1)
    mod_rings = []
    for s in range(2):
        mod_rings.append(Ring(s, dp, F32))
        mod_rings[s].give(dot(silu_mine, ada_low[s], NN).reshape(-1, 128))
    modulation = jnp.stack([ring.finish().reshape(seqs, -1) for ring in mod_rings], axis=1)
    modulation = sum_mp(modulation) + ada_biases
    modulation = modulation.reshape(seqs, 2, 6, 1, width)

    def mod(stream, which):
        return modulation[:, stream, which]

    live = live_table[0].astype(F32)[:, None, None]
    tokens = [image_tokens.astype(F32), text_tokens.astype(F32)]
    cotangents = [image_cotangent.astype(F32) * live, text_cotangent.astype(F32) * live]

    first_norm, first_inverse, joint_in = [], [], []
    for s in range(2):
        normed, inverse = layer_norm(tokens[s])
        first_norm.append(normed)
        first_inverse.append(inverse)
        joint_in.append(share((normed * (1.0 + mod(s, 1)) + mod(s, 0)).astype(BF16)))

    branch_grad = [cotangents[s] * mod(s, 5) for s in range(2)]
    branch_low, joint_in = tie([b.astype(BF16) for b in branch_grad], joint_in)
    down_up = [share(branch_low[s]) for s in range(2)]

    qkv = []
    for s in range(2):
        rows = flat(joint_in[s])
        products = []
        for t in range(3):
            product = dot(rows, attention_full[s, t], NN)
            if t != 1:
                product = product + qv_biases[s, t // 2]
            products.append(product.astype(BF16))
        qkv.append(jnp.stack(products).reshape((3,) + joint_in[s].shape[:3] + (-1,)))
    attended = attention_forward(qkv[0], qkv[1])

    residual, second_norm, second_inverse, first_branch, mlp_in = [], [], [], [], []
    for s in range(2):
        product = dot(flat(attended[s]), attention_full[s, 3], NT).reshape(joint_in[s].shape)
        branch = collect(product) + proj_biases[s]
        resid = tokens[s] + mod(s, 2) * branch
        normed, inverse = layer_norm(resid)
        first_branch.append(branch)
        residual.append(resid)
        second_norm.append(normed)
        second_inverse.append(inverse)
        mlp_in.append(share((normed * (1.0 + mod(s, 4)) + mod(s, 3)).astype(BF16)))

    pre_active, active = [None, None], [None, None]
    down_rings, up_rings, last_rings = ([Ring(s, dp) for s in range(2)] for unused in range(3))
    for s in (1, 0):
        pre_active[s] = dot(flat(mlp_in[s]), up_full[s], NN) + up_biases[s]
        active[s] = gelu_tanh(pre_active[s]).astype(BF16)
        grad = dot(flat(down_up[s]), active[s], TN).astype(BF16)
        grad, down_up = tie(grad, down_up)
        down_rings[s].give(grad)

    grad_pre, back = [], []
    for s in range(2):
        grad_active = dot(flat(down_up[s]), down_full[s], NN)
        unused, pullback = jax.vjp(gelu_tanh, pre_active[s])
        grad_pre.append(pullback(grad_active)[0].astype(BF16))
        grad_pre[s] = beat(grad_pre[s], down_rings)
        back.append(dot(grad_pre[s], up_full[s], NT).reshape(mlp_in[s].shape))
        if s == 0:
            back[0], down_up[1] = beat((back[0], down_up[1]), down_rings)
            back[0] = collect(back[0])
    grad_pre, back[1] = beat((grad_pre, back[1]), down_rings)
    back[1] = collect(back[1])
    up_grad = dot(flat(mlp_in[0]), grad_pre[0], TN).astype(BF16)
    up_grad, grad_pre[1] = beat((up_grad, grad_pre[1]), down_rings)
    up_rings[0].give(up_grad)
    up_rings[1].give(dot(flat(mlp_in[1]), grad_pre[1], TN).astype(BF16))
    back = beat(back, down_rings, up_rings)

    resid_grad, attention_low = [], []
    for s in range(2):
        grad_one = cotangents[s] + norm_back(
            second_norm[s], second_inverse[s], back[s] * (1.0 + mod(s, 4))
        )
        resid_grad.append(grad_one)
        attention_low.append((grad_one * mod(s, 2)).astype(BF16))
    resid_grad, attention_low = beat((resid_grad, attention_low), down_rings, up_rings)
    active, attention_low = tie(active, attention_low)
    attention_low = [share(rows) for rows in attention_low]
    shift_two, scale_two, gate_one, proj_bias_grad = [], [], [], []
    for s in range(2):
        shift_two.append(jnp.sum(back[s], axis=1))
        scale_two.append(jnp.sum(back[s] * second_norm[s], axis=1))
        gate_one.append(jnp.sum(resid_grad[s] * first_branch[s], axis=1))
        proj_bias_grad.append(jnp.sum(resid_grad[s] * mod(s, 2), axis=(0, 1)))
    up_bias_grad = [jnp.sum(grad_pre[s].astype(F32), axis=0) for s in range(2)]
    down_sum = [None, None]
    down_sum[0] = dot(active[0], down_full[0], NT).reshape(mlp_in[0].shape)
    down_sum[0], active[1] = beat((down_sum[0], active[1]), down_rings, up_rings)
    down_sum[1] = dot(active[1], down_full[1], NT).reshape(mlp_in[1].shape)
    down_sum = beat(down_sum, down_rings, up_rings)
    attention_low, down_sum = beat((attention_low, down_sum), down_rings, up_rings)
    down_sum = [collect(down_sum[s]) for s in range(2)]

    mixed = [
        dot(flat(attention_low[s]), attention_full[s, 3], NN).astype(BF16).reshape(attended[s].shape)
        for s in range(2)
    ]
    proj_grad = [dot(flat(attention_low[s]), flat(attended[s]), TN).astype(BF16) for s in range(2)]
    mixed, proj_grad = beat((mixed, proj_grad), down_rings, up_rings)
    for s in range(2):
        last_rings[s].give(proj_grad[s])
    grad_qkv = []
    for n in range(seqs):
        piece = attention_backward(qkv[0], qkv[1], mixed[0], mixed[1], n)
        piece, mixed = beat((piece, mixed), down_rings, up_rings)
        grad_qkv.append(piece)
    grad_qkv = [jnp.concatenate([g[s] for g in grad_qkv], axis=2) for s in range(2)]
    grad_qkv, down_sum = tie(grad_qkv, down_sum)

    back, qv_bias_grad = [], []
    for s in range(2):
        grad_rows = [flat(grad_qkv[s][t]) for t in range(3)]
        total = sum(dot(grad_rows[t], attention_full[s, t], NT) for t in range(3))
        total, grad_rows = tie(total, grad_rows)
        back.append(collect(total.reshape(joint_in[s].shape)))
        for t in range(3):
            last_rings[s].give(dot(flat(joint_in[s]), grad_rows[t], TN).astype(BF16))
        qv_bias_grad.append(
            jnp.stack([jnp.sum(grad_rows[t].astype(F32), axis=0) for t in (0, 2)])
        )
    while up_rings[0].result is None:
        beat((), down_rings, up_rings)
    beat((), last_rings)
    outputs, gate_two = [], []
    for s in range(2):
        branch = down_sum[s] + down_biases[s]
        outputs.append((live * (residual[s] + mod(s, 5) * branch)).astype(BF16))
        gate_two.append(jnp.sum(cotangents[s] * branch, axis=1))
    beat((), last_rings)
    back, gate_two = tie(back, gate_two)
    shift_one, scale_one, input_grads = [], [], []
    for s in range(2):
        shift_one.append(jnp.sum(back[s], axis=1))
        scale_one.append(jnp.sum(back[s] * first_norm[s], axis=1))
        input_grads.append(
            resid_grad[s]
            + norm_back(first_norm[s], first_inverse[s], back[s] * (1.0 + mod(s, 1)))
        )

    fc1_out = jnp.stack([ring.finish() for ring in up_rings])
    fc2_out = jnp.swapaxes(jnp.stack([ring.finish() for ring in down_rings]), 1, 2)
    last = jnp.stack([ring.finish() for ring in last_rings])
    last = jnp.moveaxis(last.reshape(2, last.shape[1], 4, -1), 2, 1)
    qkv_out = last[:, 1:]
    proj_out = jnp.swapaxes(last[:, 0], 1, 2)

    mod_rows = jnp.stack(
        [
            jnp.stack([a[s] for a in (shift_one, scale_one, gate_one, shift_two, scale_two, gate_two)], axis=1)
            for s in range(2)
        ],
        axis=1,
    )
    down_bias_grad = [jnp.sum(branch_grad[s], axis=(0, 1)) for s in range(2)]
    token_sums = jnp.concatenate(
        [mod_rows.reshape(-1), jnp.stack(proj_bias_grad).reshape(-1), jnp.stack(down_bias_grad).reshape(-1)]
    ).astype(BF16)
    if mp == 2:
        token_sums = (
            token_sums.astype(F32) + lax.ppermute(token_sums, "mp", swap).astype(F32)
        ).astype(BF16)
    else:
        token_sums = lax.psum(token_sums, "mp")
    unit_sums = jnp.concatenate(
        [jnp.stack(qv_bias_grad).reshape(-1), jnp.stack(up_bias_grad).reshape(-1)]
    ).astype(BF16)
    sums = gather_vector(jnp.concatenate([token_sums, unit_sums]))
    mod_size = mod_rows.size
    bias_size = token_sums.size + unit_sums.size - mod_size
    mod_all = sums[:, :mod_size].reshape(dp * seqs, 2, 6 * width)
    totals = jnp.sum(sums[:, mod_size : mod_size + bias_size].astype(F32), axis=0)

    def own(total, axis):
        part = total.shape[axis] // dp
        return lax.dynamic_slice_in_dim(total, my_dp * part, part, axis=axis)

    at = 2 * width
    proj_bias_out = own(totals[:at].reshape(2, width), 1)
    fc2_bias_out = own(totals[at : 2 * at].reshape(2, width), 1)
    at = 2 * at
    qv_size = 4 * qv_biases.shape[2]
    qv_bias_out = own(totals[at : at + qv_size].reshape(2, 2, -1), 2)
    fc1_bias_out = own(totals[at + qv_size :].reshape(2, -1), 1)
    ada_bias_out = own(jnp.sum(mod_all.astype(F32), axis=0), 1)
    ada_out = jnp.stack([dot(silu_mine, mod_all[:, s], TN) for s in range(2)])
    silu_grad = sum(dot(mod_all[:, s], ada_low[s], NT) for s in range(2))
    silu_grad = gather_small(silu_grad[None])
    silu_grad = lax.dynamic_slice_in_dim(silu_grad, my_dp * seqs, seqs, axis=1)
    silu_grad = jnp.moveaxis(silu_grad, 0, 1).reshape(seqs, -1)
    unused, pullback = jax.vjp(jax.nn.silu, condition.astype(F32))
    cond_out = pullback(silu_grad)[0]

    return (
        outputs[0],
        outputs[1],
        ada_out,
        ada_bias_out,
        qkv_out,
        qv_bias_out,
        proj_out,
        proj_bias_out,
        fc1_out,
        fc1_bias_out,
        fc2_out,
        fc2_bias_out,
        input_grads[0],
        input_grads[1],
        cond_out,
    )


def solution(mesh):
    tokens = P("dp", "mp", None)
    weights = (
        P(None, ("mp", "dp"), None),
        P(None, "dp"),
        P(None, None, "dp", "mp"),
        P(None, None, ("mp", "dp")),
        P(None, "mp", "dp"),
        P(None, "dp"),
        P(None, "dp", "mp"),
        P(None, ("mp", "dp")),
        P(None, "mp", "dp"),
        P(None, "dp"),
    )
    return jax.shard_map(
        functools.partial(body, mesh.shape["mp"], mesh.shape["dp"]),
        mesh=mesh,
        in_specs=(tokens, tokens, P("dp", "mp"), P("dp", None)) + weights + (tokens, tokens),
        out_specs=(tokens, tokens) + weights + (tokens, tokens, P("dp", "mp")),
        check_vma=False,
    )
```

time: 3730 us -> 980 us (0.26)
  waiting for transfers between devices: 1870 us -> 270 us
  local copies, waits for them, and re-layouts: 618 us -> 120 us
  blocking collectives: 393 us -> 0 us
  other arithmetic: 413 us -> 195 us
  matrix products: 368 us -> 217 us
  starting transfers between devices: 2.02 us -> 97.8 us
  Pallas kernels: 0 us -> 52 us
    reduce_scatter x29 -> x0, waiting for transfers between devices: 1310 us -> none  [the longest x1 270 us: body(): lax.psum_scatter(dense.astype(jnp.bfloat16), 'dp', scatter_dimension=1, t...]
    all_gather x5 -> x4, waiting for transfers between devices: 448 us -> 0.01 us  [the longest x1 0.01 us: body(): lax.all_gather(jnp.concatenate(attention_low, axis=1), 'dp', axis=2, tile...]
    all_gather x29 -> x0, blocking collectives: 393 us -> none  [the longest x1 65.7 us: body(): lax.all_gather(shards[5], 'dp', axis=1, tiled=True)]
    another operation x62 -> x19, local copies, waits for them, and re-layouts: 309 us -> 9.11 us  [the longest x3 3.5 us: body(): jnp.stack([ring.finish().reshape(seqs, -1) for ring in mod_rings], axis=1)]
    ppermute x0 -> x96, waiting for transfers between devices: none -> 270 us  [the longest x56 155 us: advance(): self.flying = [lax.ppermute(total.astype(self.kind), 'dp', self.hop)]]
    cond x150 -> x0, local copies, waits for them, and re-layouts: 231 us -> none  [the longest x8 223 us: when_live(): return lax.cond(live_flag, function, skipped, operands)]
    dot_general x76 -> x42, matrix products: 368 us -> 217 us  [dot(): lax.dot_general(left, right, (dims, ((), ())), preferred_element_type=F32)]
    convert_element_type x48 -> x62, other arithmetic: 197 us -> 77.6 us  [the longest x40 58.6 us: advance(): self.flying = [lax.ppermute(total.astype(self.kind), 'dp', self.hop)]]
  transfers between devices with their start and end apart: 41 -> 100, of which waited for: 20 -> 44; matrix products, arithmetic and copies ran while one was open for 27% -> 50% of each run, Pallas kernels for 0% -> 5%
where the time goes in v1:
time: 980 us; the launch traced here: 969 us
  waiting for transfers between devices  270 us (28%)
  matrix products  217 us (22%)
  other arithmetic  195 us (20%)
  local copies, waits for them, and re-layouts  120 us (12%)
  starting transfers between devices  97.8 us (10%)
  Pallas kernels  52 us (5%)
  between operations  17.4 us (2%)
    dot_general x42, matrix products, dot(): lax.dot_general(left, right, (dims, ((), ())), preferred_element_type=F32)  217 us
    ppermute x56, waiting for transfers between devices, advance(): self.flying = [lax.ppermute(total.astype(self.kind), 'dp', self.hop)]  155 us
    ppermute x56, starting transfers between devices, advance(): self.flying = [lax.ppermute(total.astype(self.kind), 'dp', self.hop)]  60.2 us
    convert_element_type x40, other arithmetic, advance(): self.flying = [lax.ppermute(total.astype(self.kind), 'dp', self.hop)]  58.6 us
    ppermute x8, waiting for transfers between devices, collect(): lax.ppermute(parts[1].astype(BF16), 'mp', swap).astype(F32)  48 us
    ppermute x8, waiting for transfers between devices, share(): return jnp.stack([rows, lax.ppermute(rows, 'mp', swap)])  38.5 us
    unnamed x450, local copies, waits for them, and re-layouts  37.8 us
    pallas_call x3, Pallas kernels, attention_backward(): pl.pallas_call(attention_back_kernel, grid=(1, width // lanes), in_specs=...  30.6 us
  transfers between devices with their start and end apart: 100, of which 44 were waited for; matrix products, arithmetic and copies ran while one was open for 50% of the time, Pallas kernels for 5%

profile of v1, /device:TPU:0, one launch (start us, length us, event | category | flops | bytes accessed | tf_op | source)
XLA Modules:
  0.0 969.4 jit_solution(14265396430951196489)
XLA Ops:
  53.4 5.8 collective-permute-done.13
  62.3 5.6 collective-permute-done.14
  71.1 5.3 collective-permute-done.15
  79.5 5.1 collective-permute-done.16
  87.8 5.0 collective-permute-done.17
  95.9 5.2 collective-permute-done.18
  105.0 4.2 collective-permute-done.19
  118.8 5.3 collective-permute-done.20
  130.6 11.7 %collective-permute-done.22 = bf16[3,64,1536]{2,1,0:T(8,128)(2,1)S(1)} collective-permute-done((bf16[3,64,1536]{2,1,0:T(8,128)(2,1)S(1)}, bf16[3,64,1536]{2,1,0:T(8,128)(2,1)S(1)}, u32[]{:S(2)}, u32[]{:S(2)}) %collective-permute-start.22) | collective-permute-done | bytes 589856 | tf_op jit(solution)/shard_map/ppermute | solution.py:271
  143.4 19.7 %collective-permute-done.21 = bf16[3,128,1536]{2,1,0:T(8,128)(2,1)S(1)} collective-permute-done((bf16[3,128,1536]{2,1,0:T(8,128)(2,1)S(1)}, bf16[3,128,1536]{2,1,0:T(8,128)(2,1)S(1)}, u32[]{:S(2)}, u32[]{:S(2)}) %collective-permute-start.21) | collective-permute-done | bytes 1179680 | tf_op jit(solution)/shard_map/ppermute | solution.py:271
  202.4 3.7 fusion.76
  206.1 3.7 add_convert_fusion.1
  210.4 3.9 add_convert_fusion.2
  216.7 21.4 %attention_forward.1 = (bf16[2,3,128,768]{3,2,1,0:T(8,128)(2,1)S(1)}, bf16[2,3,64,768]{3,2,1,0:T(8,128)(2,1)S(1)}) custom-call(bf16[3,2,3,128,768]{4,3,2,1,0:T(8,128)(2,1)} %pad_maximum_fusion.qi.ki.vi, bf16[3,2,3,128,768]{4,3,2,1,0:T(8,128)(2,1)} %pad_maximum_fusion.qi.ki.vi, bf16[3,2,3,128,768]{4,3,2,1,0:T(8,128)(2,1)} %pad_maximum_fusion.qi.ki.vi, ...), custom_call_target="tpu_custom_call" | custom-call | tf_op jit(solution)/shard_map/attention_forward/pallas_call | solution.py:116
  246.7 4.2 fusion.70
  251.4 6.6 collective-permute-done.25
  261.9 21.4 %collective-permute-done.23 = bf16[3,128,1536]{2,1,0:T(8,128)(2,1)S(1)} collective-permute-done((bf16[3,128,1536]{2,1,0:T(8,128)(2,1)S(1)}, bf16[3,128,1536]{2,1,0:T(8,128)(2,1)S(1)}, u32[]{:S(2)}, u32[]{:S(2)}) %collective-permute-start.23) | collective-permute-done | bytes 1179680 | tf_op jit(solution)/shard_map/ppermute | solution.py:276
  288.7 7.2 collective-permute-done.26
  297.0 11.2 %multiply_convert_fusion.1 = (bf16[384,3072]{1,0:T(8,128)(2,1)S(1)}, f32[384,3072]{1,0:T(8,128)}) fusion(f32[3072]{0:T(1024)} %add.1926, bf16[384,1536]{1,0:T(8,128)(2,1)} %bitcast.1197, bf16[2,1536,3072]{2,1,0:T(8,128)(2,1)} %all-gather.7.cloned.1.call-done), kind=kOutput, calls=%fused_computation.56 | convolution fusion | flops 3635675136 | bytes 17707008 | tf_op jit(solution)/shard_map/dot_general | solution.py:33
  308.2 5.5 convolution_convert_fusion.3
  321.0 14.7 %multiply_convert_fusion = (bf16[768,3072]{1,0:T(8,128)(2,1)S(1)}, f32[768,3072]{1,0:T(8,128)}) fusion(f32[3072]{0:T(1024)S(1)} %copy-done.187, bf16[768,1536]{1,0:T(8,128)(2,1)S(1)} %bitcast.1174, bf16[2,1536,3072]{2,1,0:T(8,128)(2,1)} %all-gather.7.cloned.1.call-done), kind=kOutput, calls=%fused_computation.31 | convolution fusion | flops 7271350272 | bytes 25964544 | tf_op jit(solution)/shard_map/dot_general | solution.py:33
  335.7 8.1 convolution_convert_fusion.2
  354.4 17.4 %fusion.6 = bf16[768,3072]{1,0:T(8,128)(2,1)S(1)} fusion(f32[768,3072]{1,0:T(8,128)} %get-tuple-element.466, bf16[768,1536]{1,0:T(8,128)(2,1)} %bitcast.1176, bf16[2,1536,3072]{2,1,0:T(8,128)(2,1)} %all-gather.9.cloned.1.call-done, f32[3072]{0:T(1024)} %add.957), kind=kOutput, calls=%fused_computation.14 | convolution fusion | flops 7297302528 | bytes 25964544 | tf_op jit(solution)/shard_map/dot_general | solution.py:33
  378.5 10.1 %fusion.13 = f32[2,3,128,1536]{3,2,1,0:T(8,128)S(1)} fusion(bf16[2,3,128,3072]{3,2,1,0:T(8,128)(2,1)S(1)} %bitcast.1143, bf16[2,1536,3072]{2,1,0:T(8,128)(2,1)} %all-gather.7.cloned.1.call-done), kind=kOutput, calls=%fused_computation.21 | convolution fusion | flops 7247757312 | bytes 18874368 | tf_op jit(solution)/shard_map/dot_general | solution.py:33
  401.5 8.3 fusion.39
  416.8 7.8 fusion.11
  441.3 12.2 %convolution_convert_fusion.1 = bf16[1536,3072]{1,0:T(8,128)(2,1)} fusion(bf16[768,1536]{1,0:T(8,128)(2,1)S(1)} %bitcast.1175, bf16[768,3072]{1,0:T(8,128)(2,1)} %copy-done.39), kind=kOutput, calls=%fused_computation.3 | convolution fusion | flops 7252475904 | bytes 16515072 | tf_op jit(solution)/shard_map/dot_general | solution.py:33
  459.6 7.1 convolution_convert_fusion
  478.2 6.0 collective-permute-done.42
  509.7 12.9 %fusion.9 = f32[2,3,128,1536]{3,2,1,0:T(8,128)} fusion(bf16[2,3,128,3072]{3,2,1,0:T(8,128)(2,1)} %bitcast.1257, bf16[2,1536,3072]{2,1,0:T(8,128)(2,1)} %all-gather.9.cloned.1.call-done), kind=kOutput, calls=%fused_computation.17 | convolution fusion | flops 7247757312 | bytes 18874368 | tf_op jit(solution)/shard_map/dot_general | solution.py:33
  524.4 3.9 fusion.112
  533.4 7.2 fusion.7
  553.7 4.9 collective-permute-done.54
  570.6 3.6 fusion.85
  574.2 3.7 fusion.75
  589.1 10.2 %attention_backward.3 = (bf16[3,2,1,128,768]{4,3,2,1,0:T(8,128)(2,1)S(1)}, bf16[3,2,1,64,768]{4,3,2,1,0:T(8,128)(2,1)S(1)}) custom-call(bf16[3,2,3,128,768]{4,3,2,1,0:T(8,128)(2,1)} %pad_maximum_fusion.qi.ki.vi, bf16[3,2,3,128,768]{4,3,2,1,0:T(8,128)(2,1)} %pad_maximum_fusion.qi.ki.vi, bf16[3,2,3,128,768]{4,3,2,1,0:T(8,128)(2,1)} %pad_maximum_fusion.qi.ki.vi, ...), custom_call_target="tpu_custom_call" | custom-call | tf_op jit(solution)/shard_map/attention_backward/pallas_call | solution.py:143
  611.3 10.2 %attention_backward.4 = (bf16[3,2,1,128,768]{4,3,2,1,0:T(8,128)(2,1)S(1)}, bf16[3,2,1,64,768]{4,3,2,1,0:T(8,128)(2,1)S(1)}) custom-call(bf16[3,2,3,128,768]{4,3,2,1,0:T(8,128)(2,1)} %pad_maximum_fusion.qi.ki.vi, bf16[3,2,3,128,768]{4,3,2,1,0:T(8,128)(2,1)} %pad_maximum_fusion.qi.ki.vi, bf16[3,2,3,128,768]{4,3,2,1,0:T(8,128)(2,1)} %pad_maximum_fusion.qi.ki.vi, ...), custom_call_target="tpu_custom_call" | custom-call | tf_op jit(solution)/shard_map/attention_backward/pallas_call | solution.py:143
  628.3 3.8 bitcast_add_fusion
  632.1 10.2 %attention_backward.5 = (bf16[3,2,1,128,768]{4,3,2,1,0:T(8,128)(2,1)S(1)}, bf16[3,2,1,64,768]{4,3,2,1,0:T(8,128)(2,1)S(1)}) custom-call(bf16[3,2,3,128,768]{4,3,2,1,0:T(8,128)(2,1)} %pad_maximum_fusion.qi.ki.vi, bf16[3,2,3,128,768]{4,3,2,1,0:T(8,128)(2,1)} %pad_maximum_fusion.qi.ki.vi, bf16[3,2,3,128,768]{4,3,2,1,0:T(8,128)(2,1)} %pad_maximum_fusion.qi.ki.vi, ...), custom_call_target="tpu_custom_call" | custom-call | tf_op jit(solution)/shard_map/attention_backward/pallas_call | solution.py:143
  657.1 4.3 convolution_convert_fusion.7
  663.2 4.4 convolution_convert_fusion.9
  667.9 4.9 fusion.62
  672.8 3.7 fusion.60
  676.5 5.9 add_add_fusion
  683.9 5.4 convolution_convert_fusion.4
  691.6 5.4 convolution_convert_fusion.6
  737.5 20.0 %collective-permute-done.65 = bf16[3,128,1536]{2,1,0:T(8,128)(2,1)S(1)} collective-permute-done((bf16[3,128,1536]{2,1,0:T(8,128)(2,1)S(1)}, bf16[3,128,1536]{2,1,0:T(8,128)(2,1)S(1)}, u32[]{:S(2)}, u32[]{:S(2)}) %collective-permute-start.65) | collective-permute-done | bytes 1179680 | tf_op jit(solution)/shard_map/ppermute | solution.py:276
  761.0 3.9 multiply_reduce_fusion
  785.7 4.3 convert_add_fusion.88
  790.1 3.7 convert_add_fusion.90
  795.7 3.7 fusion.188
  799.5 3.8 fusion.190
  805.9 4.1 collective-permute-done.76
  810.0 11.0 %collective-permute-done.77 = bf16[96,3072]{1,0:T(8,128)(2,1)} collective-permute-done((bf16[96,3072]{1,0:T(8,128)(2,1)}, bf16[96,3072]{1,0:T(8,128)(2,1)}, u32[]{:S(2)}, u32[]{:S(2)}) %collective-permute-start.77) | collective-permute-done | bytes 589856 | tf_op jit(solution)/shard_map/ppermute | solution.py:217
  825.6 16.1 %collective-permute-done.78 = bf16[96,3072]{1,0:T(8,128)(2,1)S(1)} collective-permute-done((bf16[96,3072]{1,0:T(8,128)(2,1)S(1)}, bf16[96,3072]{1,0:T(8,128)(2,1)S(1)}, u32[]{:S(2)}, u32[]{:S(2)}) %collective-permute-start.78) | collective-permute-done | bytes 589856 | tf_op jit(solution)/shard_map/ppermute | solution.py:217
  844.4 4.1 collective-permute-done.84
  848.7 8.7 collective-permute-done.79
  860.7 12.1 %collective-permute-done.80 = bf16[96,3072]{1,0:T(8,128)(2,1)S(1)} collective-permute-done((bf16[96,3072]{1,0:T(8,128)(2,1)S(1)}, bf16[96,3072]{1,0:T(8,128)(2,1)S(1)}, u32[]{:S(2)}, u32[]{:S(2)}) %collective-permute-start.80) | collective-permute-done | bytes 589856 | tf_op jit(solution)/shard_map/ppermute | solution.py:217
  875.2 11.2 %collective-permute-done.81 = bf16[96,3072]{1,0:T(8,128)(2,1)S(1)} collective-permute-done((bf16[96,3072]{1,0:T(8,128)(2,1)S(1)}, bf16[96,3072]{1,0:T(8,128)(2,1)S(1)}, u32[]{:S(2)}, u32[]{:S(2)}) %collective-permute-start.81) | collective-permute-done | bytes 589856 | tf_op jit(solution)/shard_map/ppermute | solution.py:217
  888.9 11.0 %collective-permute-done.82 = bf16[96,3072]{1,0:T(8,128)(2,1)S(1)} collective-permute-done((bf16[96,3072]{1,0:T(8,128)(2,1)S(1)}, bf16[96,3072]{1,0:T(8,128)(2,1)S(1)}, u32[]{:S(2)}, u32[]{:S(2)}) %collective-permute-start.82) | collective-permute-done | bytes 589856 | tf_op jit(solution)/shard_map/ppermute | solution.py:217
  903.3 8.6 collective-permute-done.83
  925.6 3.7 fusion.226
  947.8 3.6 collective-permute-done.94
  952.3 9.6 collective-permute-done.95
  (924 shorter events, 451.0 us)
Async XLA Ops:
  7.2 186.3 %all-gather.5.cloned.1.call-start = ((), (), s32[]{:S(2)}) async-start(), calls=%async_computation | async-start | bytes 20054016 | tf_op jit(solution)/shard_map/all_gather | solution.py:319
  11.1 285.9 %all-gather.7.cloned.1.call-start = ((), (), s32[]{:S(2)}) async-start(), calls=%async_computation.1 | async-start | bytes 20054016 | tf_op jit(solution)/shard_map/all_gather | solution.py:322
  13.2 341.2 %all-gather.9.cloned.1.call-start = ((), (), s32[]{:S(2)}) async-start(), calls=%async_computation.2 | async-start | bytes 20054016 | tf_op jit(solution)/shard_map/all_gather | solution.py:323
  17.2 901.7 %all-gather.11.cloned.1.call-start = ((), (), s32[]{:S(2)}) async-start(), calls=%async_computation.3 | async-start | bytes 2437120 | tf_op jit(solution)/shard_map/all_gather | solution.py:301
  126.0 16.3 %collective-permute-start.22 = (bf16[3,64,1536]{2,1,0:T(8,128)(2,1)S(1)}, bf16[3,64,1536]{2,1,0:T(8,128)(2,1)S(1)}, u32[]{:S(2)}, u32[]{:S(2)}) collective-permute-start(bf16[3,64,1536]{2,1,0:T(8,128)(2,1)S(1)} %fusion.90), channel_id=1, source_target_pairs={{0,1},{1,0},{2,3},{3,2},{4,5},{5,4},{6,7},{7,6},{8,9},{9,8},{10,11... | collective-permute-start | bytes 1769480 | tf_op jit(solution)/shard_map/ppermute | solution.py:271
  128.4 34.7 %collective-permute-start.21 = (bf16[3,128,1536]{2,1,0:T(8,128)(2,1)S(1)}, bf16[3,128,1536]{2,1,0:T(8,128)(2,1)S(1)}, u32[]{:S(2)}, u32[]{:S(2)}) collective-permute-start(bf16[3,128,1536]{2,1,0:T(8,128)(2,1)S(1)} %fusion.50), channel_id=1, source_target_pairs={{0,1},{1,0},{2,3},{3,2},{4,5},{5,4},{6,7},{7,6},{8,9},{9,8},{10,11... | collective-permute-start | bytes 3538952 | tf_op jit(solution)/shard_map/ppermute | solution.py:271
  164.7 26.5 %collective-permute-start.27 = (bf16[3,64,1536]{2,1,0:T(8,128)(2,1)S(1)}, bf16[3,64,1536]{2,1,0:T(8,128)(2,1)}, u32[]{:S(2)}, u32[]{:S(2)}) collective-permute-start(bf16[3,64,1536]{2,1,0:T(8,128)(2,1)S(1)} %fusion.173), channel_id=1, source_target_pairs={{0,1},{1,0},{2,3},{3,2},{4,5},{5,4},{6,7},{7,6},{8,9},{9,8},{10,11... | collective-permute-start | bytes 1769480 | tf_op jit(solution)/shard_map/ppermute | solution.py:271
  190.8 52.8 %collective-permute-start.28 = (bf16[3,128,1536]{2,1,0:T(8,128)(2,1)S(1)}, bf16[3,128,1536]{2,1,0:T(8,128)(2,1)}, u32[]{:S(2)}, u32[]{:S(2)}) collective-permute-start(bf16[3,128,1536]{2,1,0:T(8,128)(2,1)S(1)} %fusion.59), channel_id=1, source_target_pairs={{0,1},{1,0},{2,3},{3,2},{4,5},{5,4},{6,7},{7,6},{8,9},{9,8},{10,11... | collective-permute-start | bytes 3538952 | tf_op jit(solution)/shard_map/ppermute | solution.py:271
  241.7 16.3 %collective-permute-start.25 = (bf16[3,64,1536]{2,1,0:T(8,128)(2,1)S(1)}, bf16[3,64,1536]{2,1,0:T(8,128)(2,1)S(1)}, u32[]{:S(2)}, u32[]{:S(2)}) collective-permute-start(bf16[3,64,1536]{2,1,0:T(8,128)(2,1)S(1)} %bitcast.1228), channel_id=1, source_target_pairs={{0,1},{1,0},{2,3},{3,2},{4,5},{5,4},{6,7},{7,6},{8,9},{9,8},{10,11... | collective-permute-start | bytes 1769480 | tf_op jit(solution)/shard_map/ppermute | solution.py:276
  251.1 32.1 %collective-permute-start.23 = (bf16[3,128,1536]{2,1,0:T(8,128)(2,1)S(1)}, bf16[3,128,1536]{2,1,0:T(8,128)(2,1)S(1)}, u32[]{:S(2)}, u32[]{:S(2)}) collective-permute-start(bf16[3,128,1536]{2,1,0:T(8,128)(2,1)S(1)} %bitcast.1201), channel_id=1, source_target_pairs={{0,1},{1,0},{2,3},{3,2},{4,5},{5,4},{6,7},{7,6},{8,9},{9,8},{10,11... | collective-permute-start | bytes 3538952 | tf_op jit(solution)/shard_map/ppermute | solution.py:276
  259.5 36.4 %collective-permute-start.26 = (bf16[3,64,1536]{2,1,0:T(8,128)(2,1)S(1)}, bf16[3,64,1536]{2,1,0:T(8,128)(2,1)S(1)}, u32[]{:S(2)}, u32[]{:S(2)}) collective-permute-start(bf16[3,64,1536]{2,1,0:T(8,128)(2,1)S(1)} %add_convert_fusion.3), channel_id=1, source_target_pairs={{0,1},{1,0},{2,3},{3,2},{4,5},{5,4},{6,7},{7,6},{8,9},{9,8},{10,11... | collective-permute-start | bytes 1769480 | tf_op jit(solution)/shard_map/ppermute | solution.py:271
  286.7 32.8 %collective-permute-start.24 = (bf16[3,128,1536]{2,1,0:T(8,128)(2,1)}, bf16[3,128,1536]{2,1,0:T(8,128)(2,1)}, u32[]{:S(2)}, u32[]{:S(2)}) collective-permute-start(bf16[3,128,1536]{2,1,0:T(8,128)(2,1)} %add_convert_fusion), channel_id=1, source_target_pairs={{0,1},{1,0},{2,3},{3,2},{4,5},{5,4},{6,7},{7,6},{8,9},{9,8},{10,11... | collective-permute-start | bytes 3538952 | tf_op jit(solution)/shard_map/ppermute | solution.py:271
  318.8 53.0 %collective-permute-start.30 = (bf16[8,96,3072]{2,1,0:T(8,128)(2,1)}, bf16[8,96,3072]{2,1,0:T(8,128)(2,1)}, u32[]{:S(2)}, u32[]{:S(2)}) collective-permute-start(bf16[8,96,3072]{2,1,0:T(8,128)(2,1)} %dynamic-slice_bitcast_fusion.2), channel_id=1, source_target_pairs={{0,2},{2,0},{4,6},{6,4},{8,10},{10,8},{12,14},{14,12},{16,18},{18,... | collective-permute-start | bytes 14155784 | tf_op jit(solution)/shard_map/ppermute | solution.py:195
  348.8 23.0 %collective-permute-start.29 = (bf16[8,96,3072]{2,1,0:T(8,128)(2,1)}, bf16[8,96,3072]{2,1,0:T(8,128)(2,1)}, u32[]{:S(2)}, u32[]{:S(2)}) collective-permute-start(bf16[8,96,3072]{2,1,0:T(8,128)(2,1)} %dynamic-slice_bitcast_fusion.3), channel_id=1, source_target_pairs={{0,2},{2,0},{4,6},{6,4},{8,10},{10,8},{12,14},{14,12},{16,18},{18,... | collective-permute-start | bytes 14155784 | tf_op jit(solution)/shard_map/ppermute | solution.py:195
  376.5 15.3 %collective-permute-start.32 = (bf16[96,3072]{1,0:T(8,128)(2,1)S(1)}, bf16[96,3072]{1,0:T(8,128)(2,1)S(1)}, u32[]{:S(2)}, u32[]{:S(2)}) collective-permute-start(bf16[96,3072]{1,0:T(8,128)(2,1)S(1)} %fusion.169), channel_id=1, source_target_pairs={{0,4},{2,6},{8,0},{10,2},{16,8},{18,10},{24,16},{26,18},{28,24},{3... | collective-permute-start | bytes 1769480 | tf_op jit(solution)/shard_map/ppermute | solution.py:217
  378.4 15.0 %collective-permute-start.31 = (bf16[96,3072]{1,0:T(8,128)(2,1)S(1)}, bf16[96,3072]{1,0:T(8,128)(2,1)S(1)}, u32[]{:S(2)}, u32[]{:S(2)}) collective-permute-start(bf16[96,3072]{1,0:T(8,128)(2,1)S(1)} %fusion.170), channel_id=1, source_target_pairs={{0,8},{2,10},{8,16},{10,18},{16,24},{18,26},{24,28},{26,30},{28,20... | collective-permute-start | bytes 1769480 | tf_op jit(solution)/shard_map/ppermute | solution.py:217
  396.3 14.2 %collective-permute-start.35 = (bf16[96,3072]{1,0:T(8,128)(2,1)S(1)}, bf16[96,3072]{1,0:T(8,128)(2,1)S(1)}, u32[]{:S(2)}, u32[]{:S(2)}) collective-permute-start(bf16[96,3072]{1,0:T(8,128)(2,1)S(1)} %fusion.166), channel_id=1, source_target_pairs={{0,4},{2,6},{8,0},{10,2},{16,8},{18,10},{24,16},{26,18},{28,24},{3... | collective-permute-start | bytes 1769480 | tf_op jit(solution)/shard_map/ppermute | solution.py:217
  397.6 14.1 %collective-permute-start.34 = (bf16[96,3072]{1,0:T(8,128)(2,1)S(1)}, bf16[96,3072]{1,0:T(8,128)(2,1)S(1)}, u32[]{:S(2)}, u32[]{:S(2)}) collective-permute-start(bf16[96,3072]{1,0:T(8,128)(2,1)S(1)} %fusion.168), channel_id=1, source_target_pairs={{0,8},{2,10},{8,16},{10,18},{16,24},{18,26},{24,28},{26,30},{28,20... | collective-permute-start | bytes 1769480 | tf_op jit(solution)/shard_map/ppermute | solution.py:217
  399.6 54.0 %collective-permute-start.33 = (bf16[3,128,1536]{2,1,0:T(8,128)(2,1)}, bf16[3,128,1536]{2,1,0:T(8,128)(2,1)}, u32[]{:S(2)}, u32[]{:S(2)}) collective-permute-start(bf16[3,128,1536]{2,1,0:T(8,128)(2,1)} %fusion.97), channel_id=1, source_target_pairs={{0,1},{1,0},{2,3},{3,2},{4,5},{5,4},{6,7},{7,6},{8,9},{9,8},{10,11... | collective-permute-start | bytes 3538952 | tf_op jit(solution)/shard_map/ppermute | solution.py:276
  414.7 13.4 %collective-permute-start.37 = (bf16[96,3072]{1,0:T(8,128)(2,1)S(1)}, bf16[96,3072]{1,0:T(8,128)(2,1)S(1)}, u32[]{:S(2)}, u32[]{:S(2)}) collective-permute-start(bf16[96,3072]{1,0:T(8,128)(2,1)S(1)} %fusion.162), channel_id=1, source_target_pairs={{0,4},{2,6},{8,0},{10,2},{16,8},{18,10},{24,16},{26,18},{28,24},{3... | collective-permute-start | bytes 1769480 | tf_op jit(solution)/shard_map/ppermute | solution.py:217
  416.2 12.8 %collective-permute-start.36 = (bf16[96,3072]{1,0:T(8,128)(2,1)S(1)}, bf16[96,3072]{1,0:T(8,128)(2,1)}, u32[]{:S(2)}, u32[]{:S(2)}) collective-permute-start(bf16[96,3072]{1,0:T(8,128)(2,1)S(1)} %fusion.164), channel_id=1, source_target_pairs={{0,8},{2,10},{8,16},{10,18},{16,24},{18,26},{24,28},{26,30},{28,20... | collective-permute-start | bytes 1769480 | tf_op jit(solution)/shard_map/ppermute | solution.py:217
  437.8 38.8 %collective-permute-start.38 = (bf16[3,64,1536]{2,1,0:T(8,128)(2,1)}, bf16[3,64,1536]{2,1,0:T(8,128)(2,1)}, u32[]{:S(2)}, u32[]{:S(2)}) collective-permute-start(bf16[3,64,1536]{2,1,0:T(8,128)(2,1)} %fusion.182), channel_id=1, source_target_pairs={{0,1},{1,0},{2,3},{3,2},{4,5},{5,4},{6,7},{7,6},{8,9},{9,8},{10,11... | collective-permute-start | bytes 1769480 | tf_op jit(solution)/shard_map/ppermute | solution.py:276
  439.3 17.3 %collective-permute-start.40 = (bf16[96,3072]{1,0:T(8,128)(2,1)S(1)}, bf16[96,3072]{1,0:T(8,128)(2,1)S(1)}, u32[]{:S(2)}, u32[]{:S(2)}) collective-permute-start(bf16[96,3072]{1,0:T(8,128)(2,1)S(1)} %fusion.158), channel_id=1, source_target_pairs={{0,4},{2,6},{8,0},{10,2},{16,8},{18,10},{24,16},{26,18},{28,24},{3... | collective-permute-start | bytes 1769480 | tf_op jit(solution)/shard_map/ppermute | solution.py:217
  440.8 16.6 %collective-permute-start.39 = (bf16[96,3072]{1,0:T(8,128)(2,1)S(1)}, bf16[96,3072]{1,0:T(8,128)(2,1)}, u32[]{:S(2)}, u32[]{:S(2)}) collective-permute-start(bf16[96,3072]{1,0:T(8,128)(2,1)S(1)} %fusion.160), channel_id=1, source_target_pairs={{0,8},{2,10},{8,16},{10,18},{16,24},{18,26},{24,28},{26,30},{28,20... | collective-permute-start | bytes 1769480 | tf_op jit(solution)/shard_map/ppermute | solution.py:217
  475.6 52.7 %collective-permute-start.49 = (bf16[8,96,3072]{2,1,0:T(8,128)(2,1)S(1)}, bf16[8,96,3072]{2,1,0:T(8,128)(2,1)S(1)}, u32[]{:S(2)}, u32[]{:S(2)}) collective-permute-start(bf16[8,96,3072]{2,1,0:T(8,128)(2,1)S(1)} %dynamic-slice_bitcast_fusion.1), channel_id=1, source_target_pairs={{0,2},{2,0},{4,6},{6,4},{8,10},{10,8},{12,14},{14,12},{16,18},{18,... | collective-permute-start | bytes 14155784 | tf_op jit(solution)/shard_map/ppermute | solution.py:195
  476.0 52.3 %collective-permute-start.50 = (bf16[8,96,3072]{2,1,0:T(8,128)(2,1)S(1)}, bf16[8,96,3072]{2,1,0:T(8,128)(2,1)}, u32[]{:S(2)}, u32[]{:S(2)}) collective-permute-start(bf16[8,96,3072]{2,1,0:T(8,128)(2,1)S(1)} %dynamic-slice_bitcast_fusion), channel_id=1, source_target_pairs={{0,2},{2,0},{4,6},{6,4},{8,10},{10,8},{12,14},{14,12},{16,18},{18,... | collective-permute-start | bytes 14155784 | tf_op jit(solution)/shard_map/ppermute | solution.py:195
  504.9 17.8 %collective-permute-start.48 = (bf16[96,3072]{1,0:T(8,128)(2,1)}, bf16[96,3072]{1,0:T(8,128)(2,1)}, u32[]{:S(2)}, u32[]{:S(2)}) collective-permute-start(bf16[96,3072]{1,0:T(8,128)(2,1)} %fusion.146), channel_id=1, source_target_pairs={{0,4},{2,6},{8,0},{10,2},{16,8},{18,10},{24,16},{26,18},{28,24},{3... | collective-permute-start | bytes 1769480 | tf_op jit(solution)/shard_map/ppermute | solution.py:217
  508.7 15.6 %collective-permute-start.47 = (bf16[96,3072]{1,0:T(8,128)(2,1)}, bf16[96,3072]{1,0:T(8,128)(2,1)}, u32[]{:S(2)}, u32[]{:S(2)}) collective-permute-start(bf16[96,3072]{1,0:T(8,128)(2,1)} %fusion.148), channel_id=1, source_target_pairs={{0,8},{2,10},{8,16},{10,18},{16,24},{18,26},{24,28},{26,30},{28,20... | collective-permute-start | bytes 1769480 | tf_op jit(solution)/shard_map/ppermute | solution.py:217
  509.4 41.2 %collective-permute-start.46 = (bf16[3,64,1536]{2,1,0:T(8,128)(2,1)}, bf16[3,64,1536]{2,1,0:T(8,128)(2,1)}, u32[]{:S(2)}, u32[]{:S(2)}) collective-permute-start(bf16[3,64,1536]{2,1,0:T(8,128)(2,1)} %get-tuple-element.170), channel_id=1, source_target_pairs={{0,1},{1,0},{2,3},{3,2},{4,5},{5,4},{6,7},{7,6},{8,9},{9,8},{10,11... | collective-permute-start | bytes 1769480 | tf_op jit(solution)/shard_map/ppermute | solution.py:271
  522.6 29.4 %collective-permute-start.45 = (bf16[3,128,1536]{2,1,0:T(8,128)(2,1)}, bf16[3,128,1536]{2,1,0:T(8,128)(2,1)}, u32[]{:S(2)}, u32[]{:S(2)}) collective-permute-start(bf16[3,128,1536]{2,1,0:T(8,128)(2,1)} %get-tuple-element.169), channel_id=1, source_target_pairs={{0,1},{1,0},{2,3},{3,2},{4,5},{5,4},{6,7},{7,6},{8,9},{9,8},{10,11... | collective-permute-start | bytes 3538952 | tf_op jit(solution)/shard_map/ppermute | solution.py:271
  546.9 11.6 %collective-permute-start.54 = (bf16[96,3072]{1,0:T(8,128)(2,1)S(1)}, bf16[96,3072]{1,0:T(8,128)(2,1)S(1)}, u32[]{:S(2)}, u32[]{:S(2)}) collective-permute-start(bf16[96,3072]{1,0:T(8,128)(2,1)S(1)} %fusion.140), channel_id=1, source_target_pairs={{0,4},{2,6},{8,0},{10,2},{16,8},{18,10},{24,16},{26,18},{28,24},{3... | collective-permute-start | bytes 1769480 | tf_op jit(solution)/shard_map/ppermute | solution.py:217
  563.2 46.4 %collective-permute-start.64 = (bf16[3,64,1536]{2,1,0:T(8,128)(2,1)}, bf16[3,64,1536]{2,1,0:T(8,128)(2,1)S(1)}, u32[]{:S(2)}, u32[]{:S(2)}) collective-permute-start(bf16[3,64,1536]{2,1,0:T(8,128)(2,1)} %fusion.183), channel_id=1, source_target_pairs={{0,1},{1,0},{2,3},{3,2},{4,5},{5,4},{6,7},{7,6},{8,9},{9,8},{10,11... | collective-permute-start | bytes 1769480 | tf_op jit(solution)/shard_map/ppermute | solution.py:276
  563.2 14.6 %collective-permute-start.56 = (bf16[96,3072]{1,0:T(8,128)(2,1)S(1)}, bf16[96,3072]{1,0:T(8,128)(2,1)S(1)}, u32[]{:S(2)}, u32[]{:S(2)}) collective-permute-start(bf16[96,3072]{1,0:T(8,128)(2,1)S(1)} %fusion.136), channel_id=1, source_target_pairs={{0,4},{2,6},{8,0},{10,2},{16,8},{18,10},{24,16},{26,18},{28,24},{3... | collective-permute-start | bytes 1769480 | tf_op jit(solution)/shard_map/ppermute | solution.py:217
  563.6 14.3 %collective-permute-start.55 = (bf16[96,3072]{1,0:T(8,128)(2,1)S(1)}, bf16[96,3072]{1,0:T(8,128)(2,1)S(1)}, u32[]{:S(2)}, u32[]{:S(2)}) collective-permute-start(bf16[96,3072]{1,0:T(8,128)(2,1)S(1)} %fusion.138), channel_id=1, source_target_pairs={{0,8},{2,10},{8,16},{10,18},{16,24},{18,26},{24,28},{26,30},{28,20... | collective-permute-start | bytes 1769480 | tf_op jit(solution)/shard_map/ppermute | solution.py:217
  582.2 19.5 %collective-permute-start.58 = (bf16[96,3072]{1,0:T(8,128)(2,1)}, bf16[96,3072]{1,0:T(8,128)(2,1)}, u32[]{:S(2)}, u32[]{:S(2)}) collective-permute-start(bf16[96,3072]{1,0:T(8,128)(2,1)} %fusion.132), channel_id=1, source_target_pairs={{0,4},{2,6},{8,0},{10,2},{16,8},{18,10},{24,16},{26,18},{28,24},{3... | collective-permute-start | bytes 1769480 | tf_op jit(solution)/shard_map/ppermute | solution.py:217
  582.6 19.1 %collective-permute-start.57 = (bf16[96,3072]{1,0:T(8,128)(2,1)}, bf16[96,3072]{1,0:T(8,128)(2,1)}, u32[]{:S(2)}, u32[]{:S(2)}) collective-permute-start(bf16[96,3072]{1,0:T(8,128)(2,1)} %fusion.134), channel_id=1, source_target_pairs={{0,8},{2,10},{8,16},{10,18},{16,24},{18,26},{24,28},{26,30},{28,20... | collective-permute-start | bytes 1769480 | tf_op jit(solution)/shard_map/ppermute | solution.py:217
  587.1 41.2 %collective-permute-start.63 = (bf16[3,128,1536]{2,1,0:T(8,128)(2,1)}, bf16[3,128,1536]{2,1,0:T(8,128)(2,1)}, u32[]{:S(2)}, u32[]{:S(2)}) collective-permute-start(bf16[3,128,1536]{2,1,0:T(8,128)(2,1)} %fusion.98), channel_id=1, source_target_pairs={{0,1},{1,0},{2,3},{3,2},{4,5},{5,4},{6,7},{7,6},{8,9},{9,8},{10,11... | collective-permute-start | bytes 3538952 | tf_op jit(solution)/shard_map/ppermute | solution.py:276
  604.2 17.3 %collective-permute-start.60 = (bf16[96,3072]{1,0:T(8,128)(2,1)}, bf16[96,3072]{1,0:T(8,128)(2,1)}, u32[]{:S(2)}, u32[]{:S(2)}) collective-permute-start(bf16[96,3072]{1,0:T(8,128)(2,1)} %fusion.128), channel_id=1, source_target_pairs={{0,4},{2,6},{8,0},{10,2},{16,8},{18,10},{24,16},{26,18},{28,24},{3... | collective-permute-start | bytes 1769480 | tf_op jit(solution)/shard_map/ppermute | solution.py:217
  606.8 14.7 %collective-permute-start.59 = (bf16[96,3072]{1,0:T(8,128)(2,1)}, bf16[96,3072]{1,0:T(8,128)(2,1)}, u32[]{:S(2)}, u32[]{:S(2)}) collective-permute-start(bf16[96,3072]{1,0:T(8,128)(2,1)} %fusion.130), channel_id=1, source_target_pairs={{0,8},{2,10},{8,16},{10,18},{16,24},{18,26},{24,28},{26,30},{28,20... | collective-permute-start | bytes 1769480 | tf_op jit(solution)/shard_map/ppermute | solution.py:217
  609.6 168.3 %collective-permute-start.72 = (bf16[8,96,768]{2,1,0:T(8,128)(2,1)}, bf16[8,96,768]{2,1,0:T(8,128)(2,1)}, u32[]{:S(2)}, u32[]{:S(2)}) collective-permute-start(bf16[8,96,768]{2,1,0:T(8,128)(2,1)} %dynamic-slice_bitcast_fusion.7), channel_id=1, source_target_pairs={{0,2},{2,0},{4,6},{6,4},{8,10},{10,8},{12,14},{14,12},{16,18},{18,... | collective-permute-start | bytes 3538952 | tf_op jit(solution)/shard_map/ppermute | solution.py:195
  609.6 168.9 %collective-permute-start.68 = (bf16[8,96,768]{2,1,0:T(8,128)(2,1)}, bf16[8,96,768]{2,1,0:T(8,128)(2,1)}, u32[]{:S(2)}, u32[]{:S(2)}) collective-permute-start(bf16[8,96,768]{2,1,0:T(8,128)(2,1)} %dynamic-slice_bitcast_fusion.11), channel_id=1, source_target_pairs={{0,2},{2,0},{4,6},{6,4},{8,10},{10,8},{12,14},{14,12},{16,18},{18,... | collective-permute-start | bytes 3538952 | tf_op jit(solution)/shard_map/ppermute | solution.py:195
  624.0 18.3 %collective-permute-start.62 = (bf16[96,3072]{1,0:T(8,128)(2,1)}, bf16[96,3072]{1,0:T(8,128)(2,1)}, u32[]{:S(2)}, u32[]{:S(2)}) collective-permute-start(bf16[96,3072]{1,0:T(8,128)(2,1)} %fusion.124), channel_id=1, source_target_pairs={{0,4},{2,6},{8,0},{10,2},{16,8},{18,10},{24,16},{26,18},{28,24},{3... | collective-permute-start | bytes 1769480 | tf_op jit(solution)/shard_map/ppermute | solution.py:217
  626.6 15.7 %collective-permute-start.61 = (bf16[96,3072]{1,0:T(8,128)(2,1)}, bf16[96,3072]{1,0:T(8,128)(2,1)S(1)}, u32[]{:S(2)}, u32[]{:S(2)}) collective-permute-start(bf16[96,3072]{1,0:T(8,128)(2,1)} %fusion.126), channel_id=1, source_target_pairs={{0,8},{2,10},{8,16},{10,18},{16,24},{18,26},{24,28},{26,30},{28,20... | collective-permute-start | bytes 1769480 | tf_op jit(solution)/shard_map/ppermute | solution.py:217
  711.7 17.2 %collective-permute-start.91 = (bf16[96,3072]{1,0:T(8,128)(2,1)}, bf16[96,3072]{1,0:T(8,128)(2,1)}, u32[]{:S(2)}, u32[]{:S(2)}) collective-permute-start(bf16[96,3072]{1,0:T(8,128)(2,1)} %fusion.120), channel_id=1, source_target_pairs={{0,4},{2,6},{8,0},{10,2},{16,8},{18,10},{24,16},{26,18},{28,24},{3... | collective-permute-start | bytes 1769480 | tf_op jit(solution)/shard_map/ppermute | solution.py:217
  712.0 16.9 %collective-permute-start.90 = (bf16[96,3072]{1,0:T(8,128)(2,1)}, bf16[96,3072]{1,0:T(8,128)(2,1)}, u32[]{:S(2)}, u32[]{:S(2)}) collective-permute-start(bf16[96,3072]{1,0:T(8,128)(2,1)} %fusion.122), channel_id=1, source_target_pairs={{0,8},{2,10},{8,16},{10,18},{16,24},{18,26},{24,28},{26,30},{28,20... | collective-permute-start | bytes 1769480 | tf_op jit(solution)/shard_map/ppermute | solution.py:217
  713.7 22.3 %collective-permute-start.66 = (bf16[3,64,1536]{2,1,0:T(8,128)(2,1)}, bf16[3,64,1536]{2,1,0:T(8,128)(2,1)}, u32[]{:S(2)}, u32[]{:S(2)}) collective-permute-start(bf16[3,64,1536]{2,1,0:T(8,128)(2,1)} %bitcast.192), channel_id=1, source_target_pairs={{0,1},{1,0},{2,3},{3,2},{4,5},{5,4},{6,7},{7,6},{8,9},{9,8},{10,11... | collective-permute-start | bytes 1769480 | tf_op jit(solution)/shard_map/ppermute | solution.py:276
  728.8 49.8 %collective-permute-start.75 = (bf16[8,96,768]{2,1,0:T(8,128)(2,1)}, bf16[8,96,768]{2,1,0:T(8,128)(2,1)}, u32[]{:S(2)}, u32[]{:S(2)}) collective-permute-start(bf16[8,96,768]{2,1,0:T(8,128)(2,1)} %dynamic-slice_bitcast_fusion.4), channel_id=1, source_target_pairs={{0,2},{2,0},{4,6},{6,4},{8,10},{10,8},{12,14},{14,12},{16,18},{18,... | collective-permute-start | bytes 3538952 | tf_op jit(solution)/shard_map/ppermute | solution.py:195
  729.9 27.6 %collective-permute-start.65 = (bf16[3,128,1536]{2,1,0:T(8,128)(2,1)S(1)}, bf16[3,128,1536]{2,1,0:T(8,128)(2,1)S(1)}, u32[]{:S(2)}, u32[]{:S(2)}) collective-permute-start(bf16[3,128,1536]{2,1,0:T(8,128)(2,1)S(1)} %bitcast.1199), channel_id=1, source_target_pairs={{0,1},{1,0},{2,3},{3,2},{4,5},{5,4},{6,7},{7,6},{8,9},{9,8},{10,11... | collective-permute-start | bytes 3538952 | tf_op jit(solution)/shard_map/ppermute | solution.py:276
  736.0 47.8 %collective-permute-start.73 = (bf16[8,96,768]{2,1,0:T(8,128)(2,1)}, bf16[8,96,768]{2,1,0:T(8,128)(2,1)}, u32[]{:S(2)}, u32[]{:S(2)}) collective-permute-start(bf16[8,96,768]{2,1,0:T(8,128)(2,1)} %dynamic-slice_bitcast_fusion.6), channel_id=1, source_target_pairs={{0,2},{2,0},{4,6},{6,4},{8,10},{10,8},{12,14},{14,12},{16,18},{18,... | collective-permute-start | bytes 3538952 | tf_op jit(solution)/shard_map/ppermute | solution.py:195
  757.5 28.2 %collective-permute-start.74 = (bf16[8,96,768]{2,1,0:T(8,128)(2,1)S(1)}, bf16[8,96,768]{2,1,0:T(8,128)(2,1)}, u32[]{:S(2)}, u32[]{:S(2)}) collective-permute-start(bf16[8,96,768]{2,1,0:T(8,128)(2,1)S(1)} %copy-done.126), channel_id=1, source_target_pairs={{0,2},{2,0},{4,6},{6,4},{8,10},{10,8},{12,14},{14,12},{16,18},{18,... | collective-permute-start | bytes 3538952 | tf_op jit(solution)/shard_map/ppermute | solution.py:195
  783.8 21.3 %collective-permute-start.67 = (bf16[61440]{0:T(1024)(128)(2,1)S(1)}, bf16[61440]{0:T(1024)(128)(2,1)S(1)}, u32[]{:S(2)}, u32[]{:S(2)}) collective-permute-start(bf16[61440]{0:T(1024)(128)(2,1)S(1)} %constant_dynamic-update-slice_fusion.15), channel_id=1, source_target_pairs={{0,1},{1,0},{2,3},{3,2},{4,5},{5,4},{6,7},{7,6},{8,9},{9,8},{10,11... | collective-permute-start | bytes 368648 | tf_op jit(solution)/shard_map/ppermute | solution.py:499
  794.6 15.4 %collective-permute-start.76 = (bf16[96,3072]{1,0:T(8,128)(2,1)}, bf16[96,3072]{1,0:T(8,128)(2,1)}, u32[]{:S(2)}, u32[]{:S(2)}) collective-permute-start(bf16[96,3072]{1,0:T(8,128)(2,1)} %pad_maximum_fusion.15), channel_id=1, source_target_pairs={{0,8},{2,10},{8,16},{10,18},{16,24},{18,26},{24,28},{26,30},{28,20... | collective-permute-start | bytes 1769480 | tf_op jit(solution)/shard_map/ppermute | solution.py:217
  804.1 16.8 %collective-permute-start.77 = (bf16[96,3072]{1,0:T(8,128)(2,1)}, bf16[96,3072]{1,0:T(8,128)(2,1)}, u32[]{:S(2)}, u32[]{:S(2)}) collective-permute-start(bf16[96,3072]{1,0:T(8,128)(2,1)} %pad_maximum_fusion.16), channel_id=1, source_target_pairs={{0,4},{2,6},{8,0},{10,2},{16,8},{18,10},{24,16},{26,18},{28,24},{3... | collective-permute-start | bytes 1769480 | tf_op jit(solution)/shard_map/ppermute | solution.py:217
  822.2 19.5 %collective-permute-start.78 = (bf16[96,3072]{1,0:T(8,128)(2,1)S(1)}, bf16[96,3072]{1,0:T(8,128)(2,1)S(1)}, u32[]{:S(2)}, u32[]{:S(2)}) collective-permute-start(bf16[96,3072]{1,0:T(8,128)(2,1)S(1)} %fusion.99), channel_id=1, source_target_pairs={{0,8},{2,10},{8,16},{10,18},{16,24},{18,26},{24,28},{26,30},{28,20... | collective-permute-start | bytes 1769480 | tf_op jit(solution)/shard_map/ppermute | solution.py:217
  824.4 24.0 %collective-permute-start.84 = (bf16[96,3072]{1,0:T(8,128)(2,1)S(1)}, bf16[96,3072]{1,0:T(8,128)(2,1)S(1)}, u32[]{:S(2)}, u32[]{:S(2)}) collective-permute-start(bf16[96,3072]{1,0:T(8,128)(2,1)S(1)} %fusion.105), channel_id=1, source_target_pairs={{0,4},{2,6},{8,0},{10,2},{16,8},{18,10},{24,16},{26,18},{28,24},{3... | collective-permute-start | bytes 1769480 | tf_op jit(solution)/shard_map/ppermute | solution.py:217
  841.9 15.6 %collective-permute-start.79 = (bf16[96,3072]{1,0:T(8,128)(2,1)S(1)}, bf16[96,3072]{1,0:T(8,128)(2,1)S(1)}, u32[]{:S(2)}, u32[]{:S(2)}) collective-permute-start(bf16[96,3072]{1,0:T(8,128)(2,1)S(1)} %fusion.100), channel_id=1, source_target_pairs={{0,8},{2,10},{8,16},{10,18},{16,24},{18,26},{24,28},{26,30},{28,20... | collective-permute-start | bytes 1769480 | tf_op jit(solution)/shard_map/ppermute | solution.py:217
  848.7 11.8 %collective-permute-start.85 = (bf16[96,3072]{1,0:T(8,128)(2,1)S(1)}, bf16[96,3072]{1,0:T(8,128)(2,1)S(1)}, u32[]{:S(2)}, u32[]{:S(2)}) collective-permute-start(bf16[96,3072]{1,0:T(8,128)(2,1)S(1)} %fusion.106), channel_id=1, source_target_pairs={{0,4},{2,6},{8,0},{10,2},{16,8},{18,10},{24,16},{26,18},{28,24},{3... | collective-permute-start | bytes 1769480 | tf_op jit(solution)/shard_map/ppermute | solution.py:217
  857.6 15.1 %collective-permute-start.80 = (bf16[96,3072]{1,0:T(8,128)(2,1)S(1)}, bf16[96,3072]{1,0:T(8,128)(2,1)S(1)}, u32[]{:S(2)}, u32[]{:S(2)}) collective-permute-start(bf16[96,3072]{1,0:T(8,128)(2,1)S(1)} %fusion.101), channel_id=1, source_target_pairs={{0,8},{2,10},{8,16},{10,18},{16,24},{18,26},{24,28},{26,30},{28,20... | collective-permute-start | bytes 1769480 | tf_op jit(solution)/shard_map/ppermute | solution.py:217
  860.6 12.7 %collective-permute-start.86 = (bf16[96,3072]{1,0:T(8,128)(2,1)S(1)}, bf16[96,3072]{1,0:T(8,128)(2,1)S(1)}, u32[]{:S(2)}, u32[]{:S(2)}) collective-permute-start(bf16[96,3072]{1,0:T(8,128)(2,1)S(1)} %fusion.107), channel_id=1, source_target_pairs={{0,4},{2,6},{8,0},{10,2},{16,8},{18,10},{24,16},{26,18},{28,24},{3... | collective-permute-start | bytes 1769480 | tf_op jit(solution)/shard_map/ppermute | solution.py:217
  872.9 13.5 %collective-permute-start.81 = (bf16[96,3072]{1,0:T(8,128)(2,1)S(1)}, bf16[96,3072]{1,0:T(8,128)(2,1)S(1)}, u32[]{:S(2)}, u32[]{:S(2)}) collective-permute-start(bf16[96,3072]{1,0:T(8,128)(2,1)S(1)} %fusion.102), channel_id=1, source_target_pairs={{0,8},{2,10},{8,16},{10,18},{16,24},{18,26},{24,28},{26,30},{28,20... | collective-permute-start | bytes 1769480 | tf_op jit(solution)/shard_map/ppermute | solution.py:217
  873.4 13.5 %collective-permute-start.87 = (bf16[96,3072]{1,0:T(8,128)(2,1)S(1)}, bf16[96,3072]{1,0:T(8,128)(2,1)S(1)}, u32[]{:S(2)}, u32[]{:S(2)}) collective-permute-start(bf16[96,3072]{1,0:T(8,128)(2,1)S(1)} %fusion.108), channel_id=1, source_target_pairs={{0,4},{2,6},{8,0},{10,2},{16,8},{18,10},{24,16},{26,18},{28,24},{3... | collective-permute-start | bytes 1769480 | tf_op jit(solution)/shard_map/ppermute | solution.py:217
  886.6 13.4 %collective-permute-start.82 = (bf16[96,3072]{1,0:T(8,128)(2,1)S(1)}, bf16[96,3072]{1,0:T(8,128)(2,1)S(1)}, u32[]{:S(2)}, u32[]{:S(2)}) collective-permute-start(bf16[96,3072]{1,0:T(8,128)(2,1)S(1)} %fusion.103), channel_id=1, source_target_pairs={{0,8},{2,10},{8,16},{10,18},{16,24},{18,26},{24,28},{26,30},{28,20... | collective-permute-start | bytes 1769480 | tf_op jit(solution)/shard_map/ppermute | solution.py:217
  887.1 13.3 %collective-permute-start.88 = (bf16[96,3072]{1,0:T(8,128)(2,1)S(1)}, bf16[96,3072]{1,0:T(8,128)(2,1)S(1)}, u32[]{:S(2)}, u32[]{:S(2)}) collective-permute-start(bf16[96,3072]{1,0:T(8,128)(2,1)S(1)} %fusion.109), channel_id=1, source_target_pairs={{0,4},{2,6},{8,0},{10,2},{16,8},{18,10},{24,16},{26,18},{28,24},{3... | collective-permute-start | bytes 1769480 | tf_op jit(solution)/shard_map/ppermute | solution.py:217
  900.1 11.8 %collective-permute-start.83 = (bf16[96,3072]{1,0:T(8,128)(2,1)S(1)}, bf16[96,3072]{1,0:T(8,128)(2,1)S(1)}, u32[]{:S(2)}, u32[]{:S(2)}) collective-permute-start(bf16[96,3072]{1,0:T(8,128)(2,1)S(1)} %fusion.104), channel_id=1, source_target_pairs={{0,8},{2,10},{8,16},{10,18},{16,24},{18,26},{24,28},{26,30},{28,20... | collective-permute-start | bytes 1769480 | tf_op jit(solution)/shard_map/ppermute | solution.py:217
  (248 other events, 2709.4 us)
Sparse Core Ops, SparseCore 0:
  11.2 121.3 all-gather.4
  134.7 99.0 all-gather.6
  235.4 98.9 all-gather.8
  806.0 46.4 all-gather.10

commit v2 on v1

v2 whole, which is shorter than its diff:
```python
import functools

import jax
import jax.numpy as jnp
from jax import lax
from jax.experimental import pallas as pl
from jax.experimental.pallas import tpu as pltpu
from jax.sharding import PartitionSpec as P

HEAD_DIM = 64
EPSILON = 1e-06
F32 = jnp.float32
BF16 = jnp.bfloat16


def gelu_pair(values):
    root, cubic = (2.0 / 3.141592653589793) ** 0.5, 0.044715
    square = values * values
    bend = jnp.tanh(root * values * (1.0 + cubic * square))
    half = 0.5 * (1.0 + bend)
    slope = half + 0.5 * values * (1.0 - bend * bend) * root * (1.0 + 3.0 * cubic * square)
    return values * half, slope


def dot(left, right, dims):
    return lax.dot_general(left, right, (dims, ((), ())), preferred_element_type=F32)


NN = ((1,), (0,))
NT = ((1,), (1,))
TN = ((0,), (0,))


def join_rows(text_ref, image_ref):
    width = text_ref.shape[-1]
    return jnp.concatenate(
        [text_ref[...].reshape(-1, width), image_ref[...].reshape(-1, width)], axis=0
    )


def parts_of(joined):
    lanes = joined.shape[1] // 3
    return [joined[:, place * lanes : (place + 1) * lanes] for place in range(3)]


def attention_kernel(image_ref, text_ref, oi, ot):
    query, key, value = parts_of(join_rows(text_ref, image_ref))
    width = query.shape[1]
    head_of = lax.broadcasted_iota(jnp.int32, query.shape, 1) // HEAD_DIM
    out = jnp.zeros(query.shape, F32)
    for head in range(width // HEAD_DIM):
        inside = head_of == head
        scores = dot(jnp.where(inside, query, jnp.zeros_like(query)), key, NT) * HEAD_DIM**-0.5
        raised = jnp.exp(scores - jnp.max(scores, axis=1, keepdims=True))
        probs = raised * (1.0 / jnp.sum(raised, axis=1, keepdims=True))
        out = jnp.where(inside, dot(probs.astype(BF16), value, NN), out)
    text_rows = ot.shape[0] * ot.shape[1]
    ot[...] = out[:text_rows].astype(BF16).reshape(ot.shape)
    oi[...] = out[text_rows:].astype(BF16).reshape(oi.shape)


def attention_back_kernel(image_ref, text_ref, gi, gt, di, dt):
    query, key, value = parts_of(join_rows(text_ref, image_ref))
    grad = join_rows(gt, gi)
    width = query.shape[1]
    head_of = lax.broadcasted_iota(jnp.int32, query.shape, 1) // HEAD_DIM
    blank = jnp.zeros_like(query)
    dq, dk, dv = (jnp.zeros(query.shape, F32) for _ in range(3))
    scale = HEAD_DIM**-0.5
    for head in range(width // HEAD_DIM):
        inside = head_of == head
        scores = dot(jnp.where(inside, key, blank), query, NT) * scale
        raised = jnp.exp(scores - jnp.max(scores, axis=0, keepdims=True))
        probs = raised * (1.0 / jnp.sum(raised, axis=0, keepdims=True))
        grad_probs = dot(jnp.where(inside, value, blank), grad, NT)
        delta = jnp.sum(probs * grad_probs, axis=0, keepdims=True)
        grad_scores = (probs * (grad_probs - delta)).astype(BF16)
        dv = jnp.where(inside, dot(probs.astype(BF16), grad, NN), dv)
        dk = jnp.where(inside, dot(grad_scores, query, NN) * scale, dk)
        dq = jnp.where(inside, dot(grad_scores, key, TN) * scale, dq)
    text_rows = dt.shape[0] * dt.shape[1]
    low = jnp.concatenate([part.astype(BF16) for part in (dq, dk, dv)], axis=1)
    dt[...] = low[:text_rows].reshape(dt.shape)
    di[...] = low[text_rows:].reshape(di.shape)


def head_block(width):
    return 128 if width % 128 == 0 else width


def blocked(shape, lanes, first=0):
    return pl.BlockSpec(
        (shape[0], None, shape[2], lanes), lambda seq, block: (0, seq + first, 0, block)
    )


VMEM = pltpu.CompilerParams(vmem_limit_bytes=48 * 2**20)
COST = pl.CostEstimate(flops=1024, transcendentals=0, bytes_accessed=1024)


def attention_forward(image, text):
    seqs, width = image.shape[1], image.shape[3] // 3
    lanes = head_block(width)
    shapes = [jax.ShapeDtypeStruct(a.shape[:3] + (width,), BF16) for a in (image, text)]
    return pl.pallas_call(
        attention_kernel,
        grid=(seqs, width // lanes),
        in_specs=[blocked(a.shape, 3 * lanes) for a in (image, text)],
        out_specs=[blocked(s.shape, lanes) for s in shapes],
        out_shape=shapes,
        compiler_params=VMEM,
        cost_estimate=COST,
        name="attention_forward",
    )(image, text)


def attention_backward(image, text, image_grad, text_grad, first, into):
    width = image.shape[3] // 3
    lanes = head_block(width)
    specs = [blocked(a.shape, 3 * lanes, first) for a in (image, text)]
    specs += [blocked(a.shape, lanes, first) for a in (image_grad, text_grad)]
    kernel = attention_back_kernel
    if into:
        specs += [pl.BlockSpec(memory_space=pl.ANY)] * 2

        def kernel(image_ref, text_ref, gi, gt, unused_image, unused_text, di, dt):
            attention_back_kernel(image_ref, text_ref, gi, gt, di, dt)

    return pl.pallas_call(
        kernel,
        grid=(1, width // lanes),
        in_specs=specs,
        out_specs=[blocked(a.shape, 3 * lanes, first) for a in (image, text)],
        out_shape=[jax.ShapeDtypeStruct(a.shape, BF16) for a in (image, text)],
        input_output_aliases={4: 0, 5: 1} if into else {},
        compiler_params=VMEM,
        cost_estimate=COST,
        name="attention_backward",
    )(image, text, image_grad, text_grad, *into)


def centred(values):
    center = values - jnp.mean(values, axis=-1, keepdims=True)
    inverse = lax.rsqrt(jnp.mean(center * center, axis=-1, keepdims=True) + EPSILON)
    return center * inverse, inverse


def norm_back(normed, inverse, upstream):
    mean_up = jnp.mean(upstream, axis=-1, keepdims=True)
    mean_cross = jnp.mean(upstream * normed, axis=-1, keepdims=True)
    return inverse * (upstream - mean_up - normed * mean_cross)


def column_sum(values):
    return jnp.sum(values, axis=0, keepdims=True)


def enter_kernel(live_ref, tokens, cot, mod, low_ref, branch_ref, sum_ref):
    live = live_ref[pl.program_id(0)].astype(F32)
    normed, unused = centred(tokens[...].astype(F32))
    low_ref[...] = (normed * (1.0 + mod[1:2]) + mod[0:1]).astype(BF16)
    branch = cot[...].astype(F32) * live * mod[5:6]
    branch_ref[...] = branch.astype(BF16)
    sum_ref[...] = column_sum(branch)


def middle_kernel(live_ref, kept, came, tokens, bias, mod, branch_ref, resid_ref, low_ref):
    branch = kept[...] + came[...].astype(F32) + bias[...]
    resid = tokens[...].astype(F32) + mod[2:3] * branch
    normed, unused = centred(resid)
    branch_ref[...] = branch
    resid_ref[...] = resid
    low_ref[...] = (normed * (1.0 + mod[4:5]) + mod[3:4]).astype(BF16)


def middle_back_kernel(
    live_ref, kept, came, cot, resid, branch, mod, grad_ref, low_ref, sum_ref, bias_ref
):
    live = live_ref[pl.program_id(0)].astype(F32)
    back = kept[...] + came[...].astype(F32)
    normed, inverse = centred(resid[...])
    grad = cot[...].astype(F32) * live + norm_back(normed, inverse, back * (1.0 + mod[4:5]))
    grad_ref[...] = grad
    low = grad * mod[2:3]
    low_ref[...] = low.astype(BF16)
    sum_ref[0:1] = column_sum(grad * branch[...])
    sum_ref[1:2] = column_sum(back)
    sum_ref[2:3] = column_sum(back * normed)
    bias_ref[...] = column_sum(low)


def leave_kernel(live_ref, kept, came, resid, cot, bias, mod, out_ref, sum_ref):
    live = live_ref[pl.program_id(0)].astype(F32)
    branch = kept[...] + came[...].astype(F32) + bias[...]
    out_ref[...] = (live * (resid[...] + mod[5:6] * branch)).astype(BF16)
    sum_ref[...] = column_sum(cot[...].astype(F32) * live * branch)


def enter_back_kernel(live_ref, kept, came, tokens, grad, mod, grad_ref, sum_ref):
    back = kept[...] + came[...].astype(F32)
    normed, inverse = centred(tokens[...].astype(F32))
    grad_ref[...] = grad[...] + norm_back(normed, inverse, back * (1.0 + mod[1:2]))
    sum_ref[0:1] = column_sum(back)
    sum_ref[1:2] = column_sum(back * normed)


def stage(kernel, live, arrays, rows, kinds, name):
    seqs, width = live.shape[0], arrays[0].shape[-1]
    specs = []
    for array in arrays:
        if array.ndim == 2:
            specs.append(pl.BlockSpec((1, width), lambda i, live_ref: (0, 0)))
        elif array.ndim == 3:
            block = (None,) + array.shape[1:]
            specs.append(pl.BlockSpec(block, lambda i, live_ref: (i, 0, 0)))
        else:
            block = (None, None) + array.shape[2:]
            specs.append(pl.BlockSpec(block, lambda i, live_ref: (0, i, 0, 0)))
    shapes = [jax.ShapeDtypeStruct((seqs, r, width), kind) for r, kind in zip(rows, kinds)]
    return pl.pallas_call(
        kernel,
        grid_spec=pltpu.PrefetchScalarGridSpec(
            num_scalar_prefetch=1,
            grid=(seqs,),
            in_specs=specs,
            out_specs=[
                pl.BlockSpec((None, r, width), lambda i, live_ref: (i, 0, 0)) for r in rows
            ],
        ),
        out_shape=shapes,
        compiler_params=VMEM,
        cost_estimate=COST,
        name=name,
    )(live, *arrays)


def pack(arrays, picks, name):
    seqs, width = arrays[0].shape[0], arrays[0].shape[2]

    def kernel(*refs):
        refs[-1][...] = jnp.concatenate(
            [refs[array][row : row + 1] for array, row in picks], axis=0
        ).astype(BF16)

    return pl.pallas_call(
        kernel,
        grid=(seqs,),
        in_specs=[pl.BlockSpec((None,) + a.shape[1:], lambda i: (i, 0, 0)) for a in arrays],
        out_specs=pl.BlockSpec((None, len(picks), width), lambda i: (i, 0, 0)),
        out_shape=jax.ShapeDtypeStruct((seqs, len(picks), width), BF16),
        compiler_params=VMEM,
        cost_estimate=COST,
        name=name,
    )(*arrays)


def whole(array):
    return [(array, array.shape[0], 0)]


def halves(array, count):
    return [(array, array.shape[0] // count, n) for n in range(count)]


def weight_grad(left, right, core, dp):
    width, columns = left[0][0].shape[1], right[0][0].shape[1]
    rows = width // dp
    chips = max(1, 384 // (2 * rows))
    block = chips * 2 * rows
    count = len(left)

    def kernel(core_ref, *refs):
        keep_ref, give_ref = refs[2 * count :]
        value = dot(refs[0][...], refs[count][...], TN)
        for n in range(1, count):
            value = value + dot(refs[n][...], refs[count + n][...], TN)
        value = value.astype(BF16).reshape(chips, 2, rows, columns)
        first = core_ref[0] == 0

        @pl.when(first)
        def unused_first():
            keep_ref[...] = value[:, 0]
            give_ref[...] = value[:, 1]

        @pl.when(jnp.logical_not(first))
        def unused_second():
            keep_ref[...] = value[:, 1]
            give_ref[...] = value[:, 0]

    specs = [
        pl.BlockSpec((depth, block), lambda i, core_ref, which=which: (which, i))
        for unused, depth, which in left
    ]
    specs += [
        pl.BlockSpec(
            (depth, columns),
            lambda i, core_ref, which=which: (which, 0),
            pipeline_mode=pl.Buffered(1),
        )
        for unused, depth, which in right
    ]
    out = pl.BlockSpec((chips, rows, columns), lambda i, core_ref: (i, 0, 0))
    return pl.pallas_call(
        kernel,
        grid_spec=pltpu.PrefetchScalarGridSpec(
            num_scalar_prefetch=1, grid=(width // block,), in_specs=specs, out_specs=[out, out]
        ),
        out_shape=[jax.ShapeDtypeStruct((dp // 2, rows, columns), BF16)] * 2,
        compiler_params=VMEM,
        cost_estimate=COST,
        name="weight_grad",
    )(core.reshape(1), *[piece[0] for piece in left + right])


def matmul(pieces, weights, stream, dims, start, size, epilogue, outs, extra, name):
    if start % 128 or size % 128:
        weights, start = weights[:, :, start : start + size], 0
    depth = weights.shape[1]
    columns = size if dims == NN else depth
    tile = next((t for t in (512, 384) if columns % t == 0), columns)
    specs = [
        pl.BlockSpec(
            (rows, array.shape[1]),
            lambda j, which=which: (which, 0),
            pipeline_mode=pl.Buffered(1),
        )
        for array, rows, which in pieces
    ]
    if dims == NN:
        specs.append(
            pl.BlockSpec((None, depth, tile), lambda j: (stream, 0, start // tile + j))
        )
    else:
        specs.append(pl.BlockSpec((None, tile, size), lambda j: (stream, j, start // size)))
    for array in extra:
        if array.ndim == 3:
            specs.append(pl.BlockSpec((None, 1, tile), lambda j: (stream, 0, j)))
        else:
            specs.append(pl.BlockSpec((array.shape[0], tile), lambda j: (0, j)))
    count = len(pieces)

    def kernel(*refs):
        extras, results = refs[count + 1 : count + 1 + len(extra)], refs[count + 1 + len(extra) :]
        at = 0
        for n, (unused, rows, which) in enumerate(pieces):
            product = dot(refs[n][...], refs[count][...], dims)
            epilogue(n, slice(at, at + rows), product, extras, results)
            at += rows

    return pl.pallas_call(
        kernel,
        grid=(columns // tile,),
        in_specs=specs,
        out_specs=[pl.BlockSpec((rows, tile), lambda j: (0, j)) for rows, unused in outs],
        out_shape=[jax.ShapeDtypeStruct((rows, columns), kind) for rows, kind in outs],
        compiler_params=VMEM,
        cost_estimate=COST,
        name=name,
    )(*[piece[0] for piece in pieces], weights, *extra)


def low_of(n, rows, product, extras, results):
    results[0][rows] = product.astype(BF16)


def low_biased(n, rows, product, extras, results):
    results[0][rows] = (product + extras[0][...]).astype(BF16)


def gelu_biased(n, rows, product, extras, results):
    value, slope = gelu_pair(product + extras[0][...])
    results[0][rows] = value.astype(BF16)
    results[1][rows] = slope


def sloped(n, rows, product, extras, results):
    low = (product * extras[0][rows]).astype(BF16)
    results[0][rows] = low
    total = column_sum(low.astype(F32))
    results[1][...] = total if n == 0 else results[1][...] + total


def apart(n, rows, product, extras, results):
    results[n][...] = product.astype(results[n].dtype)


def ring_of(chips):
    wide = 1
    while (2 * wide) ** 2 <= chips:
        wide *= 2
    long = chips // wide
    order = [row * wide for row in range(long)]
    for turn, row in enumerate(reversed(range(long))):
        across = list(range(1, wide))
        order += [row * wide + col for col in (across if turn % 2 == 0 else across[::-1])]
    return order


class Rings:
    def __init__(self, dp, kind=BF16):
        self.kind, self.dp = kind, dp
        self.chips = dp // 2
        order = ring_of(self.chips)
        me = lax.axis_index("dp")
        chip, self.core = me // 2, me % 2
        self.hops, self.targets = [], []
        for way in (1, -1):
            self.hops.append(
                [
                    (2 * order[i] + c, 2 * order[(i + way) % self.chips] + c)
                    for i in range(self.chips)
                    for c in range(2)
                ]
            )
            targets = []
            for step in range(self.chips):
                at = jnp.int32(0)
                for spot, here in enumerate(order):
                    goal = order[(spot - way * (1 + step)) % self.chips]
                    at = at + jnp.where(chip == here, goal, 0)
                targets.append(at)
            self.targets.append(targets)
        self.views, self.flying = ([], []), ([], [])
        self.step = 0
        self.result = None

    def give(self, stream, keep, gift):
        self.views[stream].append(keep)
        swap = [(i, i ^ 1) for i in range(self.dp)]
        self.flying[stream].append(lax.ppermute(gift, "dp", swap))

    def add(self, came):
        last = self.step == self.chips - 1
        widths = [view.shape[-1] for view in self.views[0]]
        rows = self.views[0][0].shape[1]
        tile = rows // 3 if rows % 48 == 0 else rows
        at = jnp.stack([self.targets[s][self.step] for s in range(2)])
        operands, specs, places = [], [], []
        for s in range(2):
            for view, got in zip(self.views[s], self.got[s]):
                width = view.shape[-1]
                operands += [view, got]
                block = pl.BlockSpec((None, tile, width), lambda i, at, s=s: (at[s], i, 0))
                specs += [block, block]
            if came is not None:
                operands.append(came[s])
                specs.append(pl.BlockSpec((tile, sum(widths)), lambda i, at: (i, 0)))
        sizes = widths if last else [sum(widths)]
        kind = F32 if last else self.kind
        shapes = [jax.ShapeDtypeStruct((rows, size), kind) for size in sizes] * 2

        def kernel(at_ref, *refs):
            ins, outs = refs[: len(operands)], refs[len(operands) :]
            per_way = len(operands) // 2
            for s in range(2):
                mine = ins[s * per_way : (s + 1) * per_way]
                start = 0
                for number, width in enumerate(widths):
                    value = mine[2 * number][...].astype(F32) + mine[2 * number + 1][...].astype(F32)
                    if came is not None:
                        value = value + mine[-1][:, start : start + width].astype(F32)
                    if last:
                        outs[s * len(sizes) + number][...] = value
                    else:
                        outs[s][:, start : start + width] = value.astype(kind)
                    start += width

        out = pl.pallas_call(
            kernel,
            grid_spec=pltpu.PrefetchScalarGridSpec(
                num_scalar_prefetch=1,
                grid=(rows // tile,),
                in_specs=specs,
                out_specs=[
                    pl.BlockSpec((tile, shape.shape[1]), lambda i, at: (i, 0)) for shape in shapes
                ],
            ),
            out_shape=shapes,
            compiler_params=VMEM,
            cost_estimate=COST,
            name="ring_add",
        )(at, *operands)
        return [out[s * len(sizes) : (s + 1) * len(sizes)] for s in range(2)]

    def advance(self):
        if self.step == 0:
            self.got = self.flying
            total = self.add(None)
        else:
            total = self.add([flight[0] for flight in self.flying])
        self.sent = total
        if self.step == self.chips - 1:
            self.result = total
            self.flying = ([], [])
        else:
            self.flying = tuple(
                [lax.ppermute(total[s][0], "dp", self.hops[s])] for s in range(2)
            )
        self.step += 1

    def finish(self):
        while self.result is None:
            self.advance()
        return self.result


def beat(value, rings):
    if rings.result is None:
        value, rings.flying = lax.optimization_barrier((value, rings.flying))
        rings.advance()
        value, unused = lax.optimization_barrier((value, rings.sent))
    return value


def tie(*values):
    return lax.optimization_barrier(values)


def body(
    mp,
    dp,
    image_tokens,
    text_tokens,
    condition,
    live_table,
    ada_weight,
    ada_bias,
    qkv_weight,
    qv_bias,
    proj_weight,
    proj_bias,
    fc1_weight,
    fc1_bias,
    fc2_weight,
    fc2_bias,
    image_cotangent,
    text_cotangent,
):
    seqs, width = image_tokens.shape[0], image_tokens.shape[2]
    my_dp = lax.axis_index("dp")
    swap = [(0, 1), (1, 0)]

    def share(rows):
        if mp == 2:
            return whole(flat(rows)) + whole(flat(lax.ppermute(rows, "mp", swap)))
        return whole(flat(lax.all_gather(rows, "mp", axis=0, tiled=False)))

    def split(array):
        return halves(array, 2 if mp == 2 else 1)

    def collect(array, weights, stream, start, size, name):
        pieces = split(array)
        outs = [(piece[1], kind) for piece, kind in zip(pieces, (F32, BF16))]
        parts = matmul(pieces, weights, stream, NT, start, size, apart, outs, [], name)
        if mp == 2:
            shape = (1, seqs, -1, width)
            return [parts[0].reshape(shape), parts[1].reshape(shape[1:])]

        low = parts[0].astype(BF16).reshape(mp, seqs, -1, width)
        return [low, low[0]]

    def exchange(parts):
        if mp == 2:
            return parts[0], lax.ppermute(parts[1], "mp", swap)
        low = lax.psum_scatter(parts[0], "mp", scatter_dimension=0, tiled=False)
        return low.astype(F32), jnp.zeros_like(low)

    def sum_mp(values):
        if mp == 2:
            return values + lax.ppermute(values, "mp", swap)
        return lax.psum(values, "mp")

    def flat(array):
        return array.reshape(-1, array.shape[-1])

    def gather_small(rows, after=lambda rows: rows):
        shape, reach, bits = rows.shape, dp // 2, 0
        while reach >= 1:
            other = lax.ppermute(rows, "dp", [(i, i ^ reach) for i in range(dp)])
            low_half = (my_dp & reach) == 0
            rows = jnp.concatenate(
                [jnp.where(low_half, rows, other), jnp.where(low_half, other, rows)], axis=0
            )
            rows = after(rows)
            reach, bits = reach // 2, bits + 1
        rows = rows.reshape((2,) * bits + shape)
        order = tuple(reversed(range(bits))) + tuple(range(bits, bits + len(shape)))
        return rows.transpose(order).reshape((dp,) + shape)

    small = [condition, ada_bias, qv_bias, proj_bias, fc1_bias, fc2_bias]
    sizes = [a.size for a in small]
    packed = jnp.concatenate([a.astype(BF16).reshape(-1) for a in small])
    packed = jnp.pad(packed, (0, -packed.size % 2048)).reshape(-1, 128)
    packed = gather_small(packed).reshape(dp, -1)
    pieces, at = [], 0
    for array, size in zip(small, sizes):
        pieces.append(packed[:, at : at + size].reshape((dp,) + array.shape))
        at += size
    cond_all = pieces[0].reshape(dp * seqs, -1)
    ada_biases, proj_biases, up_biases, down_biases = (
        jnp.moveaxis(pieces[i], 0, 1).reshape(2, -1).astype(F32) for i in (1, 3, 4, 5)
    )
    qv_biases = jnp.moveaxis(pieces[2], 0, 2).reshape(2, 2, -1).astype(F32)

    share_rows, heads_width = qkv_weight.shape[2:]
    lanes = head_block(heads_width)
    qkv_low = qkv_weight.astype(BF16).reshape(2, 3, share_rows, -1, lanes)
    qkv_low = qkv_low.transpose(0, 2, 3, 1, 4).reshape(2, share_rows, -1)
    proj_low = jnp.swapaxes(proj_weight.astype(BF16), 1, 2)
    attention_full = lax.all_gather(
        jnp.concatenate([qkv_low, proj_low], axis=2), "dp", axis=1, tiled=True
    )
    qkv_size = 3 * heads_width
    up_full = lax.all_gather(fc1_weight.astype(BF16), "dp", axis=1, tiled=True)
    down_full = lax.all_gather(
        jnp.swapaxes(fc2_weight.astype(BF16), 1, 2), "dp", axis=1, tiled=True
    )
    biases = qv_biases.reshape(2, 2, -1, lanes)
    biases = jnp.stack([biases[:, 0], jnp.zeros_like(biases[:, 0]), biases[:, 1]], axis=2)
    biases = biases.reshape(2, 1, -1)

    ada_low = ada_weight.astype(BF16)
    ada_rows = ada_low.shape[1]
    silu_all = jax.nn.silu(cond_all.astype(F32)).astype(BF16)
    silu_mine = lax.dynamic_slice_in_dim(silu_all, my_dp * ada_rows, ada_rows, axis=1)
    core = lax.rem(my_dp, 2)
    mod_rings = Rings(dp, F32)
    for s in range(2):
        partial = dot(silu_mine, ada_low[s], NN).reshape(dp // 2, 2, -1, 128)
        keep, gift = (lax.dynamic_index_in_dim(partial, c, 1, False) for c in (core, 1 - core))
        mod_rings.give(s, keep, gift)
    modulation = jnp.stack([part[0].reshape(seqs, -1) for part in mod_rings.finish()], axis=1)
    modulation = (sum_mp(modulation) + ada_biases).reshape(seqs, 2, 6, width)
    mod = [modulation[:, s] for s in range(2)]
    live = live_table[0]
    tokens, cotangents = (image_tokens, text_tokens), (image_cotangent, text_cotangent)
    rows_of = [t.shape[1] for t in tokens]

    joint_in, branch_low, branch_sum = [], [], []
    for s in range(2):
        low, branch, total = stage(
            enter_kernel,
            live,
            [tokens[s], cotangents[s], mod[s]],
            [rows_of[s], rows_of[s], 1],
            [BF16, BF16, F32],
            "enter",
        )
        joint_in.append(share(low))
        branch_low.append(branch)
        branch_sum.append(total)
    branch_low, joint_in = tie(branch_low, [[piece[0] for piece in pieces] for pieces in joint_in])
    joint_in = [[piece for array in arrays for piece in whole(array)] for arrays in joint_in]
    down_up = [share(branch_low[s]) for s in range(2)]
    all_rows = [mp * seqs * rows_of[s] for s in range(2)]
    units = up_biases.shape[1]

    qkv = []
    for s in range(2):
        (product,) = matmul(
            joint_in[s],
            attention_full,
            s,
            NN,
            0,
            qkv_size,
            low_biased,
            [(all_rows[s], BF16)],
            [biases],
            "qkv",
        )
        qkv.append(product.reshape(mp, seqs, rows_of[s], -1))
    attended, arrived = tie(
        attention_forward(qkv[0], qkv[1]), [[piece[0] for piece in pieces] for pieces in down_up]
    )
    attended = [flat(o) for o in attended]
    down_up = [[piece for array in arrays for piece in whole(array)] for arrays in arrived]

    residual, first_branch, mlp_in = [None, None], [None, None], [None, None]
    sums = []
    for s in range(2):
        parts = collect(attended[s], attention_full, s, qkv_size, heads_width, "proj")
        sums.append(exchange(parts))
    for s in (1, 0):
        first_branch[s], residual[s], low = stage(
            middle_kernel,
            live,
            [*sums[s], tokens[s], proj_biases[s : s + 1], mod[s]],
            [rows_of[s]] * 3,
            [F32, F32, BF16],
            "middle",
        )
        mlp_in[s] = share(low)

    slope, active = [None, None], [None, None]
    rings, last_rings = Rings(dp), Rings(dp)
    up_bias_rows = up_biases.reshape(2, 1, -1)
    for s in (1, 0):
        active[s], slope[s] = matmul(
            mlp_in[s],
            up_full,
            s,
            NN,
            0,
            units,
            gelu_biased,
            [(all_rows[s], BF16), (all_rows[s], F32)],
            [up_bias_rows],
            "up",
        )
        keep, gift = weight_grad(down_up[s], split(active[s]), core, dp)
        keep, gift, slope = tie(keep, gift, slope)
        rings.give(s, keep, gift)

    grad_pre, back, up_sums = [], [], []
    for s in range(2):
        low, total = matmul(
            down_up[s],
            down_full,
            s,
            NN,
            0,
            units,
            sloped,
            [(all_rows[s], BF16), (1, F32)],
            [slope[s]],
            "down_back",
        )
        grad_pre.append(low)
        up_sums.append(total)
        back.append(collect(low, up_full, s, 0, units, "up_back"))
        back[s], slope, grad_pre = tie(back[s], slope, grad_pre)
        back[s] = exchange(back[s])
    keep, gift = weight_grad(mlp_in[0], split(grad_pre[0]), core, dp)
    keep, gift, grad_pre, back[0] = tie(keep, gift, grad_pre, back[0])
    rings.give(0, keep, gift)
    keep, gift = weight_grad(mlp_in[1], split(grad_pre[1]), core, dp)
    keep, gift, back[1] = tie(keep, gift, back[1])
    rings.give(1, keep, gift)
    back = beat(back, rings)
    back, unused = tie(back, rings.sent)

    resid_grad, attention_low, middle_sums, proj_sums = [], [], [], []
    for s in range(2):
        grad, low, total, bias_total = stage(
            middle_back_kernel,
            live,
            [*back[s], cotangents[s], residual[s], first_branch[s], mod[s]],
            [rows_of[s], rows_of[s], 3, 1],
            [F32, BF16, F32, F32],
            "middle_back",
        )
        resid_grad.append(grad)
        attention_low.append(low)
        middle_sums.append(total)
        proj_sums.append(bias_total)
    attention_low, active, middle_sums = tie(attention_low, active, middle_sums)
    attention_low = [share(rows) for rows in attention_low]
    active = beat(active, rings)
    down_sum = [collect(active[s], down_full, s, 0, units, "down") for s in range(2)]
    down_sum, middle_sums = beat((down_sum, middle_sums), rings)

    arrived, down_sum = tie([[piece[0] for piece in pieces] for pieces in attention_low], down_sum)
    attention_low = [[piece for array in arrays for piece in whole(array)] for arrays in arrived]
    down_sum = [exchange(down_sum[s]) for s in range(2)]

    mixed = []
    for s in range(2):
        (product,) = matmul(
            attention_low[s],
            attention_full,
            s,
            NN,
            qkv_size,
            heads_width,
            low_of,
            [(all_rows[s], BF16)],
            [],
            "proj_back",
        )
        mixed.append(product.reshape(mp, seqs, rows_of[s], -1))
    mixed, attended = beat((mixed, attended), rings)
    for s in range(2):
        keep, gift = weight_grad(attention_low[s], split(attended[s]), core, dp)
        keep, gift, mixed, attended = tie(keep, gift, mixed, attended)
        last_rings.give(s, keep, gift)
    grad_qkv = ()
    for n in range(seqs):
        grad_qkv = attention_backward(qkv[0], qkv[1], mixed[0], mixed[1], n, grad_qkv)
        if n == 1:
            grad_qkv, mixed, last_rings.flying, down_sum = tie(
                grad_qkv, mixed, last_rings.flying, down_sum
            )
        else:
            grad_qkv, mixed = beat((grad_qkv, mixed), rings)
    grad_qkv = [flat(g) for g in grad_qkv]

    back = [None, None]
    for s in range(2):
        back[s] = collect(grad_qkv[s], attention_full, s, 0, qkv_size, "qkv_back")
        back[s], grad_qkv = tie(back[s], grad_qkv)
        back[s] = exchange(back[s])
    for s in range(2):
        keep, gift = weight_grad(joint_in[s], split(grad_qkv[s]), core, dp)
        keep, gift, grad_qkv = tie(keep, gift, grad_qkv)
        last_rings.give(s, keep, gift)
    down_sum, grad_qkv = beat((down_sum, grad_qkv), last_rings)
    outputs, gate_two = [], []
    for s in range(2):
        out, total = stage(
            leave_kernel,
            live,
            [*down_sum[s], residual[s], cotangents[s], down_biases[s : s + 1], mod[s]],
            [rows_of[s], 1],
            [BF16, F32],
            "leave",
        )
        outputs.append(out)
        gate_two.append(total)
    qv_sums = []
    for s in range(2):
        total = jnp.sum(grad_qkv[s].astype(F32), axis=0).reshape(-1, 3, lanes)
        qv_sums += [total[:, 0], total[:, 2]]
    unit_sums = jnp.concatenate([u.reshape(-1) for u in qv_sums + up_sums])
    unit_size = unit_sums.size
    unit_sums = jnp.pad(unit_sums, (0, -unit_size % (seqs * width))).reshape(seqs, -1, width)
    unit_rows = unit_sums.shape[1]
    gate_two, unit_sums = beat((gate_two, unit_sums), rings)
    back, gate_two, unit_sums = tie(back, gate_two, unit_sums)

    input_grads, first_sums = [], []
    for s in range(2):
        grad, total = stage(
            enter_back_kernel,
            live,
            [*back[s], tokens[s], resid_grad[s], mod[s]],
            [rows_of[s], 2],
            [F32, F32],
            "enter_back",
        )
        input_grads.append(grad)
        first_sums.append(total)
    packed_sums, picks = [], []
    for s in range(2):
        at = len(packed_sums)
        packed_sums += [first_sums[s], middle_sums[s], gate_two[s]]
        picks += [(at, 0), (at, 1)] + [(at + 1, row) for row in range(3)] + [(at + 2, 0)]
    for array in proj_sums + branch_sum:
        picks.append((len(packed_sums), 0))
        packed_sums.append(array)
    token_rows = len(picks)
    picks += [(len(packed_sums), row) for row in range(unit_rows)]
    sums = pack(packed_sums + [unit_sums], picks, "pack")
    sums, input_grads = tie(sums, input_grads)
    if mp == 2:
        other = lax.ppermute(sums, "mp", swap)
        row_of = lax.broadcasted_iota(jnp.int32, sums.shape, 1)
        other = jnp.where(row_of < token_rows, other.astype(F32), 0.0)
        sums = (sums.astype(F32) + other).astype(BF16)
    else:
        sums = jnp.concatenate(
            [lax.psum(sums[:, :token_rows], "mp"), sums[:, token_rows:]], axis=1
        )
    gathered = lax.all_gather(sums, "dp", axis=0, tiled=True)
    input_grads = beat(input_grads, last_rings)
    while rings.result is None:
        input_grads = beat(input_grads, rings)
    input_grads = beat(input_grads, last_rings)
    fc2_out, fc1_out = (jnp.stack([part[n] for part in rings.finish()]) for n in range(2))
    fc2_out = jnp.swapaxes(fc2_out, 1, 2)
    fc1_out = beat(fc1_out, last_rings)
    fc2_out = beat(fc2_out, last_rings)
    gathered = beat(gathered, last_rings)

    mod_all = [gathered[:, 6 * s : 6 * s + 6].reshape(dp * seqs, 6 * width) for s in range(2)]
    silu_grad = sum(dot(mod_all[s], ada_low[s], NT) for s in range(2))
    silu_grad = gather_small(silu_grad, lambda rows: beat(rows, last_rings))
    silu_grad, gathered = tie(silu_grad, gathered)
    silu_grad = lax.dynamic_slice_in_dim(silu_grad, my_dp * seqs, seqs, axis=1)
    silu_grad = jnp.moveaxis(silu_grad, 0, 1).reshape(seqs, -1)
    unused, pullback = jax.vjp(jax.nn.silu, condition.astype(F32))
    cond_out = pullback(silu_grad)[0]
    bias_all = jnp.sum(gathered[:, 12:token_rows].astype(F32), axis=0)
    unit_all = jnp.sum(gathered[:, token_rows:].astype(F32).reshape(dp, -1), axis=0)
    qv_size = qv_biases.size

    proj_out, qkv_out = (jnp.stack([part[n] for part in last_rings.finish()]) for n in range(2))
    proj_out = jnp.swapaxes(proj_out, 1, 2)
    qkv_out = qkv_out.reshape(2, share_rows, -1, 3, lanes)
    qkv_out = qkv_out.transpose(0, 3, 1, 2, 4).reshape(qkv_weight.shape)

    def own(total, axis):
        part = total.shape[axis] // dp
        return lax.dynamic_slice_in_dim(total, my_dp * part, part, axis=axis)

    proj_bias_out = own(bias_all[0:2], 1)
    fc2_bias_out = own(bias_all[2:4], 1)
    fc1_bias_out = own(unit_all[qv_size:unit_size].reshape(2, -1), 1)
    qv_bias_out = own(unit_all[:qv_size].reshape(qv_biases.shape), 2)
    ada_bias_out = own(jnp.stack([jnp.sum(m.astype(F32), axis=0) for m in mod_all]), 1)
    ada_out = jnp.stack([dot(silu_mine, mod_all[s], TN) for s in range(2)])

    return (
        outputs[0],
        outputs[1],
        ada_out,
        ada_bias_out,
        qkv_out,
        qv_bias_out,
        proj_out,
        proj_bias_out,
        fc1_out,
        fc1_bias_out,
        fc2_out,
        fc2_bias_out,
        input_grads[0],
        input_grads[1],
        cond_out,
    )


def solution(mesh):
    tokens = P("dp", "mp", None)
    weights = (
        P(None, ("mp", "dp"), None),
        P(None, "dp"),
        P(None, None, "dp", "mp"),
        P(None, None, ("mp", "dp")),
        P(None, "mp", "dp"),
        P(None, "dp"),
        P(None, "dp", "mp"),
        P(None, ("mp", "dp")),
        P(None, "mp", "dp"),
        P(None, "dp"),
    )
    return jax.shard_map(
        functools.partial(body, mesh.shape["mp"], mesh.shape["dp"]),
        mesh=mesh,
        in_specs=(tokens, tokens, P("dp", "mp"), P("dp", None)) + weights + (tokens, tokens),
        out_specs=(tokens, tokens) + weights + (tokens, tokens, P("dp", "mp")),
        check_vma=False,
    )
```

time: 980 us -> 900 us (0.918)
  Pallas kernels: 52 us -> 380 us
  matrix products: 217 us -> 6.27 us
  other arithmetic: 195 us -> 28.1 us
  local copies, waits for them, and re-layouts: 120 us -> 89.5 us
  waiting for transfers between devices: 270 us -> 287 us
  starting transfers between devices: 97.8 us -> 82 us
    pallas_call x4 -> x63, Pallas kernels: 52 us -> 380 us  [the longest x16 145 us: matmul(): pl.pallas_call(kernel, grid=(columns // tile,), in_specs=specs, out_specs...]
    dot_general x42 -> x6, matrix products: 217 us -> 6.27 us  [dot(): lax.dot_general(left, right, (dims, ((), ())), preferred_element_type=F32)]
    convert_element_type x51 -> x2, other arithmetic: 69.4 us -> 2.39 us  [the longest x1 1.57 us: body(): qkv_low = qkv_weight.astype(BF16).reshape(2, 3, share_rows, -1, lanes)]
    add x28 -> x1, other arithmetic: 32.4 us -> 0.1 us  [body(): modulation = (sum_mp(modulation) + ada_biases).reshape(seqs, 2, 6, width)]
    another operation x25 -> x12, other arithmetic: 36.6 us -> 5.02 us  [the longest x1 2.04 us: body(): ada_out = jnp.stack([dot(silu_mine, mod_all[s], TN) for s in range(2)])]
    reduce_sum x24 -> x5, other arithmetic: 34.7 us -> 3.21 us  [the longest x1 1.67 us: body(): bias_all = jnp.sum(gathered[:, 12:token_rows].astype(F32), axis=0)]
    unnamed x450 -> x309, local copies, waits for them, and re-layouts: 37.8 us -> 63.5 us
    ppermute x87 -> x69, waiting for transfers between devices: 242 us -> 265 us  [the longest x42 155 us: advance(): lax.ppermute(total[s][0], 'dp', self.hops[s])]
  transfers between devices with their start and end apart: 100 -> 82, of which waited for: 44 -> 49; matrix products, arithmetic and copies ran while one was open for 50% -> 5% of each run, Pallas kernels for 5% -> 32%
where the time goes in v2:
time: 900 us; the launch traced here: 889 us
  Pallas kernels  380 us (42%)
  waiting for transfers between devices  287 us (32%)
  local copies, waits for them, and re-layouts  89.5 us (10%)
  starting transfers between devices  82 us (9%)
  other arithmetic  28.1 us (3%)
  between operations  15.8 us (2%)
    ppermute x42, waiting for transfers between devices, advance(): lax.ppermute(total[s][0], 'dp', self.hops[s])  155 us
    pallas_call x16, Pallas kernels, matmul(): pl.pallas_call(kernel, grid=(columns // tile,), in_specs=specs, out_specs...  145 us
    pallas_call x8, Pallas kernels, weight_grad(): pl.pallas_call(kernel, grid_spec=pltpu.PrefetchScalarGridSpec(num_scalar_...  75.2 us
    pallas_call x24, Pallas kernels, add(): pl.pallas_call(kernel, grid_spec=pltpu.PrefetchScalarGridSpec(num_scalar_...  67.5 us
    unnamed x309, local copies, waits for them, and re-layouts  63.5 us
    ppermute x8, waiting for transfers between devices, share(): return whole(flat(rows)) + whole(flat(lax.ppermute(rows, 'mp', swap)))  57.2 us
    ppermute x42, starting transfers between devices, advance(): lax.ppermute(total[s][0], 'dp', self.hops[s])  44.5 us
    pallas_call x10, Pallas kernels, stage(): pl.pallas_call(kernel, grid_spec=pltpu.PrefetchScalarGridSpec(num_scalar_...  39.1 us
  transfers between devices with their start and end apart: 82, of which 49 were waited for; matrix products, arithmetic and copies ran while one was open for 5% of the time, Pallas kernels for 32%

profile of v2, /device:TPU:0, one launch (start us, length us, event | category | flops | bytes accessed | tf_op | source)
XLA Modules:
  0.0 889.3 jit_solution(10338016256170580031)
XLA Ops:
  18.9 4.1 collective-permute-start
  54.8 5.9 collective-permute-done.6.refs_2_
  64.5 5.3 collective-permute-done.8.refs_2_
  74.9 5.4 collective-permute-done.10.refs_2_
  84.7 5.0 collective-permute-done.12.refs_2_
  94.2 5.3 collective-permute-done.14.refs_2_
  102.5 5.6 collective-permute-done.16.refs_2_
  111.3 4.8 collective-permute-done.18.refs_2_
  123.5 6.1 collective-permute-done.20
  138.1 31.8 %collective-permute-done.22 = bf16[3,64,1536]{2,1,0:T(8,128)(2,1)S(1)} collective-permute-done((bf16[3,64,1536]{2,1,0:T(8,128)(2,1)S(1)}, bf16[3,64,1536]{2,1,0:T(8,128)(2,1)S(1)}, u32[]{:S(2)}, u32[]{:S(2)}) %collective-permute-start.22) | collective-permute-done | bytes 589856 | tf_op jit(solution)/shard_map/ppermute | solution.py:545
  175.4 7.4 qkv.3
  183.6 10.7 %qkv.2 = bf16[768,2304]{1,0:T(8,128)(2,1)S(1)} custom-call(bf16[384,1536]{1,0:T(8,128)(2,1)S(1)} %bitcast.191, bf16[384,1536]{1,0:T(8,128)(2,1)S(1)} %bitcast.193, bf16[2,1536,3072]{2,1,0:T(8,128)(2,1)} %all-gather.5.cloned.1.call-done.refs_2_, f32[2,1,2304]{2,1,0:T(1,128)S(1)} %reshape.400.refs_3_), custom_call_target="tpu_custom_call" | custom-call | flops 1024 | bytes 1024 | tf_op jit(solution)/shard_map/qkv/pallas_call | solution.py:350
  196.1 20.9 %attention_forward.1 = (bf16[2,3,128,768]{3,2,1,0:T(8,128)(2,1)S(1)}, bf16[2,3,64,768]{3,2,1,0:T(8,128)(2,1)S(1)}) custom-call(bf16[2,3,128,2304]{3,2,1,0:T(8,128)(2,1)} %bitcast.164, bf16[2,3,64,2304]{3,2,1,0:T(8,128)(2,1)S(1)} %bitcast.173), custom_call_target="tpu_custom_call" | custom-call | flops 1024 | bytes 1024 | tf_op jit(solution)/shard_map/attention_forward/pallas_call | solution.py:105
  217.0 5.5 proj.2
  225.3 4.5 proj.3
  232.3 20.8 %collective-permute-done.25.came = bf16[3,128,1536]{2,1,0:T(8,128)(2,1)} collective-permute-done((bf16[3,128,1536]{2,1,0:T(8,128)(2,1)}, bf16[3,128,1536]{2,1,0:T(8,128)(2,1)}, u32[]{:S(2)}, u32[]{:S(2)}) %collective-permute-start.25) | collective-permute-done | bytes 1179680 | tf_op jit(solution)/shard_map/ppermute | solution.py:564
  253.2 5.5 middle.2
  261.4 4.4 collective-permute-done.27.came
  275.7 14.0 %collective-permute-done.28 = bf16[3,64,1536]{2,1,0:T(8,128)(2,1)S(1)} collective-permute-done((bf16[3,64,1536]{2,1,0:T(8,128)(2,1)S(1)}, bf16[3,64,1536]{2,1,0:T(8,128)(2,1)S(1)}, u32[]{:S(2)}, u32[]{:S(2)}) %collective-permute-start.28) | collective-permute-done | bytes 589856 | tf_op jit(solution)/shard_map/ppermute | solution.py:545
  293.4 10.9 %up.3 = (bf16[384,3072]{1,0:T(8,128)(2,1)S(1)}, f32[384,3072]{1,0:T(8,128)}) custom-call(bf16[192,1536]{1,0:T(8,128)(2,1)S(1)} %bitcast.211, bf16[192,1536]{1,0:T(8,128)(2,1)S(1)} %bitcast.213, bf16[2,1536,3072]{2,1,0:T(8,128)(2,1)} %all-gather.9.cloned.1.call-done.refs_2_, f32[2,1,3072]{2,1,0:T(1,128)S(1)} %copy-done.79), custom_call_target="tpu_custom_call" | custom-call | flops 1024 | bytes 1024 | tf_op jit(solution)/shard_map/up/pallas_call | solution.py:350
  304.3 9.1 %weight_grad.9 = (bf16[8,96,3072]{2,1,0:T(8,128)(2,1)}, bf16[8,96,3072]{2,1,0:T(8,128)(2,1)}) custom-call(s32[1]{0:T(128)} %bitcast.32.core_ref, bf16[192,1536]{1,0:T(8,128)(2,1)} %bitcast.35.refs_0_, bf16[192,1536]{1,0:T(8,128)(2,1)} %bitcast.36.refs_1_, bf16[384,3072]{1,0:T(8,128)(2,1)S(1)} %get-tuple-element.485.refs_2_.refs_3_.refs_0_.refs_1_, ...), custom_call_target="tpu_custom_call" | custom-call | flops 1024 | bytes 1024 | tf_op jit(solution)/shard_map/weight_grad/pallas_call | solution.py:303
  313.3 17.0 %up.2 = (bf16[768,3072]{1,0:T(8,128)(2,1)}, f32[768,3072]{1,0:T(8,128)}) custom-call(bf16[384,1536]{1,0:T(8,128)(2,1)} %bitcast.41.refs_0_, bf16[384,1536]{1,0:T(8,128)(2,1)} %bitcast.42.refs_1_, bf16[2,1536,3072]{2,1,0:T(8,128)(2,1)} %all-gather.9.cloned.1.call-done.refs_2_, f32[2,1,3072]{2,1,0:T(1,128)S(1)} %copy-done.80), custom_call_target="tpu_custom_call" | custom-call | flops 1024 | bytes 1024 | tf_op jit(solution)/shard_map/up/pallas_call | solution.py:350
  330.4 16.1 %weight_grad.8 = (bf16[8,96,3072]{2,1,0:T(8,128)(2,1)}, bf16[8,96,3072]{2,1,0:T(8,128)(2,1)}) custom-call(s32[1]{0:T(128)} %bitcast.32.core_ref, bf16[384,1536]{1,0:T(8,128)(2,1)} %bitcast.33.refs_0_, bf16[384,1536]{1,0:T(8,128)(2,1)} %bitcast.34.refs_1_, bf16[768,3072]{1,0:T(8,128)(2,1)} %get-tuple-element.482.refs_2_.refs_3_.refs_0_.refs_1_, ...), custom_call_target="tpu_custom_call" | custom-call | flops 1024 | bytes 1024 | tf_op jit(solution)/shard_map/weight_grad/pallas_call | solution.py:303
  346.4 13.9 %down_back.2 = (bf16[768,3072]{1,0:T(8,128)(2,1)}, f32[1,3072]{1,0:T(1,128)S(1)}) custom-call(bf16[384,1536]{1,0:T(8,128)(2,1)} %bitcast.33.refs_0_, bf16[384,1536]{1,0:T(8,128)(2,1)} %bitcast.34.refs_1_, bf16[2,1536,3072]{2,1,0:T(8,128)(2,1)} %all-gather.7.cloned.1.call-done.refs_2_, f32[768,3072]{1,0:T(8,128)} %get-tuple-element.413.refs_3_), custom_call_target="tpu_custom_call" | custom-call | flops 1024 | bytes 1024 | tf_op jit(solution)/shard_map/down_back/pallas_call | solution.py:350
  360.3 11.4 %up_back.2 = (f32[384,1536]{1,0:T(8,128)S(1)}, bf16[384,1536]{1,0:T(8,128)(2,1)S(1)}) custom-call(bf16[768,3072]{1,0:T(8,128)(2,1)} %get-tuple-element.423.refs_0_.refs_1_.refs_2_.refs_3_, bf16[768,3072]{1,0:T(8,128)(2,1)} %get-tuple-element.423.refs_0_.refs_1_.refs_2_.refs_3_, bf16[2,1536,3072]{2,1,0:T(8,128)(2,1)} %all-gather.9.cloned.1.call-done.refs_2_), custom_call_target="tpu_custom_call" | custom-call | flops 1024 | bytes 1024 | tf_op jit(solution)/shard_map/up_back/pallas_call | solution.py:350
  374.8 8.9 down_back.3
  384.3 8.7 up_back.3
  393.5 15.5 %weight_grad.10 = (bf16[8,96,3072]{2,1,0:T(8,128)(2,1)}, bf16[8,96,3072]{2,1,0:T(8,128)(2,1)}) custom-call(s32[1]{0:T(128)} %bitcast.32.core_ref, bf16[384,1536]{1,0:T(8,128)(2,1)} %bitcast.41.refs_0_, bf16[384,1536]{1,0:T(8,128)(2,1)} %bitcast.42.refs_1_, bf16[768,3072]{1,0:T(8,128)(2,1)} %get-tuple-element.423.refs_0_.refs_1_.refs_2_.refs_3_, ...), custom_call_target="tpu_custom_call" | custom-call | flops 1024 | bytes 1024 | tf_op jit(solution)/shard_map/weight_grad/pallas_call | solution.py:303
  409.5 8.2 weight_grad.11
  418.3 13.6 %collective-permute-done.34.refs_7_.refs_8_ = bf16[8,96,3072]{2,1,0:T(8,128)(2,1)S(1)} collective-permute-done((bf16[8,96,3072]{2,1,0:T(8,128)(2,1)}, bf16[8,96,3072]{2,1,0:T(8,128)(2,1)S(1)}, u32[]{:S(2)}, u32[]{:S(2)}) %collective-permute-start.34) | collective-permute-done | bytes 4718624 | tf_op jit(solution)/shard_map/ppermute | solution.py:430
  434.1 4.9 ring_add.32
  445.8 5.5 middle_back.2
  454.0 13.1 %collective-permute-done.37.refs_4_ = bf16[96,6144]{1,0:T(8,128)(2,1)S(1)} collective-permute-done((bf16[96,6144]{1,0:T(8,128)(2,1)}, bf16[96,6144]{1,0:T(8,128)(2,1)S(1)}, u32[]{:S(2)}, u32[]{:S(2)}) %collective-permute-start.37) | collective-permute-done | bytes 1179680 | tf_op jit(solution)/shard_map/ppermute | solution.py:497
  471.7 4.1 ring_add.33
  479.4 12.1 %down.2 = (f32[384,1536]{1,0:T(8,128)S(1)}, bf16[384,1536]{1,0:T(8,128)(2,1)}) custom-call(bf16[768,3072]{1,0:T(8,128)(2,1)} %get-tuple-element.482.refs_2_.refs_3_.refs_0_.refs_1_, bf16[768,3072]{1,0:T(8,128)(2,1)} %get-tuple-element.482.refs_2_.refs_3_.refs_0_.refs_1_, bf16[2,1536,3072]{2,1,0:T(8,128)(2,1)} %all-gather.7.cloned.1.call-done.refs_2_), custom_call_target="tpu_custom_call" | custom-call | flops 1024 | bytes 1024 | tf_op jit(solution)/shard_map/down/pallas_call | solution.py:350
  491.5 10.1 %down.3 = (f32[192,1536]{1,0:T(8,128)S(1)}, bf16[192,1536]{1,0:T(8,128)(2,1)}) custom-call(bf16[384,3072]{1,0:T(8,128)(2,1)S(1)} %get-tuple-element.485.refs_2_.refs_3_.refs_0_.refs_1_, bf16[384,3072]{1,0:T(8,128)(2,1)S(1)} %get-tuple-element.485.refs_2_.refs_3_.refs_0_.refs_1_, bf16[2,1536,3072]{2,1,0:T(8,128)(2,1)} %all-gather.7.cloned.1.call-done.refs_2_), custom_call_target="tpu_custom_call" | custom-call | flops 1024 | bytes 1024 | tf_op jit(solution)/shard_map/down/pallas_call | solution.py:350
  503.2 4.1 ring_add.34
  511.0 11.3 %collective-permute-done.36 = bf16[3,64,1536]{2,1,0:T(8,128)(2,1)S(1)} collective-permute-done((bf16[3,64,1536]{2,1,0:T(8,128)(2,1)S(1)}, bf16[3,64,1536]{2,1,0:T(8,128)(2,1)S(1)}, u32[]{:S(2)}, u32[]{:S(2)}) %collective-permute-start.36) | collective-permute-done | bytes 589856 | tf_op jit(solution)/shard_map/ppermute | solution.py:545
  525.3 4.2 proj_back.2
  533.8 4.1 ring_add.35
  542.0 4.5 weight_grad.12
  550.8 10.6 %attention_backward.3 = (bf16[2,3,128,2304]{3,2,1,0:T(8,128)(2,1)}, bf16[2,3,64,2304]{3,2,1,0:T(8,128)(2,1)S(1)}) custom-call(bf16[2,3,128,2304]{3,2,1,0:T(8,128)(2,1)} %bitcast.165, bf16[2,3,64,2304]{3,2,1,0:T(8,128)(2,1)S(1)} %bitcast.174, bf16[2,3,128,768]{3,2,1,0:T(8,128)(2,1)S(1)} %bitcast.177, bf16[2,3,64,768]{3,2,1,0:T(8,128)(2,1)S(1)} %bitcast.184), custom_call_target="tpu_custom_call" | custom-call | flops 1024 | bytes 1024 | tf_op jit(solution)/shard_map/attention_backward/pallas_call | solution.py:129
  565.3 5.2 ring_add.36
  572.4 10.8 %attention_backward.4 = (bf16[2,3,128,2304]{3,2,1,0:T(8,128)(2,1)}, bf16[2,3,64,2304]{3,2,1,0:T(8,128)(2,1)S(1)}) custom-call(bf16[2,3,128,2304]{3,2,1,0:T(8,128)(2,1)} %bitcast.166, bf16[2,3,64,2304]{3,2,1,0:T(8,128)(2,1)S(1)} %bitcast.175, bf16[2,3,128,768]{3,2,1,0:T(8,128)(2,1)S(1)} %bitcast.178, ...), custom_call_target="tpu_custom_call", output_to_operand_aliasing={{0}: (4, {}), {1}: (5, {})} | custom-call | flops 1024 | bytes 1024 | tf_op jit(solution)/shard_map/attention_backward/pallas_call | solution.py:129
  583.3 10.9 %attention_backward.5 = (bf16[2,3,128,2304]{3,2,1,0:T(8,128)(2,1)}, bf16[2,3,64,2304]{3,2,1,0:T(8,128)(2,1)S(1)}) custom-call(bf16[2,3,128,2304]{3,2,1,0:T(8,128)(2,1)} %bitcast.167, bf16[2,3,64,2304]{3,2,1,0:T(8,128)(2,1)S(1)} %bitcast.176, bf16[2,3,128,768]{3,2,1,0:T(8,128)(2,1)S(1)} %bitcast.179, ...), custom_call_target="tpu_custom_call", output_to_operand_aliasing={{0}: (4, {}), {1}: (5, {})} | custom-call | flops 1024 | bytes 1024 | tf_op jit(solution)/shard_map/attention_backward/pallas_call | solution.py:129
  594.1 4.9 collective-permute-done.49.refs_4_
  599.3 4.1 ring_add.37
  603.4 9.9 %qkv_back.2 = (f32[384,1536]{1,0:T(8,128)S(1)}, bf16[384,1536]{1,0:T(8,128)(2,1)S(1)}) custom-call(bf16[768,2304]{1,0:T(8,128)(2,1)} %bitcast.241, bf16[768,2304]{1,0:T(8,128)(2,1)} %bitcast.242, bf16[2,1536,3072]{2,1,0:T(8,128)(2,1)} %all-gather.5.cloned.1.call-done.refs_2_), custom_call_target="tpu_custom_call" | custom-call | flops 1024 | bytes 1024 | tf_op jit(solution)/shard_map/qkv_back/pallas_call | solution.py:350
  615.7 7.0 qkv_back.3
  624.6 12.1 %weight_grad.14 = (bf16[8,96,2304]{2,1,0:T(8,128)(2,1)S(1)}, bf16[8,96,2304]{2,1,0:T(8,128)(2,1)}) custom-call(s32[1]{0:T(128)} %bitcast.32.core_ref, bf16[384,1536]{1,0:T(8,128)(2,1)S(1)} %bitcast.192, bf16[384,1536]{1,0:T(8,128)(2,1)S(1)} %bitcast.194, bf16[768,2304]{1,0:T(8,128)(2,1)} %bitcast.243, bf16[768,2304]{1,0:T(8,128)(2,1)} %bitcast.244), custom_call_target="tpu_custom_call" | custom-call | flops 1024 | bytes 1024 | tf_op jit(solution)/shard_map/weight_grad/pallas_call | solution.py:303
  638.4 6.5 weight_grad.15
  674.0 4.7 leave.2
  678.9 4.9 ring_add.39
  688.3 4.4 enter_back.3
  692.7 5.6 enter_back.2
  700.4 4.4 collective-permute-done.57
  709.8 54.3 %collective-permute-done.58.refs_4_ = bf16[96,3072]{1,0:T(8,128)(2,1)S(1)} collective-permute-done((bf16[96,3072]{1,0:T(8,128)(2,1)}, bf16[96,3072]{1,0:T(8,128)(2,1)S(1)}, u32[]{:S(2)}, u32[]{:S(2)}) %collective-permute-start.58) | collective-permute-done | bytes 589856 | tf_op jit(solution)/shard_map/ppermute | solution.py:497
  773.8 4.3 ring_add.41
  778.1 4.0 collective-permute-done.62.refs_4_
  789.3 7.6 collective-permute-done.64.refs_4_
  804.3 6.3 collective-permute-done.66.refs_4_
  812.4 4.1 ring_add.44
  818.4 8.7 collective-permute-done.68.refs_4_
  853.5 6.7 collective-permute-done.73
  (607 shorter events, 287.7 us)
Async XLA Ops:
  7.2 167.1 %all-gather.5.cloned.1.call-start = ((), (), s32[]{:S(2)}) async-start(), calls=%async_computation | async-start | bytes 20054016 | tf_op jit(solution)/shard_map/all_gather | solution.py:610
  13.1 262.6 %all-gather.9.cloned.1.call-start = ((), (), s32[]{:S(2)}) async-start(), calls=%async_computation.2 | async-start | bytes 20054016 | tf_op jit(solution)/shard_map/all_gather | solution.py:614
  15.3 331.2 %all-gather.7.cloned.1.call-start = ((), (), s32[]{:S(2)}) async-start(), calls=%async_computation.1 | async-start | bytes 20054016 | tf_op jit(solution)/shard_map/all_gather | solution.py:615
  18.2 808.9 %all-gather.11.cloned.1.call-start = ((), (), s32[]{:S(2)}) async-start(), calls=%async_computation.3 | async-start | bytes 3760128 | tf_op jit(solution)/shard_map/all_gather | solution.py:864
  52.4 8.3 collective-permute-start.6
  53.4 8.0 collective-permute-start.7
  62.0 7.8 collective-permute-start.8
  64.5 7.7 collective-permute-start.9
  72.8 7.5 collective-permute-start.10
  100.4 7.7 collective-permute-start.16
  100.7 7.7 collective-permute-start.17
  121.0 8.5 collective-permute-start.20
  132.5 37.4 %collective-permute-start.21 = (bf16[3,128,1536]{2,1,0:T(8,128)(2,1)S(1)}, bf16[3,128,1536]{2,1,0:T(8,128)(2,1)S(1)}, u32[]{:S(2)}, u32[]{:S(2)}) collective-permute-start(bf16[3,128,1536]{2,1,0:T(8,128)(2,1)S(1)} %get-tuple-element.382), channel_id=1, source_target_pairs={{0,1},{1,0},{2,3},{3,2},{4,5},{5,4},{6,7},{7,6},{8,9},{9,8},{10,11... | collective-permute-start | bytes 3538952 | tf_op jit(solution)/shard_map/ppermute | solution.py:545
  136.5 33.5 %collective-permute-start.22 = (bf16[3,64,1536]{2,1,0:T(8,128)(2,1)S(1)}, bf16[3,64,1536]{2,1,0:T(8,128)(2,1)S(1)}, u32[]{:S(2)}, u32[]{:S(2)}) collective-permute-start(bf16[3,64,1536]{2,1,0:T(8,128)(2,1)S(1)} %get-tuple-element.383), channel_id=1, source_target_pairs={{0,1},{1,0},{2,3},{3,2},{4,5},{5,4},{6,7},{7,6},{8,9},{9,8},{10,11... | collective-permute-start | bytes 1769480 | tf_op jit(solution)/shard_map/ppermute | solution.py:545
  171.0 46.1 %collective-permute-start.23 = (bf16[3,128,1536]{2,1,0:T(8,128)(2,1)}, bf16[3,128,1536]{2,1,0:T(8,128)(2,1)}, u32[]{:S(2)}, u32[]{:S(2)}) collective-permute-start(bf16[3,128,1536]{2,1,0:T(8,128)(2,1)} %get-tuple-element.390), channel_id=1, source_target_pairs={{0,1},{1,0},{2,3},{3,2},{4,5},{5,4},{6,7},{7,6},{8,9},{9,8},{10,11... | collective-permute-start | bytes 3538952 | tf_op jit(solution)/shard_map/ppermute | solution.py:545
  172.2 44.8 %collective-permute-start.24 = (bf16[3,64,1536]{2,1,0:T(8,128)(2,1)}, bf16[3,64,1536]{2,1,0:T(8,128)(2,1)}, u32[]{:S(2)}, u32[]{:S(2)}) collective-permute-start(bf16[3,64,1536]{2,1,0:T(8,128)(2,1)} %get-tuple-element.391), channel_id=1, source_target_pairs={{0,1},{1,0},{2,3},{3,2},{4,5},{5,4},{6,7},{7,6},{8,9},{9,8},{10,11... | collective-permute-start | bytes 1769480 | tf_op jit(solution)/shard_map/ppermute | solution.py:545
  223.9 29.2 %collective-permute-start.25 = (bf16[3,128,1536]{2,1,0:T(8,128)(2,1)}, bf16[3,128,1536]{2,1,0:T(8,128)(2,1)}, u32[]{:S(2)}, u32[]{:S(2)}) collective-permute-start(bf16[3,128,1536]{2,1,0:T(8,128)(2,1)} %bitcast.39), channel_id=1, source_target_pairs={{0,1},{1,0},{2,3},{3,2},{4,5},{5,4},{6,7},{7,6},{8,9},{9,8},{10,11... | collective-permute-start | bytes 3538952 | tf_op jit(solution)/shard_map/ppermute | solution.py:564
  230.8 35.0 %collective-permute-start.27 = (bf16[3,64,1536]{2,1,0:T(8,128)(2,1)}, bf16[3,64,1536]{2,1,0:T(8,128)(2,1)}, u32[]{:S(2)}, u32[]{:S(2)}) collective-permute-start(bf16[3,64,1536]{2,1,0:T(8,128)(2,1)} %bitcast.47), channel_id=1, source_target_pairs={{0,1},{1,0},{2,3},{3,2},{4,5},{5,4},{6,7},{7,6},{8,9},{9,8},{10,11... | collective-permute-start | bytes 1769480 | tf_op jit(solution)/shard_map/ppermute | solution.py:564
  260.1 53.3 %collective-permute-start.26 = (bf16[3,128,1536]{2,1,0:T(8,128)(2,1)}, bf16[3,128,1536]{2,1,0:T(8,128)(2,1)}, u32[]{:S(2)}, u32[]{:S(2)}) collective-permute-start(bf16[3,128,1536]{2,1,0:T(8,128)(2,1)} %get-tuple-element.395), channel_id=1, source_target_pairs={{0,1},{1,0},{2,3},{3,2},{4,5},{5,4},{6,7},{7,6},{8,9},{9,8},{10,11... | collective-permute-start | bytes 3538952 | tf_op jit(solution)/shard_map/ppermute | solution.py:545
  272.2 17.4 %collective-permute-start.28 = (bf16[3,64,1536]{2,1,0:T(8,128)(2,1)S(1)}, bf16[3,64,1536]{2,1,0:T(8,128)(2,1)S(1)}, u32[]{:S(2)}, u32[]{:S(2)}) collective-permute-start(bf16[3,64,1536]{2,1,0:T(8,128)(2,1)S(1)} %get-tuple-element.407), channel_id=1, source_target_pairs={{0,1},{1,0},{2,3},{3,2},{4,5},{5,4},{6,7},{7,6},{8,9},{9,8},{10,11... | collective-permute-start | bytes 1769480 | tf_op jit(solution)/shard_map/ppermute | solution.py:545
  373.2 36.3 %collective-permute-start.29 = (bf16[3,128,1536]{2,1,0:T(8,128)(2,1)S(1)}, bf16[3,128,1536]{2,1,0:T(8,128)(2,1)S(1)}, u32[]{:S(2)}, u32[]{:S(2)}) collective-permute-start(bf16[3,128,1536]{2,1,0:T(8,128)(2,1)S(1)} %bitcast.238), channel_id=1, source_target_pairs={{0,1},{1,0},{2,3},{3,2},{4,5},{5,4},{6,7},{7,6},{8,9},{9,8},{10,11... | collective-permute-start | bytes 3538952 | tf_op jit(solution)/shard_map/ppermute | solution.py:564
  392.9 24.8 %collective-permute-start.30 = (bf16[3,64,1536]{2,1,0:T(8,128)(2,1)S(1)}, bf16[3,64,1536]{2,1,0:T(8,128)(2,1)S(1)}, u32[]{:S(2)}, u32[]{:S(2)}) collective-permute-start(bf16[3,64,1536]{2,1,0:T(8,128)(2,1)S(1)} %bitcast.240), channel_id=1, source_target_pairs={{0,1},{1,0},{2,3},{3,2},{4,5},{5,4},{6,7},{7,6},{8,9},{9,8},{10,11... | collective-permute-start | bytes 1769480 | tf_op jit(solution)/shard_map/ppermute | solution.py:564
  393.5 24.8 %collective-permute-start.33 = (bf16[8,96,3072]{2,1,0:T(8,128)(2,1)}, bf16[8,96,3072]{2,1,0:T(8,128)(2,1)}, u32[]{:S(2)}, u32[]{:S(2)}) collective-permute-start(bf16[8,96,3072]{2,1,0:T(8,128)(2,1)} %get-tuple-element.440), channel_id=1, source_target_pairs={{0,2},{2,0},{4,6},{6,4},{8,10},{10,8},{12,14},{14,12},{16,18},{18,... | collective-permute-start | bytes 14155784 | tf_op jit(solution)/shard_map/ppermute | solution.py:430
  409.0 9.3 %collective-permute-start.31 = (bf16[8,96,3072]{2,1,0:T(8,128)(2,1)}, bf16[8,96,3072]{2,1,0:T(8,128)(2,1)}, u32[]{:S(2)}, u32[]{:S(2)}) collective-permute-start(bf16[8,96,3072]{2,1,0:T(8,128)(2,1)} %get-tuple-element.438), channel_id=1, source_target_pairs={{0,2},{2,0},{4,6},{6,4},{8,10},{10,8},{12,14},{14,12},{16,18},{18,... | collective-permute-start | bytes 14155784 | tf_op jit(solution)/shard_map/ppermute | solution.py:430
  417.7 14.1 %collective-permute-start.34 = (bf16[8,96,3072]{2,1,0:T(8,128)(2,1)}, bf16[8,96,3072]{2,1,0:T(8,128)(2,1)S(1)}, u32[]{:S(2)}, u32[]{:S(2)}) collective-permute-start(bf16[8,96,3072]{2,1,0:T(8,128)(2,1)} %get-tuple-element.441), channel_id=1, source_target_pairs={{0,2},{2,0},{4,6},{6,4},{8,10},{10,8},{12,14},{14,12},{16,18},{18,... | collective-permute-start | bytes 14155784 | tf_op jit(solution)/shard_map/ppermute | solution.py:430
  417.8 16.2 %collective-permute-start.32 = (bf16[8,96,3072]{2,1,0:T(8,128)(2,1)}, bf16[8,96,3072]{2,1,0:T(8,128)(2,1)}, u32[]{:S(2)}, u32[]{:S(2)}) collective-permute-start(bf16[8,96,3072]{2,1,0:T(8,128)(2,1)} %get-tuple-element.439), channel_id=1, source_target_pairs={{0,2},{2,0},{4,6},{6,4},{8,10},{10,8},{12,14},{14,12},{16,18},{18,... | collective-permute-start | bytes 14155784 | tf_op jit(solution)/shard_map/ppermute | solution.py:430
  438.9 28.2 %collective-permute-start.37 = (bf16[96,6144]{1,0:T(8,128)(2,1)}, bf16[96,6144]{1,0:T(8,128)(2,1)S(1)}, u32[]{:S(2)}, u32[]{:S(2)}) collective-permute-start(bf16[96,6144]{1,0:T(8,128)(2,1)} %get-tuple-element.454), channel_id=1, source_target_pairs={{0,8},{2,10},{8,16},{10,18},{16,24},{18,26},{24,28},{26,30},{28,20... | collective-permute-start | bytes 3538952 | tf_op jit(solution)/shard_map/ppermute | solution.py:497
  439.1 29.1 %collective-permute-start.38 = (bf16[96,6144]{1,0:T(8,128)(2,1)S(1)}, bf16[96,6144]{1,0:T(8,128)(2,1)S(1)}, u32[]{:S(2)}, u32[]{:S(2)}) collective-permute-start(bf16[96,6144]{1,0:T(8,128)(2,1)S(1)} %get-tuple-element.455), channel_id=1, source_target_pairs={{0,4},{2,6},{8,0},{10,2},{16,8},{18,10},{24,16},{26,18},{28,24},{3... | collective-permute-start | bytes 3538952 | tf_op jit(solution)/shard_map/ppermute | solution.py:497
  475.8 27.2 %collective-permute-start.39 = (bf16[96,6144]{1,0:T(8,128)(2,1)S(1)}, bf16[96,6144]{1,0:T(8,128)(2,1)S(1)}, u32[]{:S(2)}, u32[]{:S(2)}) collective-permute-start(bf16[96,6144]{1,0:T(8,128)(2,1)S(1)} %get-tuple-element.480), channel_id=1, source_target_pairs={{0,8},{2,10},{8,16},{10,18},{16,24},{18,26},{24,28},{26,30},{28,20... | collective-permute-start | bytes 3538952 | tf_op jit(solution)/shard_map/ppermute | solution.py:497
  476.1 27.1 %collective-permute-start.40 = (bf16[96,6144]{1,0:T(8,128)(2,1)S(1)}, bf16[96,6144]{1,0:T(8,128)(2,1)S(1)}, u32[]{:S(2)}, u32[]{:S(2)}) collective-permute-start(bf16[96,6144]{1,0:T(8,128)(2,1)S(1)} %get-tuple-element.481), channel_id=1, source_target_pairs={{0,4},{2,6},{8,0},{10,2},{16,8},{18,10},{24,16},{26,18},{28,24},{3... | collective-permute-start | bytes 3538952 | tf_op jit(solution)/shard_map/ppermute | solution.py:497
  477.9 44.5 %collective-permute-start.35 = (bf16[3,128,1536]{2,1,0:T(8,128)(2,1)S(1)}, bf16[3,128,1536]{2,1,0:T(8,128)(2,1)S(1)}, u32[]{:S(2)}, u32[]{:S(2)}) collective-permute-start(bf16[3,128,1536]{2,1,0:T(8,128)(2,1)S(1)} %get-tuple-element.472), channel_id=1, source_target_pairs={{0,1},{1,0},{2,3},{3,2},{4,5},{5,4},{6,7},{7,6},{8,9},{9,8},{10,11... | collective-permute-start | bytes 3538952 | tf_op jit(solution)/shard_map/ppermute | solution.py:545
  507.3 26.2 %collective-permute-start.41 = (bf16[96,6144]{1,0:T(8,128)(2,1)S(1)}, bf16[96,6144]{1,0:T(8,128)(2,1)S(1)}, u32[]{:S(2)}, u32[]{:S(2)}) collective-permute-start(bf16[96,6144]{1,0:T(8,128)(2,1)S(1)} %get-tuple-element.498), channel_id=1, source_target_pairs={{0,8},{2,10},{8,16},{10,18},{16,24},{18,26},{24,28},{26,30},{28,20... | collective-permute-start | bytes 3538952 | tf_op jit(solution)/shard_map/ppermute | solution.py:497
  507.8 26.0 %collective-permute-start.42 = (bf16[96,6144]{1,0:T(8,128)(2,1)S(1)}, bf16[96,6144]{1,0:T(8,128)(2,1)S(1)}, u32[]{:S(2)}, u32[]{:S(2)}) collective-permute-start(bf16[96,6144]{1,0:T(8,128)(2,1)S(1)} %get-tuple-element.499), channel_id=1, source_target_pairs={{0,4},{2,6},{8,0},{10,2},{16,8},{18,10},{24,16},{26,18},{28,24},{3... | collective-permute-start | bytes 3538952 | tf_op jit(solution)/shard_map/ppermute | solution.py:497
  509.4 13.0 %collective-permute-start.36 = (bf16[3,64,1536]{2,1,0:T(8,128)(2,1)S(1)}, bf16[3,64,1536]{2,1,0:T(8,128)(2,1)S(1)}, u32[]{:S(2)}, u32[]{:S(2)}) collective-permute-start(bf16[3,64,1536]{2,1,0:T(8,128)(2,1)S(1)} %get-tuple-element.473), channel_id=1, source_target_pairs={{0,1},{1,0},{2,3},{3,2},{4,5},{5,4},{6,7},{7,6},{8,9},{9,8},{10,11... | collective-permute-start | bytes 1769480 | tf_op jit(solution)/shard_map/ppermute | solution.py:545
  537.9 25.1 %collective-permute-start.43 = (bf16[96,6144]{1,0:T(8,128)(2,1)S(1)}, bf16[96,6144]{1,0:T(8,128)(2,1)S(1)}, u32[]{:S(2)}, u32[]{:S(2)}) collective-permute-start(bf16[96,6144]{1,0:T(8,128)(2,1)S(1)} %get-tuple-element.514), channel_id=1, source_target_pairs={{0,8},{2,10},{8,16},{10,18},{16,24},{18,26},{24,28},{26,30},{28,20... | collective-permute-start | bytes 3538952 | tf_op jit(solution)/shard_map/ppermute | solution.py:497
  538.9 25.1 %collective-permute-start.44 = (bf16[96,6144]{1,0:T(8,128)(2,1)S(1)}, bf16[96,6144]{1,0:T(8,128)(2,1)}, u32[]{:S(2)}, u32[]{:S(2)}) collective-permute-start(bf16[96,6144]{1,0:T(8,128)(2,1)S(1)} %get-tuple-element.515), channel_id=1, source_target_pairs={{0,4},{2,6},{8,0},{10,2},{16,8},{18,10},{24,16},{26,18},{28,24},{3... | collective-permute-start | bytes 3538952 | tf_op jit(solution)/shard_map/ppermute | solution.py:497
  539.9 31.8 %collective-permute-start.48 = (bf16[3,64,1536]{2,1,0:T(8,128)(2,1)}, bf16[3,64,1536]{2,1,0:T(8,128)(2,1)S(1)}, u32[]{:S(2)}, u32[]{:S(2)}) collective-permute-start(bf16[3,64,1536]{2,1,0:T(8,128)(2,1)} %bitcast.61), channel_id=1, source_target_pairs={{0,1},{1,0},{2,3},{3,2},{4,5},{5,4},{6,7},{7,6},{8,9},{9,8},{10,11... | collective-permute-start | bytes 1769480 | tf_op jit(solution)/shard_map/ppermute | solution.py:564
  541.8 41.4 %collective-permute-start.47 = (bf16[3,128,1536]{2,1,0:T(8,128)(2,1)}, bf16[3,128,1536]{2,1,0:T(8,128)(2,1)}, u32[]{:S(2)}, u32[]{:S(2)}) collective-permute-start(bf16[3,128,1536]{2,1,0:T(8,128)(2,1)} %bitcast.59), channel_id=1, source_target_pairs={{0,1},{1,0},{2,3},{3,2},{4,5},{5,4},{6,7},{7,6},{8,9},{9,8},{10,11... | collective-permute-start | bytes 3538952 | tf_op jit(solution)/shard_map/ppermute | solution.py:564
  550.8 32.4 %collective-permute-start.46 = (bf16[8,96,768]{2,1,0:T(8,128)(2,1)}, bf16[8,96,768]{2,1,0:T(8,128)(2,1)S(1)}, u32[]{:S(2)}, u32[]{:S(2)}) collective-permute-start(bf16[8,96,768]{2,1,0:T(8,128)(2,1)} %get-tuple-element.546), channel_id=1, source_target_pairs={{0,2},{2,0},{4,6},{6,4},{8,10},{10,8},{12,14},{14,12},{16,18},{18,... | collective-permute-start | bytes 3538952 | tf_op jit(solution)/shard_map/ppermute | solution.py:430
  564.0 19.3 %collective-permute-start.45 = (bf16[8,96,768]{2,1,0:T(8,128)(2,1)}, bf16[8,96,768]{2,1,0:T(8,128)(2,1)S(1)}, u32[]{:S(2)}, u32[]{:S(2)}) collective-permute-start(bf16[8,96,768]{2,1,0:T(8,128)(2,1)} %get-tuple-element.545), channel_id=1, source_target_pairs={{0,2},{2,0},{4,6},{6,4},{8,10},{10,8},{12,14},{14,12},{16,18},{18,... | collective-permute-start | bytes 3538952 | tf_op jit(solution)/shard_map/ppermute | solution.py:430
  570.4 28.6 %collective-permute-start.49 = (bf16[96,6144]{1,0:T(8,128)(2,1)}, bf16[96,6144]{1,0:T(8,128)(2,1)S(1)}, u32[]{:S(2)}, u32[]{:S(2)}) collective-permute-start(bf16[96,6144]{1,0:T(8,128)(2,1)} %get-tuple-element.537), channel_id=1, source_target_pairs={{0,8},{2,10},{8,16},{10,18},{16,24},{18,26},{24,28},{26,30},{28,20... | collective-permute-start | bytes 3538952 | tf_op jit(solution)/shard_map/ppermute | solution.py:497
  571.8 27.5 %collective-permute-start.50 = (bf16[96,6144]{1,0:T(8,128)(2,1)S(1)}, bf16[96,6144]{1,0:T(8,128)(2,1)S(1)}, u32[]{:S(2)}, u32[]{:S(2)}) collective-permute-start(bf16[96,6144]{1,0:T(8,128)(2,1)S(1)} %get-tuple-element.538), channel_id=1, source_target_pairs={{0,4},{2,6},{8,0},{10,2},{16,8},{18,10},{24,16},{26,18},{28,24},{3... | collective-permute-start | bytes 3538952 | tf_op jit(solution)/shard_map/ppermute | solution.py:497
  645.0 11.6 %collective-permute-start.51 = (bf16[8,96,2304]{2,1,0:T(8,128)(2,1)}, bf16[8,96,2304]{2,1,0:T(8,128)(2,1)}, u32[]{:S(2)}, u32[]{:S(2)}) collective-permute-start(bf16[8,96,2304]{2,1,0:T(8,128)(2,1)} %get-tuple-element.586), channel_id=1, source_target_pairs={{0,2},{2,0},{4,6},{6,4},{8,10},{10,8},{12,14},{14,12},{16,18},{18,... | collective-permute-start | bytes 10616840 | tf_op jit(solution)/shard_map/ppermute | solution.py:430
  645.7 33.1 %collective-permute-start.55 = (bf16[96,6144]{1,0:T(8,128)(2,1)}, bf16[96,6144]{1,0:T(8,128)(2,1)}, u32[]{:S(2)}, u32[]{:S(2)}) collective-permute-start(bf16[96,6144]{1,0:T(8,128)(2,1)} %copy-done.121), channel_id=1, source_target_pairs={{0,8},{2,10},{8,16},{10,18},{16,24},{18,26},{24,28},{26,30},{28,20... | collective-permute-start | bytes 3538952 | tf_op jit(solution)/shard_map/ppermute | solution.py:497
  647.4 31.4 %collective-permute-start.56 = (bf16[96,6144]{1,0:T(8,128)(2,1)}, bf16[96,6144]{1,0:T(8,128)(2,1)}, u32[]{:S(2)}, u32[]{:S(2)}) collective-permute-start(bf16[96,6144]{1,0:T(8,128)(2,1)} %copy-done.120), channel_id=1, source_target_pairs={{0,4},{2,6},{8,0},{10,2},{16,8},{18,10},{24,16},{26,18},{28,24},{3... | collective-permute-start | bytes 3538952 | tf_op jit(solution)/shard_map/ppermute | solution.py:497
  647.7 38.1 %collective-permute-start.54 = (bf16[3,64,1536]{2,1,0:T(8,128)(2,1)}, bf16[3,64,1536]{2,1,0:T(8,128)(2,1)}, u32[]{:S(2)}, u32[]{:S(2)}) collective-permute-start(bf16[3,64,1536]{2,1,0:T(8,128)(2,1)} %bitcast.239), channel_id=1, source_target_pairs={{0,1},{1,0},{2,3},{3,2},{4,5},{5,4},{6,7},{7,6},{8,9},{9,8},{10,11... | collective-permute-start | bytes 1769480 | tf_op jit(solution)/shard_map/ppermute | solution.py:564
  651.5 36.7 %collective-permute-start.53 = (bf16[3,128,1536]{2,1,0:T(8,128)(2,1)}, bf16[3,128,1536]{2,1,0:T(8,128)(2,1)}, u32[]{:S(2)}, u32[]{:S(2)}) collective-permute-start(bf16[3,128,1536]{2,1,0:T(8,128)(2,1)} %bitcast.237), channel_id=1, source_target_pairs={{0,1},{1,0},{2,3},{3,2},{4,5},{5,4},{6,7},{7,6},{8,9},{9,8},{10,11... | collective-permute-start | bytes 3538952 | tf_op jit(solution)/shard_map/ppermute | solution.py:564
  705.7 67.1 %collective-permute-start.60 = (bf16[96,6144]{1,0:T(8,128)(2,1)}, bf16[96,6144]{1,0:T(8,128)(2,1)S(1)}, u32[]{:S(2)}, u32[]{:S(2)}) collective-permute-start(bf16[96,6144]{1,0:T(8,128)(2,1)} %copy-done.123), channel_id=1, source_target_pairs={{0,8},{2,10},{8,16},{10,18},{16,24},{18,26},{24,28},{26,30},{28,20... | collective-permute-start | bytes 3538952 | tf_op jit(solution)/shard_map/ppermute | solution.py:497
  707.0 65.8 %collective-permute-start.61 = (bf16[96,6144]{1,0:T(8,128)(2,1)}, bf16[96,6144]{1,0:T(8,128)(2,1)S(1)}, u32[]{:S(2)}, u32[]{:S(2)}) collective-permute-start(bf16[96,6144]{1,0:T(8,128)(2,1)} %copy-done.122), channel_id=1, source_target_pairs={{0,4},{2,6},{8,0},{10,2},{16,8},{18,10},{24,16},{26,18},{28,24},{3... | collective-permute-start | bytes 3538952 | tf_op jit(solution)/shard_map/ppermute | solution.py:497
  707.8 56.3 %collective-permute-start.58 = (bf16[96,3072]{1,0:T(8,128)(2,1)}, bf16[96,3072]{1,0:T(8,128)(2,1)S(1)}, u32[]{:S(2)}, u32[]{:S(2)}) collective-permute-start(bf16[96,3072]{1,0:T(8,128)(2,1)} %copy-done.126), channel_id=1, source_target_pairs={{0,8},{2,10},{8,16},{10,18},{16,24},{18,26},{24,28},{26,30},{28,20... | collective-permute-start | bytes 1769480 | tf_op jit(solution)/shard_map/ppermute | solution.py:497
  709.0 57.2 %collective-permute-start.59 = (bf16[96,3072]{1,0:T(8,128)(2,1)S(1)}, bf16[96,3072]{1,0:T(8,128)(2,1)S(1)}, u32[]{:S(2)}, u32[]{:S(2)}) collective-permute-start(bf16[96,3072]{1,0:T(8,128)(2,1)S(1)} %copy-done.125), channel_id=1, source_target_pairs={{0,4},{2,6},{8,0},{10,2},{16,8},{18,10},{24,16},{26,18},{28,24},{3... | collective-permute-start | bytes 1769480 | tf_op jit(solution)/shard_map/ppermute | solution.py:497
  770.7 11.5 %collective-permute-start.62 = (bf16[96,3072]{1,0:T(8,128)(2,1)S(1)}, bf16[96,3072]{1,0:T(8,128)(2,1)S(1)}, u32[]{:S(2)}, u32[]{:S(2)}) collective-permute-start(bf16[96,3072]{1,0:T(8,128)(2,1)S(1)} %get-tuple-element.657), channel_id=1, source_target_pairs={{0,8},{2,10},{8,16},{10,18},{16,24},{18,26},{24,28},{26,30},{28,20... | collective-permute-start | bytes 1769480 | tf_op jit(solution)/shard_map/ppermute | solution.py:497
  772.5 9.9 %collective-permute-start.63 = (bf16[96,3072]{1,0:T(8,128)(2,1)S(1)}, bf16[96,3072]{1,0:T(8,128)(2,1)S(1)}, u32[]{:S(2)}, u32[]{:S(2)}) collective-permute-start(bf16[96,3072]{1,0:T(8,128)(2,1)S(1)} %get-tuple-element.658), channel_id=1, source_target_pairs={{0,4},{2,6},{8,0},{10,2},{16,8},{18,10},{24,16},{26,18},{28,24},{3... | collective-permute-start | bytes 1769480 | tf_op jit(solution)/shard_map/ppermute | solution.py:497
  785.6 11.3 %collective-permute-start.64 = (bf16[96,3072]{1,0:T(8,128)(2,1)S(1)}, bf16[96,3072]{1,0:T(8,128)(2,1)S(1)}, u32[]{:S(2)}, u32[]{:S(2)}) collective-permute-start(bf16[96,3072]{1,0:T(8,128)(2,1)S(1)} %get-tuple-element.673), channel_id=1, source_target_pairs={{0,8},{2,10},{8,16},{10,18},{16,24},{18,26},{24,28},{26,30},{28,20... | collective-permute-start | bytes 1769480 | tf_op jit(solution)/shard_map/ppermute | solution.py:497
  787.1 10.2 %collective-permute-start.65 = (bf16[96,3072]{1,0:T(8,128)(2,1)S(1)}, bf16[96,3072]{1,0:T(8,128)(2,1)S(1)}, u32[]{:S(2)}, u32[]{:S(2)}) collective-permute-start(bf16[96,3072]{1,0:T(8,128)(2,1)S(1)} %get-tuple-element.674), channel_id=1, source_target_pairs={{0,4},{2,6},{8,0},{10,2},{16,8},{18,10},{24,16},{26,18},{28,24},{3... | collective-permute-start | bytes 1769480 | tf_op jit(solution)/shard_map/ppermute | solution.py:497
  800.6 10.1 %collective-permute-start.66 = (bf16[96,3072]{1,0:T(8,128)(2,1)S(1)}, bf16[96,3072]{1,0:T(8,128)(2,1)S(1)}, u32[]{:S(2)}, u32[]{:S(2)}) collective-permute-start(bf16[96,3072]{1,0:T(8,128)(2,1)S(1)} %get-tuple-element.677), channel_id=1, source_target_pairs={{0,8},{2,10},{8,16},{10,18},{16,24},{18,26},{24,28},{26,30},{28,20... | collective-permute-start | bytes 1769480 | tf_op jit(solution)/shard_map/ppermute | solution.py:497
  802.4 10.0 %collective-permute-start.67 = (bf16[96,3072]{1,0:T(8,128)(2,1)S(1)}, bf16[96,3072]{1,0:T(8,128)(2,1)S(1)}, u32[]{:S(2)}, u32[]{:S(2)}) collective-permute-start(bf16[96,3072]{1,0:T(8,128)(2,1)S(1)} %get-tuple-element.678), channel_id=1, source_target_pairs={{0,4},{2,6},{8,0},{10,2},{16,8},{18,10},{24,16},{26,18},{28,24},{3... | collective-permute-start | bytes 1769480 | tf_op jit(solution)/shard_map/ppermute | solution.py:497
  816.4 10.7 %collective-permute-start.68 = (bf16[96,3072]{1,0:T(8,128)(2,1)}, bf16[96,3072]{1,0:T(8,128)(2,1)S(1)}, u32[]{:S(2)}, u32[]{:S(2)}) collective-permute-start(bf16[96,3072]{1,0:T(8,128)(2,1)} %get-tuple-element.681), channel_id=1, source_target_pairs={{0,8},{2,10},{8,16},{10,18},{16,24},{18,26},{24,28},{26,30},{28,20... | collective-permute-start | bytes 1769480 | tf_op jit(solution)/shard_map/ppermute | solution.py:497
  816.9 10.2 %collective-permute-start.69 = (bf16[96,3072]{1,0:T(8,128)(2,1)}, bf16[96,3072]{1,0:T(8,128)(2,1)S(1)}, u32[]{:S(2)}, u32[]{:S(2)}) collective-permute-start(bf16[96,3072]{1,0:T(8,128)(2,1)} %get-tuple-element.682), channel_id=1, source_target_pairs={{0,4},{2,6},{8,0},{10,2},{16,8},{18,10},{24,16},{26,18},{28,24},{3... | collective-permute-start | bytes 1769480 | tf_op jit(solution)/shard_map/ppermute | solution.py:497
  831.9 13.2 %collective-permute-start.71 = (bf16[96,3072]{1,0:T(8,128)(2,1)S(1)}, bf16[96,3072]{1,0:T(8,128)(2,1)S(1)}, u32[]{:S(2)}, u32[]{:S(2)}) collective-permute-start(bf16[96,3072]{1,0:T(8,128)(2,1)S(1)} %get-tuple-element.686), channel_id=1, source_target_pairs={{0,8},{2,10},{8,16},{10,18},{16,24},{18,26},{24,28},{26,30},{28,20... | collective-permute-start | bytes 1769480 | tf_op jit(solution)/shard_map/ppermute | solution.py:497
  832.4 12.7 %collective-permute-start.72 = (bf16[96,3072]{1,0:T(8,128)(2,1)S(1)}, bf16[96,3072]{1,0:T(8,128)(2,1)S(1)}, u32[]{:S(2)}, u32[]{:S(2)}) collective-permute-start(bf16[96,3072]{1,0:T(8,128)(2,1)S(1)} %get-tuple-element.687), channel_id=1, source_target_pairs={{0,4},{2,6},{8,0},{10,2},{16,8},{18,10},{24,16},{26,18},{28,24},{3... | collective-permute-start | bytes 1769480 | tf_op jit(solution)/shard_map/ppermute | solution.py:497
  848.3 12.6 %collective-permute-start.74 = (bf16[96,3072]{1,0:T(8,128)(2,1)S(1)}, bf16[96,3072]{1,0:T(8,128)(2,1)S(1)}, u32[]{:S(2)}, u32[]{:S(2)}) collective-permute-start(bf16[96,3072]{1,0:T(8,128)(2,1)S(1)} %get-tuple-element.692), channel_id=1, source_target_pairs={{0,8},{2,10},{8,16},{10,18},{16,24},{18,26},{24,28},{26,30},{28,20... | collective-permute-start | bytes 1769480 | tf_op jit(solution)/shard_map/ppermute | solution.py:497
  850.0 10.9 %collective-permute-start.75 = (bf16[96,3072]{1,0:T(8,128)(2,1)S(1)}, bf16[96,3072]{1,0:T(8,128)(2,1)S(1)}, u32[]{:S(2)}, u32[]{:S(2)}) collective-permute-start(bf16[96,3072]{1,0:T(8,128)(2,1)S(1)} %get-tuple-element.693), channel_id=1, source_target_pairs={{0,4},{2,6},{8,0},{10,2},{16,8},{18,10},{24,16},{26,18},{28,24},{3... | collective-permute-start | bytes 1769480 | tf_op jit(solution)/shard_map/ppermute | solution.py:497
  851.2 9.0 %collective-permute-start.73 = (f32[96,48]{0,1:T(8,128)S(1)}, f32[96,48]{0,1:T(8,128)S(1)}, u32[]{:S(2)}, u32[]{:S(2)}) collective-permute-start(f32[96,48]{0,1:T(8,128)S(1)} %pad_maximum_fusion.11), channel_id=1, source_target_pairs={{0,8},{2,10},{4,12},{6,14},{8,0},{10,2},{12,4},{14,6},{16,24},{18,... | collective-permute-start | bytes 55304 | tf_op jit(solution)/shard_map/ppermute | solution.py:579
  (167 other events, 1401.4 us)
Sparse Core Ops, SparseCore 0:
  13.2 119.0 all-gather.4
  133.9 99.1 all-gather.8
  234.7 98.9 all-gather.6
  705.8 59.0 all-gather.10

commit v3 on v2

--- a/solution.py
+++ b/solution.py
@@ -433,7 +433,7 @@
         last = self.step == self.chips - 1
         widths = [view.shape[-1] for view in self.views[0]]
         rows = self.views[0][0].shape[1]
-        tile = rows // 3 if rows % 48 == 0 else rows
+        tile = rows // 2 if rows % 32 == 0 else rows
         at = jnp.stack([self.targets[s][self.step] for s in range(2)])
         operands, specs, places = [], [], []
         for s in range(2):
@@ -800,6 +800,7 @@
         back[s] = collect(grad_qkv[s], attention_full, s, 0, qkv_size, "qkv_back")
         back[s], grad_qkv = tie(back[s], grad_qkv)
         back[s] = exchange(back[s])
+    grad_qkv = beat(grad_qkv, rings)
     for s in range(2):
         keep, gift = weight_grad(joint_in[s], split(grad_qkv[s]), core, dp)
         keep, gift, grad_qkv = tie(keep, gift, grad_qkv)
@@ -825,6 +826,7 @@
     unit_size = unit_sums.size
     unit_sums = jnp.pad(unit_sums, (0, -unit_size % (seqs * width))).reshape(seqs, -1, width)
     unit_rows = unit_sums.shape[1]
+    gate_two, unit_sums = beat((gate_two, unit_sums), last_rings)
     gate_two, unit_sums = beat((gate_two, unit_sums), rings)
     back, gate_two, unit_sums = tie(back, gate_two, unit_sums)
 
@@ -851,7 +853,7 @@
     token_rows = len(picks)
     picks += [(len(packed_sums), row) for row in range(unit_rows)]
     sums = pack(packed_sums + [unit_sums], picks, "pack")
-    sums, input_grads = tie(sums, input_grads)
+    sums, input_grads = beat((sums, input_grads), last_rings)
     if mp == 2:
         other = lax.ppermute(sums, "mp", swap)
         row_of = lax.broadcasted_iota(jnp.int32, sums.shape, 1)
@@ -868,9 +870,8 @@
     input_grads = beat(input_grads, last_rings)
     fc2_out, fc1_out = (jnp.stack([part[n] for part in rings.finish()]) for n in range(2))
     fc2_out = jnp.swapaxes(fc2_out, 1, 2)
-    fc1_out = beat(fc1_out, last_rings)
-    fc2_out = beat(fc2_out, last_rings)
-    gathered = beat(gathered, last_rings)
+    fc1_out, fc2_out = beat((fc1_out, fc2_out), last_rings)
+    gathered, unused = tie(gathered, last_rings.sent)
 
     mod_all = [gathered[:, 6 * s : 6 * s + 6].reshape(dp * seqs, 6 * width) for s in range(2)]
     silu_grad = sum(dot(mod_all[s], ada_low[s], NT) for s in range(2))

time: 900 us -> 886 us (0.984)
  Pallas kernels: 380 us -> 370 us
    pallas_call x24, Pallas kernels: 67.5 us -> 56.7 us  [add(): pl.pallas_call(kernel, grid_spec=pltpu.PrefetchScalarGridSpec(num_scalar_...]
    unnamed x309 -> x321, local copies, waits for them, and re-layouts: 63.5 us -> 63.6 us
  transfers between devices with their start and end apart: 82 -> 82, of which waited for: 49 -> 48; matrix products, arithmetic and copies ran while one was open for 5% -> 5% of each run, Pallas kernels for 32% -> 34%
where the time goes in v3:
time: 886 us; the launch traced here: 877 us
  Pallas kernels  370 us (42%)
  waiting for transfers between devices  287 us (32%)
  local copies, waits for them, and re-layouts  91.6 us (10%)
  starting transfers between devices  78.7 us (9%)
  other arithmetic  28.1 us (3%)
  between operations  16.1 us (2%)
    ppermute x42, waiting for transfers between devices, advance(): lax.ppermute(total[s][0], 'dp', self.hops[s])  154 us
    pallas_call x16, Pallas kernels, matmul(): pl.pallas_call(kernel, grid=(columns // tile,), in_specs=specs, out_specs...  145 us
    pallas_call x8, Pallas kernels, weight_grad(): pl.pallas_call(kernel, grid_spec=pltpu.PrefetchScalarGridSpec(num_scalar_...  75.1 us
    unnamed x321, local copies, waits for them, and re-layouts  63.6 us
    ppermute x8, waiting for transfers between devices, share(): return whole(flat(rows)) + whole(flat(lax.ppermute(rows, 'mp', swap)))  56.7 us
    pallas_call x24, Pallas kernels, add(): pl.pallas_call(kernel, grid_spec=pltpu.PrefetchScalarGridSpec(num_scalar_...  56.7 us
    ppermute x42, starting transfers between devices, advance(): lax.ppermute(total[s][0], 'dp', self.hops[s])  44.4 us
    pallas_call x10, Pallas kernels, stage(): pl.pallas_call(kernel, grid_spec=pltpu.PrefetchScalarGridSpec(num_scalar_...  40 us
  transfers between devices with their start and end apart: 82, of which 48 were waited for; matrix products, arithmetic and copies ran while one was open for 5% of the time, Pallas kernels for 34%

profile of v3, /device:TPU:0, one launch (start us, length us, event | category | flops | bytes accessed | tf_op | source)
XLA Modules:
  0.0 877.3 jit_solution(3609670233356429099)
XLA Ops:
  18.9 4.1 collective-permute-start
  54.8 5.9 collective-permute-done.6.refs_2_
  64.6 5.3 collective-permute-done.8.refs_2_
  75.0 5.4 collective-permute-done.10.refs_2_
  84.7 5.0 collective-permute-done.12.refs_2_
  94.2 5.3 collective-permute-done.14.refs_2_
  102.6 5.6 collective-permute-done.16.refs_2_
  111.3 4.8 collective-permute-done.18.refs_2_
  123.7 6.0 collective-permute-done.20
  138.3 31.8 %collective-permute-done.22 = bf16[3,64,1536]{2,1,0:T(8,128)(2,1)S(1)} collective-permute-done((bf16[3,64,1536]{2,1,0:T(8,128)(2,1)S(1)}, bf16[3,64,1536]{2,1,0:T(8,128)(2,1)S(1)}, u32[]{:S(2)}, u32[]{:S(2)}) %collective-permute-start.22) | collective-permute-done | bytes 589856 | tf_op jit(solution)/shard_map/ppermute | solution.py:545
  175.5 7.4 qkv.3
  183.7 10.6 %qkv.2 = bf16[768,2304]{1,0:T(8,128)(2,1)S(1)} custom-call(bf16[384,1536]{1,0:T(8,128)(2,1)S(1)} %bitcast.191, bf16[384,1536]{1,0:T(8,128)(2,1)S(1)} %bitcast.193, bf16[2,1536,3072]{2,1,0:T(8,128)(2,1)} %all-gather.5.cloned.1.call-done.refs_2_, f32[2,1,2304]{2,1,0:T(1,128)S(1)} %reshape.400.refs_3_), custom_call_target="tpu_custom_call" | custom-call | flops 1024 | bytes 1024 | tf_op jit(solution)/shard_map/qkv/pallas_call | solution.py:350
  196.2 20.9 %attention_forward.1 = (bf16[2,3,128,768]{3,2,1,0:T(8,128)(2,1)S(1)}, bf16[2,3,64,768]{3,2,1,0:T(8,128)(2,1)S(1)}) custom-call(bf16[2,3,128,2304]{3,2,1,0:T(8,128)(2,1)} %bitcast.164, bf16[2,3,64,2304]{3,2,1,0:T(8,128)(2,1)S(1)} %bitcast.173), custom_call_target="tpu_custom_call" | custom-call | flops 1024 | bytes 1024 | tf_op jit(solution)/shard_map/attention_forward/pallas_call | solution.py:105
  217.1 5.5 proj.2
  225.6 4.5 proj.3
  232.4 20.8 %collective-permute-done.25.came = bf16[3,128,1536]{2,1,0:T(8,128)(2,1)} collective-permute-done((bf16[3,128,1536]{2,1,0:T(8,128)(2,1)}, bf16[3,128,1536]{2,1,0:T(8,128)(2,1)}, u32[]{:S(2)}, u32[]{:S(2)}) %collective-permute-start.25) | collective-permute-done | bytes 1179680 | tf_op jit(solution)/shard_map/ppermute | solution.py:564
  253.2 5.5 middle.2
  261.7 4.2 collective-permute-done.27.came
  276.1 13.6 %collective-permute-done.28 = bf16[3,64,1536]{2,1,0:T(8,128)(2,1)S(1)} collective-permute-done((bf16[3,64,1536]{2,1,0:T(8,128)(2,1)S(1)}, bf16[3,64,1536]{2,1,0:T(8,128)(2,1)S(1)}, u32[]{:S(2)}, u32[]{:S(2)}) %collective-permute-start.28) | collective-permute-done | bytes 589856 | tf_op jit(solution)/shard_map/ppermute | solution.py:545
  293.3 10.9 %up.3 = (bf16[384,3072]{1,0:T(8,128)(2,1)S(1)}, f32[384,3072]{1,0:T(8,128)}) custom-call(bf16[192,1536]{1,0:T(8,128)(2,1)S(1)} %bitcast.211, bf16[192,1536]{1,0:T(8,128)(2,1)S(1)} %bitcast.213, bf16[2,1536,3072]{2,1,0:T(8,128)(2,1)} %all-gather.9.cloned.1.call-done.refs_2_, f32[2,1,3072]{2,1,0:T(1,128)S(1)} %copy-done.89), custom_call_target="tpu_custom_call" | custom-call | flops 1024 | bytes 1024 | tf_op jit(solution)/shard_map/up/pallas_call | solution.py:350
  304.2 9.0 %weight_grad.9 = (bf16[8,96,3072]{2,1,0:T(8,128)(2,1)}, bf16[8,96,3072]{2,1,0:T(8,128)(2,1)}) custom-call(s32[1]{0:T(128)} %bitcast.32.core_ref, bf16[192,1536]{1,0:T(8,128)(2,1)} %bitcast.35.refs_0_, bf16[192,1536]{1,0:T(8,128)(2,1)} %bitcast.36.refs_1_, bf16[384,3072]{1,0:T(8,128)(2,1)S(1)} %get-tuple-element.493.refs_2_.refs_3_.refs_0_.refs_1_, ...), custom_call_target="tpu_custom_call" | custom-call | flops 1024 | bytes 1024 | tf_op jit(solution)/shard_map/weight_grad/pallas_call | solution.py:303
  313.3 17.0 %up.2 = (bf16[768,3072]{1,0:T(8,128)(2,1)}, f32[768,3072]{1,0:T(8,128)}) custom-call(bf16[384,1536]{1,0:T(8,128)(2,1)} %bitcast.41.refs_0_, bf16[384,1536]{1,0:T(8,128)(2,1)} %bitcast.42.refs_1_, bf16[2,1536,3072]{2,1,0:T(8,128)(2,1)} %all-gather.9.cloned.1.call-done.refs_2_, f32[2,1,3072]{2,1,0:T(1,128)S(1)} %copy-done.90), custom_call_target="tpu_custom_call" | custom-call | flops 1024 | bytes 1024 | tf_op jit(solution)/shard_map/up/pallas_call | solution.py:350
  330.3 15.7 %weight_grad.8 = (bf16[8,96,3072]{2,1,0:T(8,128)(2,1)}, bf16[8,96,3072]{2,1,0:T(8,128)(2,1)}) custom-call(s32[1]{0:T(128)} %bitcast.32.core_ref, bf16[384,1536]{1,0:T(8,128)(2,1)} %bitcast.33.refs_0_, bf16[384,1536]{1,0:T(8,128)(2,1)} %bitcast.34.refs_1_, bf16[768,3072]{1,0:T(8,128)(2,1)} %get-tuple-element.490.refs_2_.refs_3_.refs_0_.refs_1_, ...), custom_call_target="tpu_custom_call" | custom-call | flops 1024 | bytes 1024 | tf_op jit(solution)/shard_map/weight_grad/pallas_call | solution.py:303
  346.1 13.9 %down_back.2 = (bf16[768,3072]{1,0:T(8,128)(2,1)}, f32[1,3072]{1,0:T(1,128)S(1)}) custom-call(bf16[384,1536]{1,0:T(8,128)(2,1)} %bitcast.33.refs_0_, bf16[384,1536]{1,0:T(8,128)(2,1)} %bitcast.34.refs_1_, bf16[2,1536,3072]{2,1,0:T(8,128)(2,1)} %all-gather.7.cloned.1.call-done.refs_2_, f32[768,3072]{1,0:T(8,128)} %get-tuple-element.421.refs_3_), custom_call_target="tpu_custom_call" | custom-call | flops 1024 | bytes 1024 | tf_op jit(solution)/shard_map/down_back/pallas_call | solution.py:350
  360.0 11.4 %up_back.2 = (f32[384,1536]{1,0:T(8,128)S(1)}, bf16[384,1536]{1,0:T(8,128)(2,1)S(1)}) custom-call(bf16[768,3072]{1,0:T(8,128)(2,1)} %get-tuple-element.431.refs_0_.refs_1_.refs_2_.refs_3_, bf16[768,3072]{1,0:T(8,128)(2,1)} %get-tuple-element.431.refs_0_.refs_1_.refs_2_.refs_3_, bf16[2,1536,3072]{2,1,0:T(8,128)(2,1)} %all-gather.9.cloned.1.call-done.refs_2_), custom_call_target="tpu_custom_call" | custom-call | flops 1024 | bytes 1024 | tf_op jit(solution)/shard_map/up_back/pallas_call | solution.py:350
  374.4 8.9 %down_back.3 = (bf16[384,3072]{1,0:T(8,128)(2,1)S(1)}, f32[1,3072]{1,0:T(1,128)S(1)}) custom-call(bf16[192,1536]{1,0:T(8,128)(2,1)} %bitcast.35.refs_0_, bf16[192,1536]{1,0:T(8,128)(2,1)} %bitcast.36.refs_1_, bf16[2,1536,3072]{2,1,0:T(8,128)(2,1)} %all-gather.7.cloned.1.call-done.refs_2_, f32[384,3072]{1,0:T(8,128)} %get-tuple-element.426.refs_3_), custom_call_target="tpu_custom_call" | custom-call | flops 1024 | bytes 1024 | tf_op jit(solution)/shard_map/down_back/pallas_call | solution.py:350
  383.9 8.7 up_back.3
  393.1 15.6 %weight_grad.10 = (bf16[8,96,3072]{2,1,0:T(8,128)(2,1)}, bf16[8,96,3072]{2,1,0:T(8,128)(2,1)}) custom-call(s32[1]{0:T(128)} %bitcast.32.core_ref, bf16[384,1536]{1,0:T(8,128)(2,1)} %bitcast.41.refs_0_, bf16[384,1536]{1,0:T(8,128)(2,1)} %bitcast.42.refs_1_, bf16[768,3072]{1,0:T(8,128)(2,1)} %get-tuple-element.431.refs_0_.refs_1_.refs_2_.refs_3_, ...), custom_call_target="tpu_custom_call" | custom-call | flops 1024 | bytes 1024 | tf_op jit(solution)/shard_map/weight_grad/pallas_call | solution.py:303
  409.2 8.2 weight_grad.11
  418.0 13.6 %collective-permute-done.34.refs_7_.refs_8_ = bf16[8,96,3072]{2,1,0:T(8,128)(2,1)S(1)} collective-permute-done((bf16[8,96,3072]{2,1,0:T(8,128)(2,1)}, bf16[8,96,3072]{2,1,0:T(8,128)(2,1)S(1)}, u32[]{:S(2)}, u32[]{:S(2)}) %collective-permute-start.34) | collective-permute-done | bytes 4718624 | tf_op jit(solution)/shard_map/ppermute | solution.py:430
  433.7 4.3 ring_add.32
  440.1 3.6 middle_back.3
  444.9 5.5 middle_back.2
  453.2 13.1 %collective-permute-done.37.refs_4_ = bf16[96,6144]{1,0:T(8,128)(2,1)S(1)} collective-permute-done((bf16[96,6144]{1,0:T(8,128)(2,1)}, bf16[96,6144]{1,0:T(8,128)(2,1)S(1)}, u32[]{:S(2)}, u32[]{:S(2)}) %collective-permute-start.37) | collective-permute-done | bytes 1179680 | tf_op jit(solution)/shard_map/ppermute | solution.py:497
  477.9 12.1 %down.2 = (f32[384,1536]{1,0:T(8,128)S(1)}, bf16[384,1536]{1,0:T(8,128)(2,1)}) custom-call(bf16[768,3072]{1,0:T(8,128)(2,1)} %get-tuple-element.490.refs_2_.refs_3_.refs_0_.refs_1_, bf16[768,3072]{1,0:T(8,128)(2,1)} %get-tuple-element.490.refs_2_.refs_3_.refs_0_.refs_1_, bf16[2,1536,3072]{2,1,0:T(8,128)(2,1)} %all-gather.7.cloned.1.call-done.refs_2_), custom_call_target="tpu_custom_call" | custom-call | flops 1024 | bytes 1024 | tf_op jit(solution)/shard_map/down/pallas_call | solution.py:350
  490.0 10.1 %down.3 = (f32[192,1536]{1,0:T(8,128)S(1)}, bf16[192,1536]{1,0:T(8,128)(2,1)}) custom-call(bf16[384,3072]{1,0:T(8,128)(2,1)S(1)} %get-tuple-element.493.refs_2_.refs_3_.refs_0_.refs_1_, bf16[384,3072]{1,0:T(8,128)(2,1)S(1)} %get-tuple-element.493.refs_2_.refs_3_.refs_0_.refs_1_, bf16[2,1536,3072]{2,1,0:T(8,128)(2,1)} %all-gather.7.cloned.1.call-done.refs_2_), custom_call_target="tpu_custom_call" | custom-call | flops 1024 | bytes 1024 | tf_op jit(solution)/shard_map/down/pallas_call | solution.py:350
  508.6 11.4 %collective-permute-done.36 = bf16[3,64,1536]{2,1,0:T(8,128)(2,1)S(1)} collective-permute-done((bf16[3,64,1536]{2,1,0:T(8,128)(2,1)S(1)}, bf16[3,64,1536]{2,1,0:T(8,128)(2,1)S(1)}, u32[]{:S(2)}, u32[]{:S(2)}) %collective-permute-start.36) | collective-permute-done | bytes 589856 | tf_op jit(solution)/shard_map/ppermute | solution.py:545
  522.9 4.2 proj_back.2
  527.1 4.1 collective-permute-done.41.refs_4_
  538.9 4.6 weight_grad.12
  547.9 10.6 %attention_backward.3 = (bf16[2,3,128,2304]{3,2,1,0:T(8,128)(2,1)}, bf16[2,3,64,2304]{3,2,1,0:T(8,128)(2,1)S(1)}) custom-call(bf16[2,3,128,2304]{3,2,1,0:T(8,128)(2,1)} %bitcast.165, bf16[2,3,64,2304]{3,2,1,0:T(8,128)(2,1)S(1)} %bitcast.174, bf16[2,3,128,768]{3,2,1,0:T(8,128)(2,1)S(1)} %bitcast.177, bf16[2,3,64,768]{3,2,1,0:T(8,128)(2,1)S(1)} %bitcast.184), custom_call_target="tpu_custom_call" | custom-call | flops 1024 | bytes 1024 | tf_op jit(solution)/shard_map/attention_backward/pallas_call | solution.py:129
  562.1 4.5 ring_add.36
  568.6 10.6 %attention_backward.4 = (bf16[2,3,128,2304]{3,2,1,0:T(8,128)(2,1)}, bf16[2,3,64,2304]{3,2,1,0:T(8,128)(2,1)S(1)}) custom-call(bf16[2,3,128,2304]{3,2,1,0:T(8,128)(2,1)} %bitcast.166, bf16[2,3,64,2304]{3,2,1,0:T(8,128)(2,1)S(1)} %bitcast.175, bf16[2,3,128,768]{3,2,1,0:T(8,128)(2,1)S(1)} %bitcast.178, ...), custom_call_target="tpu_custom_call", output_to_operand_aliasing={{0}: (4, {}), {1}: (5, {})} | custom-call | flops 1024 | bytes 1024 | tf_op jit(solution)/shard_map/attention_backward/pallas_call | solution.py:129
  579.2 10.9 %attention_backward.5 = (bf16[2,3,128,2304]{3,2,1,0:T(8,128)(2,1)}, bf16[2,3,64,2304]{3,2,1,0:T(8,128)(2,1)S(1)}) custom-call(bf16[2,3,128,2304]{3,2,1,0:T(8,128)(2,1)} %bitcast.167, bf16[2,3,64,2304]{3,2,1,0:T(8,128)(2,1)S(1)} %bitcast.176, bf16[2,3,128,768]{3,2,1,0:T(8,128)(2,1)S(1)} %bitcast.179, ...), custom_call_target="tpu_custom_call", output_to_operand_aliasing={{0}: (4, {}), {1}: (5, {})} | custom-call | flops 1024 | bytes 1024 | tf_op jit(solution)/shard_map/attention_backward/pallas_call | solution.py:129
  590.1 5.1 collective-permute-done.49.refs_4_
  595.8 3.4 ring_add.37
  601.3 9.2 %qkv_back.2 = (f32[384,1536]{1,0:T(8,128)S(1)}, bf16[384,1536]{1,0:T(8,128)(2,1)S(1)}) custom-call(bf16[768,2304]{1,0:T(8,128)(2,1)} %bitcast.241, bf16[768,2304]{1,0:T(8,128)(2,1)} %bitcast.242, bf16[2,1536,3072]{2,1,0:T(8,128)(2,1)} %all-gather.5.cloned.1.call-done.refs_2_), custom_call_target="tpu_custom_call" | custom-call | flops 1024 | bytes 1024 | tf_op jit(solution)/shard_map/qkv_back/pallas_call | solution.py:350
  611.9 7.2 qkv_back.3
  621.0 5.1 collective-permute-done.51.refs_4_
  632.5 12.1 %weight_grad.14 = (bf16[8,96,2304]{2,1,0:T(8,128)(2,1)S(1)}, bf16[8,96,2304]{2,1,0:T(8,128)(2,1)}) custom-call(s32[1]{0:T(128)} %bitcast.32.core_ref, bf16[384,1536]{1,0:T(8,128)(2,1)S(1)} %bitcast.192, bf16[384,1536]{1,0:T(8,128)(2,1)S(1)} %bitcast.194, bf16[768,2304]{1,0:T(8,128)(2,1)} %bitcast.243, bf16[768,2304]{1,0:T(8,128)(2,1)} %bitcast.244), custom_call_target="tpu_custom_call" | custom-call | flops 1024 | bytes 1024 | tf_op jit(solution)/shard_map/weight_grad/pallas_call | solution.py:303
  646.3 6.6 weight_grad.15
  659.4 5.1 collective-permute-done.53.refs_3_
  674.6 21.6 %collective-permute-done.57.refs_4_ = bf16[96,3072]{1,0:T(8,128)(2,1)} collective-permute-done((bf16[96,3072]{1,0:T(8,128)(2,1)}, bf16[96,3072]{1,0:T(8,128)(2,1)}, u32[]{:S(2)}, u32[]{:S(2)}) %collective-permute-start.57) | collective-permute-done | bytes 589856 | tf_op jit(solution)/shard_map/ppermute | solution.py:497
  703.5 4.7 leave.2
  714.5 4.1 ring_add.41
  720.6 5.2 enter_back.3
  725.9 5.6 enter_back.2
  736.7 4.2 collective-permute-done.63
  744.2 15.2 %collective-permute-done.64.refs_4_ = bf16[96,3072]{1,0:T(8,128)(2,1)S(1)} collective-permute-done((bf16[96,3072]{1,0:T(8,128)(2,1)}, bf16[96,3072]{1,0:T(8,128)(2,1)S(1)}, u32[]{:S(2)}, u32[]{:S(2)}) %collective-permute-start.64) | collective-permute-done | bytes 589856 | tf_op jit(solution)/shard_map/ppermute | solution.py:497
  768.2 19.8 %collective-permute-done.66.refs_4_ = bf16[96,3072]{1,0:T(8,128)(2,1)S(1)} collective-permute-done((bf16[96,3072]{1,0:T(8,128)(2,1)}, bf16[96,3072]{1,0:T(8,128)(2,1)S(1)}, u32[]{:S(2)}, u32[]{:S(2)}) %collective-permute-start.66) | collective-permute-done | bytes 589856 | tf_op jit(solution)/shard_map/ppermute | solution.py:497
  788.0 8.0 collective-permute-done.67.refs_9_
  806.0 9.8 %collective-permute-done.68.refs_4_ = bf16[96,3072]{1,0:T(8,128)(2,1)S(1)} collective-permute-done((bf16[96,3072]{1,0:T(8,128)(2,1)S(1)}, bf16[96,3072]{1,0:T(8,128)(2,1)S(1)}, u32[]{:S(2)}, u32[]{:S(2)}) %collective-permute-start.68) | collective-permute-done | bytes 589856 | tf_op jit(solution)/shard_map/ppermute | solution.py:497
  831.0 3.9 collective-permute-done.70
  841.3 6.7 collective-permute-done.73
  (619 shorter events, 284.1 us)
Async XLA Ops:
  7.2 167.2 %all-gather.5.cloned.1.call-start = ((), (), s32[]{:S(2)}) async-start(), calls=%async_computation | async-start | bytes 20054016 | tf_op jit(solution)/shard_map/all_gather | solution.py:610
  13.1 263.0 %all-gather.9.cloned.1.call-start = ((), (), s32[]{:S(2)}) async-start(), calls=%async_computation.2 | async-start | bytes 20054016 | tf_op jit(solution)/shard_map/all_gather | solution.py:614
  15.3 330.7 %all-gather.7.cloned.1.call-start = ((), (), s32[]{:S(2)}) async-start(), calls=%async_computation.1 | async-start | bytes 20054016 | tf_op jit(solution)/shard_map/all_gather | solution.py:615
  18.2 803.0 %all-gather.11.cloned.1.call-start = ((), (), s32[]{:S(2)}) async-start(), calls=%async_computation.3 | async-start | bytes 3760128 | tf_op jit(solution)/shard_map/all_gather | solution.py:866
  52.4 8.3 collective-permute-start.6
  53.5 8.0 collective-permute-start.7
  62.1 7.8 collective-permute-start.8
  64.5 7.7 collective-permute-start.9
  72.8 7.5 collective-permute-start.10
  100.4 7.7 collective-permute-start.16
  100.7 7.7 collective-permute-start.17
  121.1 8.6 collective-permute-start.20
  132.7 37.4 %collective-permute-start.21 = (bf16[3,128,1536]{2,1,0:T(8,128)(2,1)S(1)}, bf16[3,128,1536]{2,1,0:T(8,128)(2,1)S(1)}, u32[]{:S(2)}, u32[]{:S(2)}) collective-permute-start(bf16[3,128,1536]{2,1,0:T(8,128)(2,1)S(1)} %get-tuple-element.390), channel_id=1, source_target_pairs={{0,1},{1,0},{2,3},{3,2},{4,5},{5,4},{6,7},{7,6},{8,9},{9,8},{10,11... | collective-permute-start | bytes 3538952 | tf_op jit(solution)/shard_map/ppermute | solution.py:545
  136.9 33.2 %collective-permute-start.22 = (bf16[3,64,1536]{2,1,0:T(8,128)(2,1)S(1)}, bf16[3,64,1536]{2,1,0:T(8,128)(2,1)S(1)}, u32[]{:S(2)}, u32[]{:S(2)}) collective-permute-start(bf16[3,64,1536]{2,1,0:T(8,128)(2,1)S(1)} %get-tuple-element.391), channel_id=1, source_target_pairs={{0,1},{1,0},{2,3},{3,2},{4,5},{5,4},{6,7},{7,6},{8,9},{9,8},{10,11... | collective-permute-start | bytes 1769480 | tf_op jit(solution)/shard_map/ppermute | solution.py:545
  171.1 46.0 %collective-permute-start.23 = (bf16[3,128,1536]{2,1,0:T(8,128)(2,1)}, bf16[3,128,1536]{2,1,0:T(8,128)(2,1)}, u32[]{:S(2)}, u32[]{:S(2)}) collective-permute-start(bf16[3,128,1536]{2,1,0:T(8,128)(2,1)} %get-tuple-element.398), channel_id=1, source_target_pairs={{0,1},{1,0},{2,3},{3,2},{4,5},{5,4},{6,7},{7,6},{8,9},{9,8},{10,11... | collective-permute-start | bytes 3538952 | tf_op jit(solution)/shard_map/ppermute | solution.py:545
  172.6 44.5 %collective-permute-start.24 = (bf16[3,64,1536]{2,1,0:T(8,128)(2,1)}, bf16[3,64,1536]{2,1,0:T(8,128)(2,1)}, u32[]{:S(2)}, u32[]{:S(2)}) collective-permute-start(bf16[3,64,1536]{2,1,0:T(8,128)(2,1)} %get-tuple-element.399), channel_id=1, source_target_pairs={{0,1},{1,0},{2,3},{3,2},{4,5},{5,4},{6,7},{7,6},{8,9},{9,8},{10,11... | collective-permute-start | bytes 1769480 | tf_op jit(solution)/shard_map/ppermute | solution.py:545
  224.0 29.2 %collective-permute-start.25 = (bf16[3,128,1536]{2,1,0:T(8,128)(2,1)}, bf16[3,128,1536]{2,1,0:T(8,128)(2,1)}, u32[]{:S(2)}, u32[]{:S(2)}) collective-permute-start(bf16[3,128,1536]{2,1,0:T(8,128)(2,1)} %bitcast.39), channel_id=1, source_target_pairs={{0,1},{1,0},{2,3},{3,2},{4,5},{5,4},{6,7},{7,6},{8,9},{9,8},{10,11... | collective-permute-start | bytes 3538952 | tf_op jit(solution)/shard_map/ppermute | solution.py:564
  231.1 34.8 %collective-permute-start.27 = (bf16[3,64,1536]{2,1,0:T(8,128)(2,1)}, bf16[3,64,1536]{2,1,0:T(8,128)(2,1)}, u32[]{:S(2)}, u32[]{:S(2)}) collective-permute-start(bf16[3,64,1536]{2,1,0:T(8,128)(2,1)} %bitcast.47), channel_id=1, source_target_pairs={{0,1},{1,0},{2,3},{3,2},{4,5},{5,4},{6,7},{7,6},{8,9},{9,8},{10,11... | collective-permute-start | bytes 1769480 | tf_op jit(solution)/shard_map/ppermute | solution.py:564
  260.2 53.1 %collective-permute-start.26 = (bf16[3,128,1536]{2,1,0:T(8,128)(2,1)}, bf16[3,128,1536]{2,1,0:T(8,128)(2,1)}, u32[]{:S(2)}, u32[]{:S(2)}) collective-permute-start(bf16[3,128,1536]{2,1,0:T(8,128)(2,1)} %get-tuple-element.403), channel_id=1, source_target_pairs={{0,1},{1,0},{2,3},{3,2},{4,5},{5,4},{6,7},{7,6},{8,9},{9,8},{10,11... | collective-permute-start | bytes 3538952 | tf_op jit(solution)/shard_map/ppermute | solution.py:545
  272.3 17.3 %collective-permute-start.28 = (bf16[3,64,1536]{2,1,0:T(8,128)(2,1)S(1)}, bf16[3,64,1536]{2,1,0:T(8,128)(2,1)S(1)}, u32[]{:S(2)}, u32[]{:S(2)}) collective-permute-start(bf16[3,64,1536]{2,1,0:T(8,128)(2,1)S(1)} %get-tuple-element.415), channel_id=1, source_target_pairs={{0,1},{1,0},{2,3},{3,2},{4,5},{5,4},{6,7},{7,6},{8,9},{9,8},{10,11... | collective-permute-start | bytes 1769480 | tf_op jit(solution)/shard_map/ppermute | solution.py:545
  372.8 36.4 %collective-permute-start.29 = (bf16[3,128,1536]{2,1,0:T(8,128)(2,1)S(1)}, bf16[3,128,1536]{2,1,0:T(8,128)(2,1)S(1)}, u32[]{:S(2)}, u32[]{:S(2)}) collective-permute-start(bf16[3,128,1536]{2,1,0:T(8,128)(2,1)S(1)} %bitcast.238), channel_id=1, source_target_pairs={{0,1},{1,0},{2,3},{3,2},{4,5},{5,4},{6,7},{7,6},{8,9},{9,8},{10,11... | collective-permute-start | bytes 3538952 | tf_op jit(solution)/shard_map/ppermute | solution.py:564
  392.6 24.8 %collective-permute-start.30 = (bf16[3,64,1536]{2,1,0:T(8,128)(2,1)S(1)}, bf16[3,64,1536]{2,1,0:T(8,128)(2,1)S(1)}, u32[]{:S(2)}, u32[]{:S(2)}) collective-permute-start(bf16[3,64,1536]{2,1,0:T(8,128)(2,1)S(1)} %bitcast.240), channel_id=1, source_target_pairs={{0,1},{1,0},{2,3},{3,2},{4,5},{5,4},{6,7},{7,6},{8,9},{9,8},{10,11... | collective-permute-start | bytes 1769480 | tf_op jit(solution)/shard_map/ppermute | solution.py:564
  393.1 24.9 %collective-permute-start.33 = (bf16[8,96,3072]{2,1,0:T(8,128)(2,1)}, bf16[8,96,3072]{2,1,0:T(8,128)(2,1)}, u32[]{:S(2)}, u32[]{:S(2)}) collective-permute-start(bf16[8,96,3072]{2,1,0:T(8,128)(2,1)} %get-tuple-element.448), channel_id=1, source_target_pairs={{0,2},{2,0},{4,6},{6,4},{8,10},{10,8},{12,14},{14,12},{16,18},{18,... | collective-permute-start | bytes 14155784 | tf_op jit(solution)/shard_map/ppermute | solution.py:430
  408.7 9.3 %collective-permute-start.31 = (bf16[8,96,3072]{2,1,0:T(8,128)(2,1)}, bf16[8,96,3072]{2,1,0:T(8,128)(2,1)}, u32[]{:S(2)}, u32[]{:S(2)}) collective-permute-start(bf16[8,96,3072]{2,1,0:T(8,128)(2,1)} %get-tuple-element.446), channel_id=1, source_target_pairs={{0,2},{2,0},{4,6},{6,4},{8,10},{10,8},{12,14},{14,12},{16,18},{18,... | collective-permute-start | bytes 14155784 | tf_op jit(solution)/shard_map/ppermute | solution.py:430
  417.4 14.1 %collective-permute-start.34 = (bf16[8,96,3072]{2,1,0:T(8,128)(2,1)}, bf16[8,96,3072]{2,1,0:T(8,128)(2,1)S(1)}, u32[]{:S(2)}, u32[]{:S(2)}) collective-permute-start(bf16[8,96,3072]{2,1,0:T(8,128)(2,1)} %get-tuple-element.449), channel_id=1, source_target_pairs={{0,2},{2,0},{4,6},{6,4},{8,10},{10,8},{12,14},{14,12},{16,18},{18,... | collective-permute-start | bytes 14155784 | tf_op jit(solution)/shard_map/ppermute | solution.py:430
  417.5 16.2 %collective-permute-start.32 = (bf16[8,96,3072]{2,1,0:T(8,128)(2,1)}, bf16[8,96,3072]{2,1,0:T(8,128)(2,1)}, u32[]{:S(2)}, u32[]{:S(2)}) collective-permute-start(bf16[8,96,3072]{2,1,0:T(8,128)(2,1)} %get-tuple-element.447), channel_id=1, source_target_pairs={{0,2},{2,0},{4,6},{6,4},{8,10},{10,8},{12,14},{14,12},{16,18},{18,... | collective-permute-start | bytes 14155784 | tf_op jit(solution)/shard_map/ppermute | solution.py:430
  438.0 28.2 %collective-permute-start.37 = (bf16[96,6144]{1,0:T(8,128)(2,1)}, bf16[96,6144]{1,0:T(8,128)(2,1)S(1)}, u32[]{:S(2)}, u32[]{:S(2)}) collective-permute-start(bf16[96,6144]{1,0:T(8,128)(2,1)} %get-tuple-element.462), channel_id=1, source_target_pairs={{0,8},{2,10},{8,16},{10,18},{16,24},{18,26},{24,28},{26,30},{28,20... | collective-permute-start | bytes 3538952 | tf_op jit(solution)/shard_map/ppermute | solution.py:497
  438.5 28.8 %collective-permute-start.38 = (bf16[96,6144]{1,0:T(8,128)(2,1)S(1)}, bf16[96,6144]{1,0:T(8,128)(2,1)S(1)}, u32[]{:S(2)}, u32[]{:S(2)}) collective-permute-start(bf16[96,6144]{1,0:T(8,128)(2,1)S(1)} %get-tuple-element.463), channel_id=1, source_target_pairs={{0,4},{2,6},{8,0},{10,2},{16,8},{18,10},{24,16},{26,18},{28,24},{3... | collective-permute-start | bytes 3538952 | tf_op jit(solution)/shard_map/ppermute | solution.py:497
  474.2 27.2 %collective-permute-start.39 = (bf16[96,6144]{1,0:T(8,128)(2,1)S(1)}, bf16[96,6144]{1,0:T(8,128)(2,1)S(1)}, u32[]{:S(2)}, u32[]{:S(2)}) collective-permute-start(bf16[96,6144]{1,0:T(8,128)(2,1)S(1)} %get-tuple-element.488), channel_id=1, source_target_pairs={{0,8},{2,10},{8,16},{10,18},{16,24},{18,26},{24,28},{26,30},{28,20... | collective-permute-start | bytes 3538952 | tf_op jit(solution)/shard_map/ppermute | solution.py:497
  474.7 26.9 %collective-permute-start.40 = (bf16[96,6144]{1,0:T(8,128)(2,1)S(1)}, bf16[96,6144]{1,0:T(8,128)(2,1)S(1)}, u32[]{:S(2)}, u32[]{:S(2)}) collective-permute-start(bf16[96,6144]{1,0:T(8,128)(2,1)S(1)} %get-tuple-element.489), channel_id=1, source_target_pairs={{0,4},{2,6},{8,0},{10,2},{16,8},{18,10},{24,16},{26,18},{28,24},{3... | collective-permute-start | bytes 3538952 | tf_op jit(solution)/shard_map/ppermute | solution.py:497
  476.3 43.7 %collective-permute-start.35 = (bf16[3,128,1536]{2,1,0:T(8,128)(2,1)S(1)}, bf16[3,128,1536]{2,1,0:T(8,128)(2,1)S(1)}, u32[]{:S(2)}, u32[]{:S(2)}) collective-permute-start(bf16[3,128,1536]{2,1,0:T(8,128)(2,1)S(1)} %get-tuple-element.480), channel_id=1, source_target_pairs={{0,1},{1,0},{2,3},{3,2},{4,5},{5,4},{6,7},{7,6},{8,9},{9,8},{10,11... | collective-permute-start | bytes 3538952 | tf_op jit(solution)/shard_map/ppermute | solution.py:545
  505.0 26.1 %collective-permute-start.41 = (bf16[96,6144]{1,0:T(8,128)(2,1)S(1)}, bf16[96,6144]{1,0:T(8,128)(2,1)S(1)}, u32[]{:S(2)}, u32[]{:S(2)}) collective-permute-start(bf16[96,6144]{1,0:T(8,128)(2,1)S(1)} %get-tuple-element.506), channel_id=1, source_target_pairs={{0,8},{2,10},{8,16},{10,18},{16,24},{18,26},{24,28},{26,30},{28,20... | collective-permute-start | bytes 3538952 | tf_op jit(solution)/shard_map/ppermute | solution.py:497
  505.7 25.7 %collective-permute-start.42 = (bf16[96,6144]{1,0:T(8,128)(2,1)S(1)}, bf16[96,6144]{1,0:T(8,128)(2,1)S(1)}, u32[]{:S(2)}, u32[]{:S(2)}) collective-permute-start(bf16[96,6144]{1,0:T(8,128)(2,1)S(1)} %get-tuple-element.507), channel_id=1, source_target_pairs={{0,4},{2,6},{8,0},{10,2},{16,8},{18,10},{24,16},{26,18},{28,24},{3... | collective-permute-start | bytes 3538952 | tf_op jit(solution)/shard_map/ppermute | solution.py:497
  507.1 12.9 %collective-permute-start.36 = (bf16[3,64,1536]{2,1,0:T(8,128)(2,1)S(1)}, bf16[3,64,1536]{2,1,0:T(8,128)(2,1)S(1)}, u32[]{:S(2)}, u32[]{:S(2)}) collective-permute-start(bf16[3,64,1536]{2,1,0:T(8,128)(2,1)S(1)} %get-tuple-element.481), channel_id=1, source_target_pairs={{0,1},{1,0},{2,3},{3,2},{4,5},{5,4},{6,7},{7,6},{8,9},{9,8},{10,11... | collective-permute-start | bytes 1769480 | tf_op jit(solution)/shard_map/ppermute | solution.py:545
  534.8 25.0 %collective-permute-start.43 = (bf16[96,6144]{1,0:T(8,128)(2,1)S(1)}, bf16[96,6144]{1,0:T(8,128)(2,1)S(1)}, u32[]{:S(2)}, u32[]{:S(2)}) collective-permute-start(bf16[96,6144]{1,0:T(8,128)(2,1)S(1)} %get-tuple-element.522), channel_id=1, source_target_pairs={{0,8},{2,10},{8,16},{10,18},{16,24},{18,26},{24,28},{26,30},{28,20... | collective-permute-start | bytes 3538952 | tf_op jit(solution)/shard_map/ppermute | solution.py:497
  536.1 24.7 %collective-permute-start.44 = (bf16[96,6144]{1,0:T(8,128)(2,1)S(1)}, bf16[96,6144]{1,0:T(8,128)(2,1)}, u32[]{:S(2)}, u32[]{:S(2)}) collective-permute-start(bf16[96,6144]{1,0:T(8,128)(2,1)S(1)} %get-tuple-element.523), channel_id=1, source_target_pairs={{0,4},{2,6},{8,0},{10,2},{16,8},{18,10},{24,16},{26,18},{28,24},{3... | collective-permute-start | bytes 3538952 | tf_op jit(solution)/shard_map/ppermute | solution.py:497
  536.9 31.4 %collective-permute-start.48 = (bf16[3,64,1536]{2,1,0:T(8,128)(2,1)}, bf16[3,64,1536]{2,1,0:T(8,128)(2,1)S(1)}, u32[]{:S(2)}, u32[]{:S(2)}) collective-permute-start(bf16[3,64,1536]{2,1,0:T(8,128)(2,1)} %bitcast.61), channel_id=1, source_target_pairs={{0,1},{1,0},{2,3},{3,2},{4,5},{5,4},{6,7},{7,6},{8,9},{9,8},{10,11... | collective-permute-start | bytes 1769480 | tf_op jit(solution)/shard_map/ppermute | solution.py:564
  538.5 40.6 %collective-permute-start.47 = (bf16[3,128,1536]{2,1,0:T(8,128)(2,1)}, bf16[3,128,1536]{2,1,0:T(8,128)(2,1)}, u32[]{:S(2)}, u32[]{:S(2)}) collective-permute-start(bf16[3,128,1536]{2,1,0:T(8,128)(2,1)} %bitcast.59), channel_id=1, source_target_pairs={{0,1},{1,0},{2,3},{3,2},{4,5},{5,4},{6,7},{7,6},{8,9},{9,8},{10,11... | collective-permute-start | bytes 3538952 | tf_op jit(solution)/shard_map/ppermute | solution.py:564
  547.9 31.3 %collective-permute-start.46 = (bf16[8,96,768]{2,1,0:T(8,128)(2,1)}, bf16[8,96,768]{2,1,0:T(8,128)(2,1)S(1)}, u32[]{:S(2)}, u32[]{:S(2)}) collective-permute-start(bf16[8,96,768]{2,1,0:T(8,128)(2,1)} %get-tuple-element.554), channel_id=1, source_target_pairs={{0,2},{2,0},{4,6},{6,4},{8,10},{10,8},{12,14},{14,12},{16,18},{18,... | collective-permute-start | bytes 3538952 | tf_op jit(solution)/shard_map/ppermute | solution.py:430
  560.8 18.4 %collective-permute-start.45 = (bf16[8,96,768]{2,1,0:T(8,128)(2,1)}, bf16[8,96,768]{2,1,0:T(8,128)(2,1)S(1)}, u32[]{:S(2)}, u32[]{:S(2)}) collective-permute-start(bf16[8,96,768]{2,1,0:T(8,128)(2,1)} %get-tuple-element.553), channel_id=1, source_target_pairs={{0,2},{2,0},{4,6},{6,4},{8,10},{10,8},{12,14},{14,12},{16,18},{18,... | collective-permute-start | bytes 3538952 | tf_op jit(solution)/shard_map/ppermute | solution.py:430
  566.6 28.6 %collective-permute-start.49 = (bf16[96,6144]{1,0:T(8,128)(2,1)}, bf16[96,6144]{1,0:T(8,128)(2,1)S(1)}, u32[]{:S(2)}, u32[]{:S(2)}) collective-permute-start(bf16[96,6144]{1,0:T(8,128)(2,1)} %get-tuple-element.545), channel_id=1, source_target_pairs={{0,8},{2,10},{8,16},{10,18},{16,24},{18,26},{24,28},{26,30},{28,20... | collective-permute-start | bytes 3538952 | tf_op jit(solution)/shard_map/ppermute | solution.py:497
  568.3 27.5 %collective-permute-start.50 = (bf16[96,6144]{1,0:T(8,128)(2,1)S(1)}, bf16[96,6144]{1,0:T(8,128)(2,1)S(1)}, u32[]{:S(2)}, u32[]{:S(2)}) collective-permute-start(bf16[96,6144]{1,0:T(8,128)(2,1)S(1)} %get-tuple-element.546), channel_id=1, source_target_pairs={{0,4},{2,6},{8,0},{10,2},{16,8},{18,10},{24,16},{26,18},{28,24},{3... | collective-permute-start | bytes 3538952 | tf_op jit(solution)/shard_map/ppermute | solution.py:497
  599.2 27.0 %collective-permute-start.51 = (bf16[96,6144]{1,0:T(8,128)(2,1)S(1)}, bf16[96,6144]{1,0:T(8,128)(2,1)S(1)}, u32[]{:S(2)}, u32[]{:S(2)}) collective-permute-start(bf16[96,6144]{1,0:T(8,128)(2,1)S(1)} %get-tuple-element.573), channel_id=1, source_target_pairs={{0,8},{2,10},{8,16},{10,18},{16,24},{18,26},{24,28},{26,30},{28,20... | collective-permute-start | bytes 3538952 | tf_op jit(solution)/shard_map/ppermute | solution.py:497
  601.0 26.6 %collective-permute-start.52 = (bf16[96,6144]{1,0:T(8,128)(2,1)S(1)}, bf16[96,6144]{1,0:T(8,128)(2,1)S(1)}, u32[]{:S(2)}, u32[]{:S(2)}) collective-permute-start(bf16[96,6144]{1,0:T(8,128)(2,1)S(1)} %get-tuple-element.574), channel_id=1, source_target_pairs={{0,4},{2,6},{8,0},{10,2},{16,8},{18,10},{24,16},{26,18},{28,24},{3... | collective-permute-start | bytes 3538952 | tf_op jit(solution)/shard_map/ppermute | solution.py:497
  652.9 11.6 %collective-permute-start.53 = (bf16[8,96,2304]{2,1,0:T(8,128)(2,1)}, bf16[8,96,2304]{2,1,0:T(8,128)(2,1)}, u32[]{:S(2)}, u32[]{:S(2)}) collective-permute-start(bf16[8,96,2304]{2,1,0:T(8,128)(2,1)} %get-tuple-element.602), channel_id=1, source_target_pairs={{0,2},{2,0},{4,6},{6,4},{8,10},{10,8},{12,14},{14,12},{16,18},{18,... | collective-permute-start | bytes 10616840 | tf_op jit(solution)/shard_map/ppermute | solution.py:430
  653.6 67.0 %collective-permute-start.55 = (bf16[3,128,1536]{2,1,0:T(8,128)(2,1)}, bf16[3,128,1536]{2,1,0:T(8,128)(2,1)}, u32[]{:S(2)}, u32[]{:S(2)}) collective-permute-start(bf16[3,128,1536]{2,1,0:T(8,128)(2,1)} %bitcast.237), channel_id=1, source_target_pairs={{0,1},{1,0},{2,3},{3,2},{4,5},{5,4},{6,7},{7,6},{8,9},{9,8},{10,11... | collective-permute-start | bytes 3538952 | tf_op jit(solution)/shard_map/ppermute | solution.py:564
  655.7 58.4 %collective-permute-start.59 = (bf16[96,6144]{1,0:T(8,128)(2,1)}, bf16[96,6144]{1,0:T(8,128)(2,1)}, u32[]{:S(2)}, u32[]{:S(2)}) collective-permute-start(bf16[96,6144]{1,0:T(8,128)(2,1)} %copy-done.132), channel_id=1, source_target_pairs={{0,8},{2,10},{8,16},{10,18},{16,24},{18,26},{24,28},{26,30},{28,20... | collective-permute-start | bytes 3538952 | tf_op jit(solution)/shard_map/ppermute | solution.py:497
  657.4 57.0 %collective-permute-start.60 = (bf16[96,6144]{1,0:T(8,128)(2,1)}, bf16[96,6144]{1,0:T(8,128)(2,1)}, u32[]{:S(2)}, u32[]{:S(2)}) collective-permute-start(bf16[96,6144]{1,0:T(8,128)(2,1)} %copy-done.131), channel_id=1, source_target_pairs={{0,4},{2,6},{8,0},{10,2},{16,8},{18,10},{24,16},{26,18},{28,24},{3... | collective-permute-start | bytes 3538952 | tf_op jit(solution)/shard_map/ppermute | solution.py:497
  671.6 24.7 %collective-permute-start.57 = (bf16[96,3072]{1,0:T(8,128)(2,1)}, bf16[96,3072]{1,0:T(8,128)(2,1)}, u32[]{:S(2)}, u32[]{:S(2)}) collective-permute-start(bf16[96,3072]{1,0:T(8,128)(2,1)} %get-tuple-element.619), channel_id=1, source_target_pairs={{0,8},{2,10},{8,16},{10,18},{16,24},{18,26},{24,28},{26,30},{28,20... | collective-permute-start | bytes 1769480 | tf_op jit(solution)/shard_map/ppermute | solution.py:497
  673.5 34.7 %collective-permute-start.58 = (bf16[96,3072]{1,0:T(8,128)(2,1)}, bf16[96,3072]{1,0:T(8,128)(2,1)}, u32[]{:S(2)}, u32[]{:S(2)}) collective-permute-start(bf16[96,3072]{1,0:T(8,128)(2,1)} %get-tuple-element.620), channel_id=1, source_target_pairs={{0,4},{2,6},{8,0},{10,2},{16,8},{18,10},{24,16},{26,18},{28,24},{3... | collective-permute-start | bytes 1769480 | tf_op jit(solution)/shard_map/ppermute | solution.py:497
  696.2 24.3 %collective-permute-start.56 = (bf16[3,64,1536]{2,1,0:T(8,128)(2,1)}, bf16[3,64,1536]{2,1,0:T(8,128)(2,1)}, u32[]{:S(2)}, u32[]{:S(2)}) collective-permute-start(bf16[3,64,1536]{2,1,0:T(8,128)(2,1)} %bitcast.239), channel_id=1, source_target_pairs={{0,1},{1,0},{2,3},{3,2},{4,5},{5,4},{6,7},{7,6},{8,9},{9,8},{10,11... | collective-permute-start | bytes 1769480 | tf_op jit(solution)/shard_map/ppermute | solution.py:564
  712.3 19.5 %collective-permute-start.61 = (bf16[96,3072]{1,0:T(8,128)(2,1)S(1)}, bf16[96,3072]{1,0:T(8,128)(2,1)S(1)}, u32[]{:S(2)}, u32[]{:S(2)}) collective-permute-start(bf16[96,3072]{1,0:T(8,128)(2,1)S(1)} %get-tuple-element.642), channel_id=1, source_target_pairs={{0,8},{2,10},{8,16},{10,18},{16,24},{18,26},{24,28},{26,30},{28,20... | collective-permute-start | bytes 1769480 | tf_op jit(solution)/shard_map/ppermute | solution.py:497
  714.1 17.7 %collective-permute-start.62 = (bf16[96,3072]{1,0:T(8,128)(2,1)S(1)}, bf16[96,3072]{1,0:T(8,128)(2,1)S(1)}, u32[]{:S(2)}, u32[]{:S(2)}) collective-permute-start(bf16[96,3072]{1,0:T(8,128)(2,1)S(1)} %get-tuple-element.643), channel_id=1, source_target_pairs={{0,4},{2,6},{8,0},{10,2},{16,8},{18,10},{24,16},{26,18},{28,24},{3... | collective-permute-start | bytes 1769480 | tf_op jit(solution)/shard_map/ppermute | solution.py:497
  741.8 17.6 %collective-permute-start.64 = (bf16[96,3072]{1,0:T(8,128)(2,1)}, bf16[96,3072]{1,0:T(8,128)(2,1)S(1)}, u32[]{:S(2)}, u32[]{:S(2)}) collective-permute-start(bf16[96,3072]{1,0:T(8,128)(2,1)} %copy-done.134), channel_id=1, source_target_pairs={{0,8},{2,10},{8,16},{10,18},{16,24},{18,26},{24,28},{26,30},{28,20... | collective-permute-start | bytes 1769480 | tf_op jit(solution)/shard_map/ppermute | solution.py:497
  743.6 18.2 %collective-permute-start.65 = (bf16[96,3072]{1,0:T(8,128)(2,1)S(1)}, bf16[96,3072]{1,0:T(8,128)(2,1)S(1)}, u32[]{:S(2)}, u32[]{:S(2)}) collective-permute-start(bf16[96,3072]{1,0:T(8,128)(2,1)S(1)} %get-tuple-element.684), channel_id=1, source_target_pairs={{0,4},{2,6},{8,0},{10,2},{16,8},{18,10},{24,16},{26,18},{28,24},{3... | collective-permute-start | bytes 1769480 | tf_op jit(solution)/shard_map/ppermute | solution.py:497
  766.2 21.8 %collective-permute-start.66 = (bf16[96,3072]{1,0:T(8,128)(2,1)}, bf16[96,3072]{1,0:T(8,128)(2,1)S(1)}, u32[]{:S(2)}, u32[]{:S(2)}) collective-permute-start(bf16[96,3072]{1,0:T(8,128)(2,1)} %get-tuple-element.692), channel_id=1, source_target_pairs={{0,8},{2,10},{8,16},{10,18},{16,24},{18,26},{24,28},{26,30},{28,20... | collective-permute-start | bytes 1769480 | tf_op jit(solution)/shard_map/ppermute | solution.py:497
  767.3 28.7 %collective-permute-start.67 = (bf16[96,3072]{1,0:T(8,128)(2,1)}, bf16[96,3072]{1,0:T(8,128)(2,1)S(1)}, u32[]{:S(2)}, u32[]{:S(2)}) collective-permute-start(bf16[96,3072]{1,0:T(8,128)(2,1)} %get-tuple-element.693), channel_id=1, source_target_pairs={{0,4},{2,6},{8,0},{10,2},{16,8},{18,10},{24,16},{26,18},{28,24},{3... | collective-permute-start | bytes 1769480 | tf_op jit(solution)/shard_map/ppermute | solution.py:497
  799.8 16.0 %collective-permute-start.68 = (bf16[96,3072]{1,0:T(8,128)(2,1)S(1)}, bf16[96,3072]{1,0:T(8,128)(2,1)S(1)}, u32[]{:S(2)}, u32[]{:S(2)}) collective-permute-start(bf16[96,3072]{1,0:T(8,128)(2,1)S(1)} %get-tuple-element.698), channel_id=1, source_target_pairs={{0,8},{2,10},{8,16},{10,18},{16,24},{18,26},{24,28},{26,30},{28,20... | collective-permute-start | bytes 1769480 | tf_op jit(solution)/shard_map/ppermute | solution.py:497
  799.9 16.2 %collective-permute-start.69 = (bf16[96,3072]{1,0:T(8,128)(2,1)S(1)}, bf16[96,3072]{1,0:T(8,128)(2,1)S(1)}, u32[]{:S(2)}, u32[]{:S(2)}) collective-permute-start(bf16[96,3072]{1,0:T(8,128)(2,1)S(1)} %get-tuple-element.699), channel_id=1, source_target_pairs={{0,4},{2,6},{8,0},{10,2},{16,8},{18,10},{24,16},{26,18},{28,24},{3... | collective-permute-start | bytes 1769480 | tf_op jit(solution)/shard_map/ppermute | solution.py:497
  819.3 15.7 %collective-permute-start.71 = (bf16[96,3072]{1,0:T(8,128)(2,1)}, bf16[96,3072]{1,0:T(8,128)(2,1)S(1)}, u32[]{:S(2)}, u32[]{:S(2)}) collective-permute-start(bf16[96,3072]{1,0:T(8,128)(2,1)} %get-tuple-element.702), channel_id=1, source_target_pairs={{0,8},{2,10},{8,16},{10,18},{16,24},{18,26},{24,28},{26,30},{28,20... | collective-permute-start | bytes 1769480 | tf_op jit(solution)/shard_map/ppermute | solution.py:497
  819.3 15.7 %collective-permute-start.72 = (bf16[96,3072]{1,0:T(8,128)(2,1)}, bf16[96,3072]{1,0:T(8,128)(2,1)S(1)}, u32[]{:S(2)}, u32[]{:S(2)}) collective-permute-start(bf16[96,3072]{1,0:T(8,128)(2,1)} %get-tuple-element.703), channel_id=1, source_target_pairs={{0,4},{2,6},{8,0},{10,2},{16,8},{18,10},{24,16},{26,18},{28,24},{3... | collective-permute-start | bytes 1769480 | tf_op jit(solution)/shard_map/ppermute | solution.py:497
  837.7 11.0 %collective-permute-start.74 = (bf16[96,3072]{1,0:T(8,128)(2,1)S(1)}, bf16[96,3072]{1,0:T(8,128)(2,1)S(1)}, u32[]{:S(2)}, u32[]{:S(2)}) collective-permute-start(bf16[96,3072]{1,0:T(8,128)(2,1)S(1)} %get-tuple-element.708), channel_id=1, source_target_pairs={{0,8},{2,10},{8,16},{10,18},{16,24},{18,26},{24,28},{26,30},{28,20... | collective-permute-start | bytes 1769480 | tf_op jit(solution)/shard_map/ppermute | solution.py:497
  837.8 10.9 %collective-permute-start.75 = (bf16[96,3072]{1,0:T(8,128)(2,1)S(1)}, bf16[96,3072]{1,0:T(8,128)(2,1)S(1)}, u32[]{:S(2)}, u32[]{:S(2)}) collective-permute-start(bf16[96,3072]{1,0:T(8,128)(2,1)S(1)} %get-tuple-element.709), channel_id=1, source_target_pairs={{0,4},{2,6},{8,0},{10,2},{16,8},{18,10},{24,16},{26,18},{28,24},{3... | collective-permute-start | bytes 1769480 | tf_op jit(solution)/shard_map/ppermute | solution.py:497
  853.1 7.6 collective-permute-start.76
  (173 other events, 1290.9 us)
Sparse Core Ops, SparseCore 0:
  13.2 119.0 all-gather.4
  133.9 99.1 all-gather.8
  234.6 98.9 all-gather.6
  742.0 53.6 all-gather.10

commit v4 on v3

--- a/solution.py
+++ b/solution.py
@@ -433,7 +433,7 @@
         last = self.step == self.chips - 1
         widths = [view.shape[-1] for view in self.views[0]]
         rows = self.views[0][0].shape[1]
-        tile = rows // 2 if rows % 32 == 0 else rows
+        tile = rows // 2 if rows % 32 == 0 and sum(widths) > 4096 else rows
         at = jnp.stack([self.targets[s][self.step] for s in range(2)])
         operands, specs, places = [], [], []
         for s in range(2):

time: 886 us -> 885 us (level)
  transfers between devices with their start and end apart: 82 -> 82, of which waited for: 48 -> 49; matrix products, arithmetic and copies ran while one was open for 5% -> 5% of each run, Pallas kernels for 34% -> 34%
where the time goes in v4:
time: 885 us; the launch traced here: 876 us
  Pallas kernels  370 us (42%)
  waiting for transfers between devices  284 us (32%)
  local copies, waits for them, and re-layouts  91.8 us (10%)
  starting transfers between devices  79.4 us (9%)
  other arithmetic  28.1 us (3%)
  between operations  16.1 us (2%)
    ppermute x42, waiting for transfers between devices, advance(): lax.ppermute(total[s][0], 'dp', self.hops[s])  152 us
    pallas_call x16, Pallas kernels, matmul(): pl.pallas_call(kernel, grid=(columns // tile,), in_specs=specs, out_specs...  145 us
    pallas_call x8, Pallas kernels, weight_grad(): pl.pallas_call(kernel, grid_spec=pltpu.PrefetchScalarGridSpec(num_scalar_...  75.1 us
    unnamed x321, local copies, waits for them, and re-layouts  63.6 us
    pallas_call x24, Pallas kernels, add(): pl.pallas_call(kernel, grid_spec=pltpu.PrefetchScalarGridSpec(num_scalar_...  57.2 us
    ppermute x8, waiting for transfers between devices, share(): return whole(flat(rows)) + whole(flat(lax.ppermute(rows, 'mp', swap)))  56.8 us
    ppermute x42, starting transfers between devices, advance(): lax.ppermute(total[s][0], 'dp', self.hops[s])  44.4 us
    pallas_call x10, Pallas kernels, stage(): pl.pallas_call(kernel, grid_spec=pltpu.PrefetchScalarGridSpec(num_scalar_...  40 us
  transfers between devices with their start and end apart: 82, of which 49 were waited for; matrix products, arithmetic and copies ran while one was open for 5% of the time, Pallas kernels for 34%

profile of v4, /device:TPU:0, one launch (start us, length us, event | category | flops | bytes accessed | tf_op | source)
XLA Modules:
  0.0 876.2 jit_solution(17169714327271042307)
XLA Ops:
  18.9 4.1 collective-permute-start
  54.8 5.9 collective-permute-done.6.refs_2_
  64.6 5.3 collective-permute-done.8.refs_2_
  75.0 5.4 collective-permute-done.10.refs_2_
  84.7 5.0 collective-permute-done.12.refs_2_
  94.2 5.3 collective-permute-done.14.refs_2_
  102.6 5.6 collective-permute-done.16.refs_2_
  111.3 4.8 collective-permute-done.18.refs_2_
  123.7 5.9 collective-permute-done.20
  138.2 31.8 %collective-permute-done.22 = bf16[3,64,1536]{2,1,0:T(8,128)(2,1)S(1)} collective-permute-done((bf16[3,64,1536]{2,1,0:T(8,128)(2,1)S(1)}, bf16[3,64,1536]{2,1,0:T(8,128)(2,1)S(1)}, u32[]{:S(2)}, u32[]{:S(2)}) %collective-permute-start.22) | collective-permute-done | bytes 589856 | tf_op jit(solution)/shard_map/ppermute | solution.py:545
  175.4 7.4 qkv.3
  183.7 10.6 %qkv.2 = bf16[768,2304]{1,0:T(8,128)(2,1)S(1)} custom-call(bf16[384,1536]{1,0:T(8,128)(2,1)S(1)} %bitcast.191, bf16[384,1536]{1,0:T(8,128)(2,1)S(1)} %bitcast.193, bf16[2,1536,3072]{2,1,0:T(8,128)(2,1)} %all-gather.5.cloned.1.call-done.refs_2_, f32[2,1,2304]{2,1,0:T(1,128)S(1)} %reshape.400.refs_3_), custom_call_target="tpu_custom_call" | custom-call | flops 1024 | bytes 1024 | tf_op jit(solution)/shard_map/qkv/pallas_call | solution.py:350
  196.1 20.9 %attention_forward.1 = (bf16[2,3,128,768]{3,2,1,0:T(8,128)(2,1)S(1)}, bf16[2,3,64,768]{3,2,1,0:T(8,128)(2,1)S(1)}) custom-call(bf16[2,3,128,2304]{3,2,1,0:T(8,128)(2,1)} %bitcast.164, bf16[2,3,64,2304]{3,2,1,0:T(8,128)(2,1)S(1)} %bitcast.173), custom_call_target="tpu_custom_call" | custom-call | flops 1024 | bytes 1024 | tf_op jit(solution)/shard_map/attention_forward/pallas_call | solution.py:105
  217.1 5.5 proj.2
  225.7 4.4 proj.3
  232.3 20.8 %collective-permute-done.25.came = bf16[3,128,1536]{2,1,0:T(8,128)(2,1)} collective-permute-done((bf16[3,128,1536]{2,1,0:T(8,128)(2,1)}, bf16[3,128,1536]{2,1,0:T(8,128)(2,1)}, u32[]{:S(2)}, u32[]{:S(2)}) %collective-permute-start.25) | collective-permute-done | bytes 1179680 | tf_op jit(solution)/shard_map/ppermute | solution.py:564
  253.2 5.5 middle.2
  261.8 4.0 collective-permute-done.27.came
  276.1 13.5 %collective-permute-done.28 = bf16[3,64,1536]{2,1,0:T(8,128)(2,1)S(1)} collective-permute-done((bf16[3,64,1536]{2,1,0:T(8,128)(2,1)S(1)}, bf16[3,64,1536]{2,1,0:T(8,128)(2,1)S(1)}, u32[]{:S(2)}, u32[]{:S(2)}) %collective-permute-start.28) | collective-permute-done | bytes 589856 | tf_op jit(solution)/shard_map/ppermute | solution.py:545
  293.4 10.9 %up.3 = (bf16[384,3072]{1,0:T(8,128)(2,1)S(1)}, f32[384,3072]{1,0:T(8,128)}) custom-call(bf16[192,1536]{1,0:T(8,128)(2,1)S(1)} %bitcast.211, bf16[192,1536]{1,0:T(8,128)(2,1)S(1)} %bitcast.213, bf16[2,1536,3072]{2,1,0:T(8,128)(2,1)} %all-gather.9.cloned.1.call-done.refs_2_, f32[2,1,3072]{2,1,0:T(1,128)S(1)} %copy-done.89), custom_call_target="tpu_custom_call" | custom-call | flops 1024 | bytes 1024 | tf_op jit(solution)/shard_map/up/pallas_call | solution.py:350
  304.3 9.0 %weight_grad.9 = (bf16[8,96,3072]{2,1,0:T(8,128)(2,1)}, bf16[8,96,3072]{2,1,0:T(8,128)(2,1)}) custom-call(s32[1]{0:T(128)} %bitcast.32.core_ref, bf16[192,1536]{1,0:T(8,128)(2,1)} %bitcast.35.refs_0_, bf16[192,1536]{1,0:T(8,128)(2,1)} %bitcast.36.refs_1_, bf16[384,3072]{1,0:T(8,128)(2,1)S(1)} %get-tuple-element.493.refs_2_.refs_3_.refs_0_.refs_1_, ...), custom_call_target="tpu_custom_call" | custom-call | flops 1024 | bytes 1024 | tf_op jit(solution)/shard_map/weight_grad/pallas_call | solution.py:303
  313.3 17.1 %up.2 = (bf16[768,3072]{1,0:T(8,128)(2,1)}, f32[768,3072]{1,0:T(8,128)}) custom-call(bf16[384,1536]{1,0:T(8,128)(2,1)} %bitcast.41.refs_0_, bf16[384,1536]{1,0:T(8,128)(2,1)} %bitcast.42.refs_1_, bf16[2,1536,3072]{2,1,0:T(8,128)(2,1)} %all-gather.9.cloned.1.call-done.refs_2_, f32[2,1,3072]{2,1,0:T(1,128)S(1)} %copy-done.90), custom_call_target="tpu_custom_call" | custom-call | flops 1024 | bytes 1024 | tf_op jit(solution)/shard_map/up/pallas_call | solution.py:350
  330.3 15.8 %weight_grad.8 = (bf16[8,96,3072]{2,1,0:T(8,128)(2,1)}, bf16[8,96,3072]{2,1,0:T(8,128)(2,1)}) custom-call(s32[1]{0:T(128)} %bitcast.32.core_ref, bf16[384,1536]{1,0:T(8,128)(2,1)} %bitcast.33.refs_0_, bf16[384,1536]{1,0:T(8,128)(2,1)} %bitcast.34.refs_1_, bf16[768,3072]{1,0:T(8,128)(2,1)} %get-tuple-element.490.refs_2_.refs_3_.refs_0_.refs_1_, ...), custom_call_target="tpu_custom_call" | custom-call | flops 1024 | bytes 1024 | tf_op jit(solution)/shard_map/weight_grad/pallas_call | solution.py:303
  346.1 13.9 %down_back.2 = (bf16[768,3072]{1,0:T(8,128)(2,1)}, f32[1,3072]{1,0:T(1,128)S(1)}) custom-call(bf16[384,1536]{1,0:T(8,128)(2,1)} %bitcast.33.refs_0_, bf16[384,1536]{1,0:T(8,128)(2,1)} %bitcast.34.refs_1_, bf16[2,1536,3072]{2,1,0:T(8,128)(2,1)} %all-gather.7.cloned.1.call-done.refs_2_, f32[768,3072]{1,0:T(8,128)} %get-tuple-element.421.refs_3_), custom_call_target="tpu_custom_call" | custom-call | flops 1024 | bytes 1024 | tf_op jit(solution)/shard_map/down_back/pallas_call | solution.py:350
  360.0 11.4 %up_back.2 = (f32[384,1536]{1,0:T(8,128)S(1)}, bf16[384,1536]{1,0:T(8,128)(2,1)S(1)}) custom-call(bf16[768,3072]{1,0:T(8,128)(2,1)} %get-tuple-element.431.refs_0_.refs_1_.refs_2_.refs_3_, bf16[768,3072]{1,0:T(8,128)(2,1)} %get-tuple-element.431.refs_0_.refs_1_.refs_2_.refs_3_, bf16[2,1536,3072]{2,1,0:T(8,128)(2,1)} %all-gather.9.cloned.1.call-done.refs_2_), custom_call_target="tpu_custom_call" | custom-call | flops 1024 | bytes 1024 | tf_op jit(solution)/shard_map/up_back/pallas_call | solution.py:350
  374.4 8.9 %down_back.3 = (bf16[384,3072]{1,0:T(8,128)(2,1)S(1)}, f32[1,3072]{1,0:T(1,128)S(1)}) custom-call(bf16[192,1536]{1,0:T(8,128)(2,1)} %bitcast.35.refs_0_, bf16[192,1536]{1,0:T(8,128)(2,1)} %bitcast.36.refs_1_, bf16[2,1536,3072]{2,1,0:T(8,128)(2,1)} %all-gather.7.cloned.1.call-done.refs_2_, f32[384,3072]{1,0:T(8,128)} %get-tuple-element.426.refs_3_), custom_call_target="tpu_custom_call" | custom-call | flops 1024 | bytes 1024 | tf_op jit(solution)/shard_map/down_back/pallas_call | solution.py:350
  383.9 8.7 up_back.3
  393.1 15.6 %weight_grad.10 = (bf16[8,96,3072]{2,1,0:T(8,128)(2,1)}, bf16[8,96,3072]{2,1,0:T(8,128)(2,1)}) custom-call(s32[1]{0:T(128)} %bitcast.32.core_ref, bf16[384,1536]{1,0:T(8,128)(2,1)} %bitcast.41.refs_0_, bf16[384,1536]{1,0:T(8,128)(2,1)} %bitcast.42.refs_1_, bf16[768,3072]{1,0:T(8,128)(2,1)} %get-tuple-element.431.refs_0_.refs_1_.refs_2_.refs_3_, ...), custom_call_target="tpu_custom_call" | custom-call | flops 1024 | bytes 1024 | tf_op jit(solution)/shard_map/weight_grad/pallas_call | solution.py:303
  409.2 8.2 weight_grad.11
  418.1 13.6 %collective-permute-done.34.refs_7_.refs_8_ = bf16[8,96,3072]{2,1,0:T(8,128)(2,1)S(1)} collective-permute-done((bf16[8,96,3072]{2,1,0:T(8,128)(2,1)}, bf16[8,96,3072]{2,1,0:T(8,128)(2,1)S(1)}, u32[]{:S(2)}, u32[]{:S(2)}) %collective-permute-start.34) | collective-permute-done | bytes 4718624 | tf_op jit(solution)/shard_map/ppermute | solution.py:430
  433.8 4.3 ring_add.32
  440.1 3.6 middle_back.3
  445.0 5.5 middle_back.2
  453.2 13.1 %collective-permute-done.37.refs_4_ = bf16[96,6144]{1,0:T(8,128)(2,1)S(1)} collective-permute-done((bf16[96,6144]{1,0:T(8,128)(2,1)}, bf16[96,6144]{1,0:T(8,128)(2,1)S(1)}, u32[]{:S(2)}, u32[]{:S(2)}) %collective-permute-start.37) | collective-permute-done | bytes 1179680 | tf_op jit(solution)/shard_map/ppermute | solution.py:497
  477.9 12.1 %down.2 = (f32[384,1536]{1,0:T(8,128)S(1)}, bf16[384,1536]{1,0:T(8,128)(2,1)}) custom-call(bf16[768,3072]{1,0:T(8,128)(2,1)} %get-tuple-element.490.refs_2_.refs_3_.refs_0_.refs_1_, bf16[768,3072]{1,0:T(8,128)(2,1)} %get-tuple-element.490.refs_2_.refs_3_.refs_0_.refs_1_, bf16[2,1536,3072]{2,1,0:T(8,128)(2,1)} %all-gather.7.cloned.1.call-done.refs_2_), custom_call_target="tpu_custom_call" | custom-call | flops 1024 | bytes 1024 | tf_op jit(solution)/shard_map/down/pallas_call | solution.py:350
  490.0 10.1 %down.3 = (f32[192,1536]{1,0:T(8,128)S(1)}, bf16[192,1536]{1,0:T(8,128)(2,1)}) custom-call(bf16[384,3072]{1,0:T(8,128)(2,1)S(1)} %get-tuple-element.493.refs_2_.refs_3_.refs_0_.refs_1_, bf16[384,3072]{1,0:T(8,128)(2,1)S(1)} %get-tuple-element.493.refs_2_.refs_3_.refs_0_.refs_1_, bf16[2,1536,3072]{2,1,0:T(8,128)(2,1)} %all-gather.7.cloned.1.call-done.refs_2_), custom_call_target="tpu_custom_call" | custom-call | flops 1024 | bytes 1024 | tf_op jit(solution)/shard_map/down/pallas_call | solution.py:350
  501.6 3.4 ring_add.34
  508.6 11.4 %collective-permute-done.36 = bf16[3,64,1536]{2,1,0:T(8,128)(2,1)S(1)} collective-permute-done((bf16[3,64,1536]{2,1,0:T(8,128)(2,1)S(1)}, bf16[3,64,1536]{2,1,0:T(8,128)(2,1)S(1)}, u32[]{:S(2)}, u32[]{:S(2)}) %collective-permute-start.36) | collective-permute-done | bytes 589856 | tf_op jit(solution)/shard_map/ppermute | solution.py:545
  523.0 4.2 proj_back.2
  527.2 4.1 collective-permute-done.41.refs_4_
  538.9 4.6 weight_grad.12
  547.9 10.6 %attention_backward.3 = (bf16[2,3,128,2304]{3,2,1,0:T(8,128)(2,1)}, bf16[2,3,64,2304]{3,2,1,0:T(8,128)(2,1)S(1)}) custom-call(bf16[2,3,128,2304]{3,2,1,0:T(8,128)(2,1)} %bitcast.165, bf16[2,3,64,2304]{3,2,1,0:T(8,128)(2,1)S(1)} %bitcast.174, bf16[2,3,128,768]{3,2,1,0:T(8,128)(2,1)S(1)} %bitcast.177, bf16[2,3,64,768]{3,2,1,0:T(8,128)(2,1)S(1)} %bitcast.184), custom_call_target="tpu_custom_call" | custom-call | flops 1024 | bytes 1024 | tf_op jit(solution)/shard_map/attention_backward/pallas_call | solution.py:129
  562.2 4.5 ring_add.36
  568.7 10.6 %attention_backward.4 = (bf16[2,3,128,2304]{3,2,1,0:T(8,128)(2,1)}, bf16[2,3,64,2304]{3,2,1,0:T(8,128)(2,1)S(1)}) custom-call(bf16[2,3,128,2304]{3,2,1,0:T(8,128)(2,1)} %bitcast.166, bf16[2,3,64,2304]{3,2,1,0:T(8,128)(2,1)S(1)} %bitcast.175, bf16[2,3,128,768]{3,2,1,0:T(8,128)(2,1)S(1)} %bitcast.178, ...), custom_call_target="tpu_custom_call", output_to_operand_aliasing={{0}: (4, {}), {1}: (5, {})} | custom-call | flops 1024 | bytes 1024 | tf_op jit(solution)/shard_map/attention_backward/pallas_call | solution.py:129
  579.3 10.9 %attention_backward.5 = (bf16[2,3,128,2304]{3,2,1,0:T(8,128)(2,1)}, bf16[2,3,64,2304]{3,2,1,0:T(8,128)(2,1)S(1)}) custom-call(bf16[2,3,128,2304]{3,2,1,0:T(8,128)(2,1)} %bitcast.167, bf16[2,3,64,2304]{3,2,1,0:T(8,128)(2,1)S(1)} %bitcast.176, bf16[2,3,128,768]{3,2,1,0:T(8,128)(2,1)S(1)} %bitcast.179, ...), custom_call_target="tpu_custom_call", output_to_operand_aliasing={{0}: (4, {}), {1}: (5, {})} | custom-call | flops 1024 | bytes 1024 | tf_op jit(solution)/shard_map/attention_backward/pallas_call | solution.py:129
  590.2 5.1 collective-permute-done.49.refs_4_
  601.3 9.2 %qkv_back.2 = (f32[384,1536]{1,0:T(8,128)S(1)}, bf16[384,1536]{1,0:T(8,128)(2,1)S(1)}) custom-call(bf16[768,2304]{1,0:T(8,128)(2,1)} %bitcast.241, bf16[768,2304]{1,0:T(8,128)(2,1)} %bitcast.242, bf16[2,1536,3072]{2,1,0:T(8,128)(2,1)} %all-gather.5.cloned.1.call-done.refs_2_), custom_call_target="tpu_custom_call" | custom-call | flops 1024 | bytes 1024 | tf_op jit(solution)/shard_map/qkv_back/pallas_call | solution.py:350
  611.9 7.2 qkv_back.3
  621.1 5.3 collective-permute-done.51.refs_4_
  632.5 12.1 %weight_grad.14 = (bf16[8,96,2304]{2,1,0:T(8,128)(2,1)S(1)}, bf16[8,96,2304]{2,1,0:T(8,128)(2,1)}) custom-call(s32[1]{0:T(128)} %bitcast.32.core_ref, bf16[384,1536]{1,0:T(8,128)(2,1)S(1)} %bitcast.192, bf16[384,1536]{1,0:T(8,128)(2,1)S(1)} %bitcast.194, bf16[768,2304]{1,0:T(8,128)(2,1)} %bitcast.243, bf16[768,2304]{1,0:T(8,128)(2,1)} %bitcast.244), custom_call_target="tpu_custom_call" | custom-call | flops 1024 | bytes 1024 | tf_op jit(solution)/shard_map/weight_grad/pallas_call | solution.py:303
  646.3 6.6 weight_grad.15
  659.5 5.1 collective-permute-done.53.refs_3_
  668.3 3.4 ring_add.39
  674.8 21.4 %collective-permute-done.57.refs_4_ = bf16[96,3072]{1,0:T(8,128)(2,1)} collective-permute-done((bf16[96,3072]{1,0:T(8,128)(2,1)}, bf16[96,3072]{1,0:T(8,128)(2,1)}, u32[]{:S(2)}, u32[]{:S(2)}) %collective-permute-start.57) | collective-permute-done | bytes 589856 | tf_op jit(solution)/shard_map/ppermute | solution.py:497
  703.5 4.7 leave.2
  714.5 4.3 ring_add.41
  720.9 5.2 enter_back.3
  726.2 5.6 enter_back.2
  737.0 4.2 collective-permute-done.63
  744.2 15.3 %collective-permute-done.64.refs_4_ = bf16[96,3072]{1,0:T(8,128)(2,1)S(1)} collective-permute-done((bf16[96,3072]{1,0:T(8,128)(2,1)}, bf16[96,3072]{1,0:T(8,128)(2,1)S(1)}, u32[]{:S(2)}, u32[]{:S(2)}) %collective-permute-start.64) | collective-permute-done | bytes 589856 | tf_op jit(solution)/shard_map/ppermute | solution.py:497
  766.7 19.2 %collective-permute-done.66.refs_4_ = bf16[96,3072]{1,0:T(8,128)(2,1)S(1)} collective-permute-done((bf16[96,3072]{1,0:T(8,128)(2,1)}, bf16[96,3072]{1,0:T(8,128)(2,1)S(1)}, u32[]{:S(2)}, u32[]{:S(2)}) %collective-permute-start.66) | collective-permute-done | bytes 589856 | tf_op jit(solution)/shard_map/ppermute | solution.py:497
  785.8 8.8 %collective-permute-done.67.refs_9_ = bf16[96,3072]{1,0:T(8,128)(2,1)S(1)} collective-permute-done((bf16[96,3072]{1,0:T(8,128)(2,1)}, bf16[96,3072]{1,0:T(8,128)(2,1)S(1)}, u32[]{:S(2)}, u32[]{:S(2)}) %collective-permute-start.67) | collective-permute-done | bytes 589856 | tf_op jit(solution)/shard_map/ppermute | solution.py:497
  804.7 8.9 %collective-permute-done.68.refs_4_ = bf16[96,3072]{1,0:T(8,128)(2,1)S(1)} collective-permute-done((bf16[96,3072]{1,0:T(8,128)(2,1)S(1)}, bf16[96,3072]{1,0:T(8,128)(2,1)S(1)}, u32[]{:S(2)}, u32[]{:S(2)}) %collective-permute-start.68) | collective-permute-done | bytes 589856 | tf_op jit(solution)/shard_map/ppermute | solution.py:497
  839.6 6.7 collective-permute-done.73
  (619 shorter events, 284.0 us)
Async XLA Ops:
  7.2 167.2 %all-gather.5.cloned.1.call-start = ((), (), s32[]{:S(2)}) async-start(), calls=%async_computation | async-start | bytes 20054016 | tf_op jit(solution)/shard_map/all_gather | solution.py:610
  13.1 263.1 %all-gather.9.cloned.1.call-start = ((), (), s32[]{:S(2)}) async-start(), calls=%async_computation.2 | async-start | bytes 20054016 | tf_op jit(solution)/shard_map/all_gather | solution.py:614
  15.3 330.8 %all-gather.7.cloned.1.call-start = ((), (), s32[]{:S(2)}) async-start(), calls=%async_computation.1 | async-start | bytes 20054016 | tf_op jit(solution)/shard_map/all_gather | solution.py:615
  18.2 801.0 %all-gather.11.cloned.1.call-start = ((), (), s32[]{:S(2)}) async-start(), calls=%async_computation.3 | async-start | bytes 3760128 | tf_op jit(solution)/shard_map/all_gather | solution.py:866
  52.4 8.3 collective-permute-start.6
  53.6 8.0 collective-permute-start.7
  62.1 7.8 collective-permute-start.8
  64.5 7.7 collective-permute-start.9
  72.8 7.5 collective-permute-start.10
  100.4 7.7 collective-permute-start.16
  100.7 7.7 collective-permute-start.17
  121.1 8.6 collective-permute-start.20
  132.6 37.4 %collective-permute-start.21 = (bf16[3,128,1536]{2,1,0:T(8,128)(2,1)S(1)}, bf16[3,128,1536]{2,1,0:T(8,128)(2,1)S(1)}, u32[]{:S(2)}, u32[]{:S(2)}) collective-permute-start(bf16[3,128,1536]{2,1,0:T(8,128)(2,1)S(1)} %get-tuple-element.390), channel_id=1, source_target_pairs={{0,1},{1,0},{2,3},{3,2},{4,5},{5,4},{6,7},{7,6},{8,9},{9,8},{10,11... | collective-permute-start | bytes 3538952 | tf_op jit(solution)/shard_map/ppermute | solution.py:545
  136.9 33.1 %collective-permute-start.22 = (bf16[3,64,1536]{2,1,0:T(8,128)(2,1)S(1)}, bf16[3,64,1536]{2,1,0:T(8,128)(2,1)S(1)}, u32[]{:S(2)}, u32[]{:S(2)}) collective-permute-start(bf16[3,64,1536]{2,1,0:T(8,128)(2,1)S(1)} %get-tuple-element.391), channel_id=1, source_target_pairs={{0,1},{1,0},{2,3},{3,2},{4,5},{5,4},{6,7},{7,6},{8,9},{9,8},{10,11... | collective-permute-start | bytes 1769480 | tf_op jit(solution)/shard_map/ppermute | solution.py:545
  171.0 46.0 %collective-permute-start.23 = (bf16[3,128,1536]{2,1,0:T(8,128)(2,1)}, bf16[3,128,1536]{2,1,0:T(8,128)(2,1)}, u32[]{:S(2)}, u32[]{:S(2)}) collective-permute-start(bf16[3,128,1536]{2,1,0:T(8,128)(2,1)} %get-tuple-element.398), channel_id=1, source_target_pairs={{0,1},{1,0},{2,3},{3,2},{4,5},{5,4},{6,7},{7,6},{8,9},{9,8},{10,11... | collective-permute-start | bytes 3538952 | tf_op jit(solution)/shard_map/ppermute | solution.py:545
  172.7 44.4 %collective-permute-start.24 = (bf16[3,64,1536]{2,1,0:T(8,128)(2,1)}, bf16[3,64,1536]{2,1,0:T(8,128)(2,1)}, u32[]{:S(2)}, u32[]{:S(2)}) collective-permute-start(bf16[3,64,1536]{2,1,0:T(8,128)(2,1)} %get-tuple-element.399), channel_id=1, source_target_pairs={{0,1},{1,0},{2,3},{3,2},{4,5},{5,4},{6,7},{7,6},{8,9},{9,8},{10,11... | collective-permute-start | bytes 1769480 | tf_op jit(solution)/shard_map/ppermute | solution.py:545
  224.0 29.2 %collective-permute-start.25 = (bf16[3,128,1536]{2,1,0:T(8,128)(2,1)}, bf16[3,128,1536]{2,1,0:T(8,128)(2,1)}, u32[]{:S(2)}, u32[]{:S(2)}) collective-permute-start(bf16[3,128,1536]{2,1,0:T(8,128)(2,1)} %bitcast.39), channel_id=1, source_target_pairs={{0,1},{1,0},{2,3},{3,2},{4,5},{5,4},{6,7},{7,6},{8,9},{9,8},{10,11... | collective-permute-start | bytes 3538952 | tf_op jit(solution)/shard_map/ppermute | solution.py:564
  231.1 34.7 %collective-permute-start.27 = (bf16[3,64,1536]{2,1,0:T(8,128)(2,1)}, bf16[3,64,1536]{2,1,0:T(8,128)(2,1)}, u32[]{:S(2)}, u32[]{:S(2)}) collective-permute-start(bf16[3,64,1536]{2,1,0:T(8,128)(2,1)} %bitcast.47), channel_id=1, source_target_pairs={{0,1},{1,0},{2,3},{3,2},{4,5},{5,4},{6,7},{7,6},{8,9},{9,8},{10,11... | collective-permute-start | bytes 1769480 | tf_op jit(solution)/shard_map/ppermute | solution.py:564
  260.1 53.2 %collective-permute-start.26 = (bf16[3,128,1536]{2,1,0:T(8,128)(2,1)}, bf16[3,128,1536]{2,1,0:T(8,128)(2,1)}, u32[]{:S(2)}, u32[]{:S(2)}) collective-permute-start(bf16[3,128,1536]{2,1,0:T(8,128)(2,1)} %get-tuple-element.403), channel_id=1, source_target_pairs={{0,1},{1,0},{2,3},{3,2},{4,5},{5,4},{6,7},{7,6},{8,9},{9,8},{10,11... | collective-permute-start | bytes 3538952 | tf_op jit(solution)/shard_map/ppermute | solution.py:545
  272.3 17.4 %collective-permute-start.28 = (bf16[3,64,1536]{2,1,0:T(8,128)(2,1)S(1)}, bf16[3,64,1536]{2,1,0:T(8,128)(2,1)S(1)}, u32[]{:S(2)}, u32[]{:S(2)}) collective-permute-start(bf16[3,64,1536]{2,1,0:T(8,128)(2,1)S(1)} %get-tuple-element.415), channel_id=1, source_target_pairs={{0,1},{1,0},{2,3},{3,2},{4,5},{5,4},{6,7},{7,6},{8,9},{9,8},{10,11... | collective-permute-start | bytes 1769480 | tf_op jit(solution)/shard_map/ppermute | solution.py:545
  372.9 36.3 %collective-permute-start.29 = (bf16[3,128,1536]{2,1,0:T(8,128)(2,1)S(1)}, bf16[3,128,1536]{2,1,0:T(8,128)(2,1)S(1)}, u32[]{:S(2)}, u32[]{:S(2)}) collective-permute-start(bf16[3,128,1536]{2,1,0:T(8,128)(2,1)S(1)} %bitcast.238), channel_id=1, source_target_pairs={{0,1},{1,0},{2,3},{3,2},{4,5},{5,4},{6,7},{7,6},{8,9},{9,8},{10,11... | collective-permute-start | bytes 3538952 | tf_op jit(solution)/shard_map/ppermute | solution.py:564
  392.6 24.8 %collective-permute-start.30 = (bf16[3,64,1536]{2,1,0:T(8,128)(2,1)S(1)}, bf16[3,64,1536]{2,1,0:T(8,128)(2,1)S(1)}, u32[]{:S(2)}, u32[]{:S(2)}) collective-permute-start(bf16[3,64,1536]{2,1,0:T(8,128)(2,1)S(1)} %bitcast.240), channel_id=1, source_target_pairs={{0,1},{1,0},{2,3},{3,2},{4,5},{5,4},{6,7},{7,6},{8,9},{9,8},{10,11... | collective-permute-start | bytes 1769480 | tf_op jit(solution)/shard_map/ppermute | solution.py:564
  393.1 24.9 %collective-permute-start.33 = (bf16[8,96,3072]{2,1,0:T(8,128)(2,1)}, bf16[8,96,3072]{2,1,0:T(8,128)(2,1)}, u32[]{:S(2)}, u32[]{:S(2)}) collective-permute-start(bf16[8,96,3072]{2,1,0:T(8,128)(2,1)} %get-tuple-element.448), channel_id=1, source_target_pairs={{0,2},{2,0},{4,6},{6,4},{8,10},{10,8},{12,14},{14,12},{16,18},{18,... | collective-permute-start | bytes 14155784 | tf_op jit(solution)/shard_map/ppermute | solution.py:430
  408.7 9.3 %collective-permute-start.31 = (bf16[8,96,3072]{2,1,0:T(8,128)(2,1)}, bf16[8,96,3072]{2,1,0:T(8,128)(2,1)}, u32[]{:S(2)}, u32[]{:S(2)}) collective-permute-start(bf16[8,96,3072]{2,1,0:T(8,128)(2,1)} %get-tuple-element.446), channel_id=1, source_target_pairs={{0,2},{2,0},{4,6},{6,4},{8,10},{10,8},{12,14},{14,12},{16,18},{18,... | collective-permute-start | bytes 14155784 | tf_op jit(solution)/shard_map/ppermute | solution.py:430
  417.5 14.1 %collective-permute-start.34 = (bf16[8,96,3072]{2,1,0:T(8,128)(2,1)}, bf16[8,96,3072]{2,1,0:T(8,128)(2,1)S(1)}, u32[]{:S(2)}, u32[]{:S(2)}) collective-permute-start(bf16[8,96,3072]{2,1,0:T(8,128)(2,1)} %get-tuple-element.449), channel_id=1, source_target_pairs={{0,2},{2,0},{4,6},{6,4},{8,10},{10,8},{12,14},{14,12},{16,18},{18,... | collective-permute-start | bytes 14155784 | tf_op jit(solution)/shard_map/ppermute | solution.py:430
  417.6 16.2 %collective-permute-start.32 = (bf16[8,96,3072]{2,1,0:T(8,128)(2,1)}, bf16[8,96,3072]{2,1,0:T(8,128)(2,1)}, u32[]{:S(2)}, u32[]{:S(2)}) collective-permute-start(bf16[8,96,3072]{2,1,0:T(8,128)(2,1)} %get-tuple-element.447), channel_id=1, source_target_pairs={{0,2},{2,0},{4,6},{6,4},{8,10},{10,8},{12,14},{14,12},{16,18},{18,... | collective-permute-start | bytes 14155784 | tf_op jit(solution)/shard_map/ppermute | solution.py:430
  438.1 28.2 %collective-permute-start.37 = (bf16[96,6144]{1,0:T(8,128)(2,1)}, bf16[96,6144]{1,0:T(8,128)(2,1)S(1)}, u32[]{:S(2)}, u32[]{:S(2)}) collective-permute-start(bf16[96,6144]{1,0:T(8,128)(2,1)} %get-tuple-element.462), channel_id=1, source_target_pairs={{0,8},{2,10},{8,16},{10,18},{16,24},{18,26},{24,28},{26,30},{28,20... | collective-permute-start | bytes 3538952 | tf_op jit(solution)/shard_map/ppermute | solution.py:497
  438.5 28.9 %collective-permute-start.38 = (bf16[96,6144]{1,0:T(8,128)(2,1)S(1)}, bf16[96,6144]{1,0:T(8,128)(2,1)S(1)}, u32[]{:S(2)}, u32[]{:S(2)}) collective-permute-start(bf16[96,6144]{1,0:T(8,128)(2,1)S(1)} %get-tuple-element.463), channel_id=1, source_target_pairs={{0,4},{2,6},{8,0},{10,2},{16,8},{18,10},{24,16},{26,18},{28,24},{3... | collective-permute-start | bytes 3538952 | tf_op jit(solution)/shard_map/ppermute | solution.py:497
  474.3 27.2 %collective-permute-start.39 = (bf16[96,6144]{1,0:T(8,128)(2,1)S(1)}, bf16[96,6144]{1,0:T(8,128)(2,1)S(1)}, u32[]{:S(2)}, u32[]{:S(2)}) collective-permute-start(bf16[96,6144]{1,0:T(8,128)(2,1)S(1)} %get-tuple-element.488), channel_id=1, source_target_pairs={{0,8},{2,10},{8,16},{10,18},{16,24},{18,26},{24,28},{26,30},{28,20... | collective-permute-start | bytes 3538952 | tf_op jit(solution)/shard_map/ppermute | solution.py:497
  474.7 26.9 %collective-permute-start.40 = (bf16[96,6144]{1,0:T(8,128)(2,1)S(1)}, bf16[96,6144]{1,0:T(8,128)(2,1)S(1)}, u32[]{:S(2)}, u32[]{:S(2)}) collective-permute-start(bf16[96,6144]{1,0:T(8,128)(2,1)S(1)} %get-tuple-element.489), channel_id=1, source_target_pairs={{0,4},{2,6},{8,0},{10,2},{16,8},{18,10},{24,16},{26,18},{28,24},{3... | collective-permute-start | bytes 3538952 | tf_op jit(solution)/shard_map/ppermute | solution.py:497
  476.4 43.7 %collective-permute-start.35 = (bf16[3,128,1536]{2,1,0:T(8,128)(2,1)S(1)}, bf16[3,128,1536]{2,1,0:T(8,128)(2,1)S(1)}, u32[]{:S(2)}, u32[]{:S(2)}) collective-permute-start(bf16[3,128,1536]{2,1,0:T(8,128)(2,1)S(1)} %get-tuple-element.480), channel_id=1, source_target_pairs={{0,1},{1,0},{2,3},{3,2},{4,5},{5,4},{6,7},{7,6},{8,9},{9,8},{10,11... | collective-permute-start | bytes 3538952 | tf_op jit(solution)/shard_map/ppermute | solution.py:545
  505.0 26.2 %collective-permute-start.41 = (bf16[96,6144]{1,0:T(8,128)(2,1)S(1)}, bf16[96,6144]{1,0:T(8,128)(2,1)S(1)}, u32[]{:S(2)}, u32[]{:S(2)}) collective-permute-start(bf16[96,6144]{1,0:T(8,128)(2,1)S(1)} %get-tuple-element.506), channel_id=1, source_target_pairs={{0,8},{2,10},{8,16},{10,18},{16,24},{18,26},{24,28},{26,30},{28,20... | collective-permute-start | bytes 3538952 | tf_op jit(solution)/shard_map/ppermute | solution.py:497
  505.7 25.7 %collective-permute-start.42 = (bf16[96,6144]{1,0:T(8,128)(2,1)S(1)}, bf16[96,6144]{1,0:T(8,128)(2,1)S(1)}, u32[]{:S(2)}, u32[]{:S(2)}) collective-permute-start(bf16[96,6144]{1,0:T(8,128)(2,1)S(1)} %get-tuple-element.507), channel_id=1, source_target_pairs={{0,4},{2,6},{8,0},{10,2},{16,8},{18,10},{24,16},{26,18},{28,24},{3... | collective-permute-start | bytes 3538952 | tf_op jit(solution)/shard_map/ppermute | solution.py:497
  507.1 13.0 %collective-permute-start.36 = (bf16[3,64,1536]{2,1,0:T(8,128)(2,1)S(1)}, bf16[3,64,1536]{2,1,0:T(8,128)(2,1)S(1)}, u32[]{:S(2)}, u32[]{:S(2)}) collective-permute-start(bf16[3,64,1536]{2,1,0:T(8,128)(2,1)S(1)} %get-tuple-element.481), channel_id=1, source_target_pairs={{0,1},{1,0},{2,3},{3,2},{4,5},{5,4},{6,7},{7,6},{8,9},{9,8},{10,11... | collective-permute-start | bytes 1769480 | tf_op jit(solution)/shard_map/ppermute | solution.py:545
  534.8 25.1 %collective-permute-start.43 = (bf16[96,6144]{1,0:T(8,128)(2,1)S(1)}, bf16[96,6144]{1,0:T(8,128)(2,1)S(1)}, u32[]{:S(2)}, u32[]{:S(2)}) collective-permute-start(bf16[96,6144]{1,0:T(8,128)(2,1)S(1)} %get-tuple-element.522), channel_id=1, source_target_pairs={{0,8},{2,10},{8,16},{10,18},{16,24},{18,26},{24,28},{26,30},{28,20... | collective-permute-start | bytes 3538952 | tf_op jit(solution)/shard_map/ppermute | solution.py:497
  536.1 24.9 %collective-permute-start.44 = (bf16[96,6144]{1,0:T(8,128)(2,1)S(1)}, bf16[96,6144]{1,0:T(8,128)(2,1)}, u32[]{:S(2)}, u32[]{:S(2)}) collective-permute-start(bf16[96,6144]{1,0:T(8,128)(2,1)S(1)} %get-tuple-element.523), channel_id=1, source_target_pairs={{0,4},{2,6},{8,0},{10,2},{16,8},{18,10},{24,16},{26,18},{28,24},{3... | collective-permute-start | bytes 3538952 | tf_op jit(solution)/shard_map/ppermute | solution.py:497
  536.9 31.5 %collective-permute-start.48 = (bf16[3,64,1536]{2,1,0:T(8,128)(2,1)}, bf16[3,64,1536]{2,1,0:T(8,128)(2,1)S(1)}, u32[]{:S(2)}, u32[]{:S(2)}) collective-permute-start(bf16[3,64,1536]{2,1,0:T(8,128)(2,1)} %bitcast.61), channel_id=1, source_target_pairs={{0,1},{1,0},{2,3},{3,2},{4,5},{5,4},{6,7},{7,6},{8,9},{9,8},{10,11... | collective-permute-start | bytes 1769480 | tf_op jit(solution)/shard_map/ppermute | solution.py:564
  538.5 40.8 %collective-permute-start.47 = (bf16[3,128,1536]{2,1,0:T(8,128)(2,1)}, bf16[3,128,1536]{2,1,0:T(8,128)(2,1)}, u32[]{:S(2)}, u32[]{:S(2)}) collective-permute-start(bf16[3,128,1536]{2,1,0:T(8,128)(2,1)} %bitcast.59), channel_id=1, source_target_pairs={{0,1},{1,0},{2,3},{3,2},{4,5},{5,4},{6,7},{7,6},{8,9},{9,8},{10,11... | collective-permute-start | bytes 3538952 | tf_op jit(solution)/shard_map/ppermute | solution.py:564
  547.9 31.4 %collective-permute-start.46 = (bf16[8,96,768]{2,1,0:T(8,128)(2,1)}, bf16[8,96,768]{2,1,0:T(8,128)(2,1)S(1)}, u32[]{:S(2)}, u32[]{:S(2)}) collective-permute-start(bf16[8,96,768]{2,1,0:T(8,128)(2,1)} %get-tuple-element.554), channel_id=1, source_target_pairs={{0,2},{2,0},{4,6},{6,4},{8,10},{10,8},{12,14},{14,12},{16,18},{18,... | collective-permute-start | bytes 3538952 | tf_op jit(solution)/shard_map/ppermute | solution.py:430
  560.9 18.4 %collective-permute-start.45 = (bf16[8,96,768]{2,1,0:T(8,128)(2,1)}, bf16[8,96,768]{2,1,0:T(8,128)(2,1)S(1)}, u32[]{:S(2)}, u32[]{:S(2)}) collective-permute-start(bf16[8,96,768]{2,1,0:T(8,128)(2,1)} %get-tuple-element.553), channel_id=1, source_target_pairs={{0,2},{2,0},{4,6},{6,4},{8,10},{10,8},{12,14},{14,12},{16,18},{18,... | collective-permute-start | bytes 3538952 | tf_op jit(solution)/shard_map/ppermute | solution.py:430
  566.7 28.6 %collective-permute-start.49 = (bf16[96,6144]{1,0:T(8,128)(2,1)}, bf16[96,6144]{1,0:T(8,128)(2,1)S(1)}, u32[]{:S(2)}, u32[]{:S(2)}) collective-permute-start(bf16[96,6144]{1,0:T(8,128)(2,1)} %get-tuple-element.545), channel_id=1, source_target_pairs={{0,8},{2,10},{8,16},{10,18},{16,24},{18,26},{24,28},{26,30},{28,20... | collective-permute-start | bytes 3538952 | tf_op jit(solution)/shard_map/ppermute | solution.py:497
  568.3 27.5 %collective-permute-start.50 = (bf16[96,6144]{1,0:T(8,128)(2,1)S(1)}, bf16[96,6144]{1,0:T(8,128)(2,1)S(1)}, u32[]{:S(2)}, u32[]{:S(2)}) collective-permute-start(bf16[96,6144]{1,0:T(8,128)(2,1)S(1)} %get-tuple-element.546), channel_id=1, source_target_pairs={{0,4},{2,6},{8,0},{10,2},{16,8},{18,10},{24,16},{26,18},{28,24},{3... | collective-permute-start | bytes 3538952 | tf_op jit(solution)/shard_map/ppermute | solution.py:497
  599.2 27.1 %collective-permute-start.51 = (bf16[96,6144]{1,0:T(8,128)(2,1)S(1)}, bf16[96,6144]{1,0:T(8,128)(2,1)S(1)}, u32[]{:S(2)}, u32[]{:S(2)}) collective-permute-start(bf16[96,6144]{1,0:T(8,128)(2,1)S(1)} %get-tuple-element.573), channel_id=1, source_target_pairs={{0,8},{2,10},{8,16},{10,18},{16,24},{18,26},{24,28},{26,30},{28,20... | collective-permute-start | bytes 3538952 | tf_op jit(solution)/shard_map/ppermute | solution.py:497
  601.0 26.6 %collective-permute-start.52 = (bf16[96,6144]{1,0:T(8,128)(2,1)S(1)}, bf16[96,6144]{1,0:T(8,128)(2,1)S(1)}, u32[]{:S(2)}, u32[]{:S(2)}) collective-permute-start(bf16[96,6144]{1,0:T(8,128)(2,1)S(1)} %get-tuple-element.574), channel_id=1, source_target_pairs={{0,4},{2,6},{8,0},{10,2},{16,8},{18,10},{24,16},{26,18},{28,24},{3... | collective-permute-start | bytes 3538952 | tf_op jit(solution)/shard_map/ppermute | solution.py:497
  652.9 11.6 %collective-permute-start.53 = (bf16[8,96,2304]{2,1,0:T(8,128)(2,1)}, bf16[8,96,2304]{2,1,0:T(8,128)(2,1)}, u32[]{:S(2)}, u32[]{:S(2)}) collective-permute-start(bf16[8,96,2304]{2,1,0:T(8,128)(2,1)} %get-tuple-element.602), channel_id=1, source_target_pairs={{0,2},{2,0},{4,6},{6,4},{8,10},{10,8},{12,14},{14,12},{16,18},{18,... | collective-permute-start | bytes 10616840 | tf_op jit(solution)/shard_map/ppermute | solution.py:430
  653.6 67.3 %collective-permute-start.55 = (bf16[3,128,1536]{2,1,0:T(8,128)(2,1)}, bf16[3,128,1536]{2,1,0:T(8,128)(2,1)}, u32[]{:S(2)}, u32[]{:S(2)}) collective-permute-start(bf16[3,128,1536]{2,1,0:T(8,128)(2,1)} %bitcast.237), channel_id=1, source_target_pairs={{0,1},{1,0},{2,3},{3,2},{4,5},{5,4},{6,7},{7,6},{8,9},{9,8},{10,11... | collective-permute-start | bytes 3538952 | tf_op jit(solution)/shard_map/ppermute | solution.py:564
  655.7 58.4 %collective-permute-start.59 = (bf16[96,6144]{1,0:T(8,128)(2,1)}, bf16[96,6144]{1,0:T(8,128)(2,1)}, u32[]{:S(2)}, u32[]{:S(2)}) collective-permute-start(bf16[96,6144]{1,0:T(8,128)(2,1)} %copy-done.132), channel_id=1, source_target_pairs={{0,8},{2,10},{8,16},{10,18},{16,24},{18,26},{24,28},{26,30},{28,20... | collective-permute-start | bytes 3538952 | tf_op jit(solution)/shard_map/ppermute | solution.py:497
  657.4 57.0 %collective-permute-start.60 = (bf16[96,6144]{1,0:T(8,128)(2,1)}, bf16[96,6144]{1,0:T(8,128)(2,1)}, u32[]{:S(2)}, u32[]{:S(2)}) collective-permute-start(bf16[96,6144]{1,0:T(8,128)(2,1)} %copy-done.131), channel_id=1, source_target_pairs={{0,4},{2,6},{8,0},{10,2},{16,8},{18,10},{24,16},{26,18},{28,24},{3... | collective-permute-start | bytes 3538952 | tf_op jit(solution)/shard_map/ppermute | solution.py:497
  671.7 24.5 %collective-permute-start.57 = (bf16[96,3072]{1,0:T(8,128)(2,1)}, bf16[96,3072]{1,0:T(8,128)(2,1)}, u32[]{:S(2)}, u32[]{:S(2)}) collective-permute-start(bf16[96,3072]{1,0:T(8,128)(2,1)} %get-tuple-element.619), channel_id=1, source_target_pairs={{0,8},{2,10},{8,16},{10,18},{16,24},{18,26},{24,28},{26,30},{28,20... | collective-permute-start | bytes 1769480 | tf_op jit(solution)/shard_map/ppermute | solution.py:497
  673.6 34.6 %collective-permute-start.58 = (bf16[96,3072]{1,0:T(8,128)(2,1)}, bf16[96,3072]{1,0:T(8,128)(2,1)}, u32[]{:S(2)}, u32[]{:S(2)}) collective-permute-start(bf16[96,3072]{1,0:T(8,128)(2,1)} %get-tuple-element.620), channel_id=1, source_target_pairs={{0,4},{2,6},{8,0},{10,2},{16,8},{18,10},{24,16},{26,18},{28,24},{3... | collective-permute-start | bytes 1769480 | tf_op jit(solution)/shard_map/ppermute | solution.py:497
  696.2 24.6 %collective-permute-start.56 = (bf16[3,64,1536]{2,1,0:T(8,128)(2,1)}, bf16[3,64,1536]{2,1,0:T(8,128)(2,1)}, u32[]{:S(2)}, u32[]{:S(2)}) collective-permute-start(bf16[3,64,1536]{2,1,0:T(8,128)(2,1)} %bitcast.239), channel_id=1, source_target_pairs={{0,1},{1,0},{2,3},{3,2},{4,5},{5,4},{6,7},{7,6},{8,9},{9,8},{10,11... | collective-permute-start | bytes 1769480 | tf_op jit(solution)/shard_map/ppermute | solution.py:564
  712.3 19.7 %collective-permute-start.61 = (bf16[96,3072]{1,0:T(8,128)(2,1)S(1)}, bf16[96,3072]{1,0:T(8,128)(2,1)S(1)}, u32[]{:S(2)}, u32[]{:S(2)}) collective-permute-start(bf16[96,3072]{1,0:T(8,128)(2,1)S(1)} %get-tuple-element.642), channel_id=1, source_target_pairs={{0,8},{2,10},{8,16},{10,18},{16,24},{18,26},{24,28},{26,30},{28,20... | collective-permute-start | bytes 1769480 | tf_op jit(solution)/shard_map/ppermute | solution.py:497
  714.1 17.9 %collective-permute-start.62 = (bf16[96,3072]{1,0:T(8,128)(2,1)S(1)}, bf16[96,3072]{1,0:T(8,128)(2,1)S(1)}, u32[]{:S(2)}, u32[]{:S(2)}) collective-permute-start(bf16[96,3072]{1,0:T(8,128)(2,1)S(1)} %get-tuple-element.643), channel_id=1, source_target_pairs={{0,4},{2,6},{8,0},{10,2},{16,8},{18,10},{24,16},{26,18},{28,24},{3... | collective-permute-start | bytes 1769480 | tf_op jit(solution)/shard_map/ppermute | solution.py:497
  742.1 17.4 %collective-permute-start.64 = (bf16[96,3072]{1,0:T(8,128)(2,1)}, bf16[96,3072]{1,0:T(8,128)(2,1)S(1)}, u32[]{:S(2)}, u32[]{:S(2)}) collective-permute-start(bf16[96,3072]{1,0:T(8,128)(2,1)} %copy-done.134), channel_id=1, source_target_pairs={{0,8},{2,10},{8,16},{10,18},{16,24},{18,26},{24,28},{26,30},{28,20... | collective-permute-start | bytes 1769480 | tf_op jit(solution)/shard_map/ppermute | solution.py:497
  743.9 16.1 %collective-permute-start.65 = (bf16[96,3072]{1,0:T(8,128)(2,1)S(1)}, bf16[96,3072]{1,0:T(8,128)(2,1)S(1)}, u32[]{:S(2)}, u32[]{:S(2)}) collective-permute-start(bf16[96,3072]{1,0:T(8,128)(2,1)S(1)} %get-tuple-element.684), channel_id=1, source_target_pairs={{0,4},{2,6},{8,0},{10,2},{16,8},{18,10},{24,16},{26,18},{28,24},{3... | collective-permute-start | bytes 1769480 | tf_op jit(solution)/shard_map/ppermute | solution.py:497
  764.6 21.3 %collective-permute-start.66 = (bf16[96,3072]{1,0:T(8,128)(2,1)}, bf16[96,3072]{1,0:T(8,128)(2,1)S(1)}, u32[]{:S(2)}, u32[]{:S(2)}) collective-permute-start(bf16[96,3072]{1,0:T(8,128)(2,1)} %get-tuple-element.692), channel_id=1, source_target_pairs={{0,8},{2,10},{8,16},{10,18},{16,24},{18,26},{24,28},{26,30},{28,20... | collective-permute-start | bytes 1769480 | tf_op jit(solution)/shard_map/ppermute | solution.py:497
  766.7 28.0 %collective-permute-start.67 = (bf16[96,3072]{1,0:T(8,128)(2,1)}, bf16[96,3072]{1,0:T(8,128)(2,1)S(1)}, u32[]{:S(2)}, u32[]{:S(2)}) collective-permute-start(bf16[96,3072]{1,0:T(8,128)(2,1)} %get-tuple-element.693), channel_id=1, source_target_pairs={{0,4},{2,6},{8,0},{10,2},{16,8},{18,10},{24,16},{26,18},{28,24},{3... | collective-permute-start | bytes 1769480 | tf_op jit(solution)/shard_map/ppermute | solution.py:497
  798.5 15.1 %collective-permute-start.68 = (bf16[96,3072]{1,0:T(8,128)(2,1)S(1)}, bf16[96,3072]{1,0:T(8,128)(2,1)S(1)}, u32[]{:S(2)}, u32[]{:S(2)}) collective-permute-start(bf16[96,3072]{1,0:T(8,128)(2,1)S(1)} %get-tuple-element.698), channel_id=1, source_target_pairs={{0,8},{2,10},{8,16},{10,18},{16,24},{18,26},{24,28},{26,30},{28,20... | collective-permute-start | bytes 1769480 | tf_op jit(solution)/shard_map/ppermute | solution.py:497
  798.7 14.9 %collective-permute-start.69 = (bf16[96,3072]{1,0:T(8,128)(2,1)S(1)}, bf16[96,3072]{1,0:T(8,128)(2,1)S(1)}, u32[]{:S(2)}, u32[]{:S(2)}) collective-permute-start(bf16[96,3072]{1,0:T(8,128)(2,1)S(1)} %get-tuple-element.699), channel_id=1, source_target_pairs={{0,4},{2,6},{8,0},{10,2},{16,8},{18,10},{24,16},{26,18},{28,24},{3... | collective-permute-start | bytes 1769480 | tf_op jit(solution)/shard_map/ppermute | solution.py:497
  816.9 16.1 %collective-permute-start.71 = (bf16[96,3072]{1,0:T(8,128)(2,1)}, bf16[96,3072]{1,0:T(8,128)(2,1)S(1)}, u32[]{:S(2)}, u32[]{:S(2)}) collective-permute-start(bf16[96,3072]{1,0:T(8,128)(2,1)} %get-tuple-element.702), channel_id=1, source_target_pairs={{0,8},{2,10},{8,16},{10,18},{16,24},{18,26},{24,28},{26,30},{28,20... | collective-permute-start | bytes 1769480 | tf_op jit(solution)/shard_map/ppermute | solution.py:497
  816.9 16.7 %collective-permute-start.72 = (bf16[96,3072]{1,0:T(8,128)(2,1)}, bf16[96,3072]{1,0:T(8,128)(2,1)S(1)}, u32[]{:S(2)}, u32[]{:S(2)}) collective-permute-start(bf16[96,3072]{1,0:T(8,128)(2,1)} %get-tuple-element.703), channel_id=1, source_target_pairs={{0,4},{2,6},{8,0},{10,2},{16,8},{18,10},{24,16},{26,18},{28,24},{3... | collective-permute-start | bytes 1769480 | tf_op jit(solution)/shard_map/ppermute | solution.py:497
  836.0 11.0 %collective-permute-start.74 = (bf16[96,3072]{1,0:T(8,128)(2,1)S(1)}, bf16[96,3072]{1,0:T(8,128)(2,1)S(1)}, u32[]{:S(2)}, u32[]{:S(2)}) collective-permute-start(bf16[96,3072]{1,0:T(8,128)(2,1)S(1)} %get-tuple-element.708), channel_id=1, source_target_pairs={{0,8},{2,10},{8,16},{10,18},{16,24},{18,26},{24,28},{26,30},{28,20... | collective-permute-start | bytes 1769480 | tf_op jit(solution)/shard_map/ppermute | solution.py:497
  836.1 10.9 %collective-permute-start.75 = (bf16[96,3072]{1,0:T(8,128)(2,1)S(1)}, bf16[96,3072]{1,0:T(8,128)(2,1)S(1)}, u32[]{:S(2)}, u32[]{:S(2)}) collective-permute-start(bf16[96,3072]{1,0:T(8,128)(2,1)S(1)} %get-tuple-element.709), channel_id=1, source_target_pairs={{0,4},{2,6},{8,0},{10,2},{16,8},{18,10},{24,16},{26,18},{28,24},{3... | collective-permute-start | bytes 1769480 | tf_op jit(solution)/shard_map/ppermute | solution.py:497
  851.4 8.1 collective-permute-start.76
  (173 other events, 1290.9 us)
Sparse Core Ops, SparseCore 0:
  13.2 119.0 all-gather.4
  133.9 99.1 all-gather.8
  234.6 98.9 all-gather.6
  742.2 52.8 all-gather.10
